TPU v7x, 512 devices: a whole 4x4x16 slice. The times are simulated.
512 devices in a mesh: grp: 8 (over z_hi, x), tm: 64 (over y, z_lo, core).
Axes of the slice: x: 4, y: 4, z: 16 (z_hi: 2, z_lo: 8; z = z_hi * 8 + z_lo), core: 2. Of those that a mesh axis runs over, the one named last changes fastest.
Arguments:
- residual: bfloat16 [8, 8192, 1536], P('grp', 'tm'), may hold values from -6 to 6
- queries: bfloat16 [8, 8192, 1536], P('grp', 'tm'), may hold values from -16 to 16
- key_rows: bfloat16 [8, 8192, 1536], P('grp', 'tm'), may hold values from -6 to 6
- value_rows: bfloat16 [8, 8192, 1536], P('grp', 'tm'), may hold values from -6 to 6
- conv_weight: float32 [31, 1536], replicated, may hold values from -1 to 1
- lengths: int32 [8], P('grp'), may hold values from 4096 to 8192
- frame_lang: int32 [8, 8192], P('grp', 'tm'), may hold values from 0 to 7, as said below
- up_weight: bfloat16 [8, 1536, 6144], P('grp', None, 'tm'), may hold values from -0.15625 to 0.15625
- down_weight: bfloat16 [8, 6144, 1536], P('grp', 'tm'), may hold values from -0.078125 to 0.078125
Outputs:
- output: bfloat16 [8, 8192, 1536], P('grp', 'tm')
Inputs may be any that keep to these rules, and one draw needn't show every extreme that they name: `frame_lang`: the language of the segment that holds each frame.
All inputs are finite; a program needn't handle non-finite values.
Results may differ from a plain program's by a relative error of at most 0.0095.
Values may be sent and summed in bfloat16 or wider, within the bound.
A program may use at most 64 MiB of HBM per device.

v0:
```python
import math

import jax
import jax.numpy as jnp
from jax import lax
from jax.sharding import PartitionSpec as P

HEAD = 128
WIN = 128


def with_halo(cells, sides, width):
    for axis, dim in sides:
        count = lax.axis_size(axis)
        ends = count - 1
        head = lax.slice_in_dim(cells, 0, width, axis=dim)
        tail = lax.slice_in_dim(cells, cells.shape[dim] - width, cells.shape[dim], axis=dim)
        cells = jnp.concatenate(
            [
                lax.ppermute(tail, axis, [(i, (i + 1) % count) for i in range(ends)]),
                cells,
                lax.ppermute(head, axis, [((i + 1) % count, i) for i in range(ends)]),
            ],
            axis=dim,
        )
    return cells


def from_partner(array, axis, bit):
    return lax.ppermute(array, axis, [(i, i ^ 1 << bit) for i in range(lax.axis_size(axis))])


def layer_norm(values):
    row_mean = jnp.mean(values, axis=-1, keepdims=True)
    centred = values - row_mean
    spread = jnp.mean(centred * centred, axis=-1, keepdims=True)
    return centred * lax.rsqrt(spread + 1e-05)


def time_rim(source, rim_width):
    return with_halo(source, (("tm", 0),), rim_width)


def partner_join(shard_piece, bit_index, join_dim, tm_place):
    partner = from_partner(shard_piece, "tm", bit_index)
    is_upper = tm_place >> bit_index & 1 == 1
    upper_first = jnp.concatenate([partner, shard_piece], axis=join_dim)
    lower_first = jnp.concatenate([shard_piece, partner], axis=join_dim)
    return jnp.where(is_upper, upper_first, lower_first)


def partner_fold(partial_value, bit_index, tm_place):
    half_rows = partial_value.shape[0] // 2
    is_upper = tm_place >> bit_index & 1 == 1
    kept_half = jnp.where(is_upper, partial_value[half_rows:], partial_value[:half_rows])
    sent_half = jnp.where(is_upper, partial_value[:half_rows], partial_value[half_rows:])
    return kept_half + from_partner(sent_half.astype(jnp.bfloat16), "tm", bit_index).astype(
        sent_half.dtype
    )


def expert_blocks(up_weight, down_weight, low_bits, tm_place):
    up_block = up_weight[0]
    down_block = down_weight[0]
    for bit_index in range(low_bits):
        up_block = partner_join(up_block, bit_index, 1, tm_place)
        down_block = partner_join(down_block, bit_index, 0, tm_place)
    return (up_block, down_block)


def attend(query_rows, widened, query_pos, key_pos, length):
    frames, model_width = query_rows.shape
    head_count = model_width // HEAD
    query_heads = query_rows.reshape(frames, head_count, HEAD)
    key_heads = widened[:, 0].reshape(-1, head_count, HEAD)
    value_heads = widened[:, 1].reshape(-1, head_count, HEAD)
    scores = jnp.einsum(
        "ihd,jhd->hij", query_heads, key_heads, preferred_element_type=jnp.float32
    ) / math.sqrt(HEAD)
    in_window = jnp.abs(query_pos[:, None] - key_pos[None, :]) <= WIN
    is_live = ((key_pos >= 0) & (key_pos < length))[None, :] | (
        query_pos[:, None] == key_pos[None, :]
    )
    allowed = (in_window & is_live)[None, :, :]
    row_top = jnp.max(jnp.where(allowed, scores, -jnp.inf), axis=-1, keepdims=True)
    weights = jnp.where(allowed, jnp.exp(scores - row_top), 0.0)
    attn_probs = (weights / jnp.sum(weights, axis=-1, keepdims=True)).astype(jnp.bfloat16)
    head_mix = jnp.einsum(
        "hij,jhd->ihd", attn_probs, value_heads, preferred_element_type=jnp.float32
    )
    return head_mix.reshape(frames, model_width).astype(jnp.bfloat16)


def body(
    residual,
    queries,
    key_rows,
    value_rows,
    conv_weight,
    lengths,
    frame_lang,
    up_weight,
    down_weight,
):
    frames = residual.shape[1]
    model_width = residual.shape[2]
    conv_reach = (conv_weight.shape[0] - 1) // 2
    tm_place = lax.axis_index("tm")
    total_bits = lax.axis_size("tm").bit_length() - 1
    experts = lax.axis_size("grp")
    slot_count = 5 * frames // (4 * experts)
    row_bits = 3
    low_bits = total_bits - row_bits
    frame_start = tm_place * frames
    query_pos = frame_start + jnp.arange(frames, dtype=jnp.int32)
    key_pos = frame_start - WIN + jnp.arange(frames + 2 * WIN, dtype=jnp.int32)
    length = lengths[0]
    is_valid = query_pos < length
    key_value = jnp.stack([key_rows[0], value_rows[0]], axis=1)
    widened = time_rim(key_value, WIN)
    attended = attend(queries[0], widened, query_pos, key_pos, length)
    middle = (residual[0].astype(jnp.float32) + attended.astype(jnp.float32)).astype(jnp.bfloat16)
    normed = (layer_norm(middle.astype(jnp.float32)) * is_valid[:, None]).astype(jnp.bfloat16)
    beside_all = time_rim(normed, conv_reach)
    conv_sum = jnp.zeros((frames, model_width), jnp.float32)
    for kernel_tap in range(conv_weight.shape[0]):
        conv_sum = conv_sum + conv_weight[kernel_tap] * beside_all[
            kernel_tap : kernel_tap + frames
        ].astype(jnp.float32)
    conv_out = (middle.astype(jnp.float32) + jax.nn.silu(conv_sum)).astype(jnp.bfloat16)
    ffn_in = layer_norm(conv_out.astype(jnp.float32)).astype(jnp.bfloat16)
    up_block, down_block = expert_blocks(up_weight, down_weight, low_bits, tm_place)
    language = frame_lang[0]
    onehot = (
        (language[:, None] == jnp.arange(experts, dtype=jnp.int32)[None, :]) & is_valid[:, None]
    ).astype(jnp.int32)
    before = jnp.cumsum(onehot, axis=0) - onehot
    slot_index = jnp.sum(before * onehot, axis=1)
    is_kept = is_valid & (slot_index < slot_count)
    target = language * slot_count + slot_index
    route_table = (
        (target[None, :] == jnp.arange(experts * slot_count, dtype=jnp.int32)[:, None])
        & is_kept[None, :]
    ).astype(jnp.bfloat16)
    outgoing = jnp.dot(route_table, ffn_in, preferred_element_type=jnp.float32).astype(jnp.bfloat16)
    outgoing = outgoing.reshape(experts, slot_count, model_width)
    arrived = lax.all_to_all(outgoing, "grp", split_axis=0, concat_axis=0, tiled=True)
    item_count = arrived.shape[1]
    frame_rows = arrived.reshape(-1, model_width)
    for bit_index in range(low_bits, total_bits):
        frame_rows = partner_join(frame_rows, bit_index, 0, tm_place)
    hidden = jax.nn.silu(jnp.dot(frame_rows, up_block, preferred_element_type=jnp.float32)).astype(
        jnp.bfloat16
    )
    partial_value = jnp.dot(hidden, down_block, preferred_element_type=jnp.float32)
    for bit_index in reversed(range(low_bits, total_bits)):
        partial_value = partner_fold(partial_value, bit_index, tm_place)
    outbound = partial_value.astype(jnp.bfloat16).reshape(experts, item_count, model_width)
    returned = lax.all_to_all(outbound, "grp", split_axis=0, concat_axis=0, tiled=True)
    expert_out = lax.dot_general(
        route_table,
        returned.reshape(-1, model_width),
        (((0,), (0,)), ((), ())),
        preferred_element_type=jnp.float32,
    )
    output = is_valid[:, None] * (conv_out.astype(jnp.float32) + 0.5 * expert_out)
    return output.astype(jnp.bfloat16)[None]


def solution(mesh):
    in_specs = (
        P("grp", "tm", None),
        P("grp", "tm", None),
        P("grp", "tm", None),
        P("grp", "tm", None),
        P(),
        P("grp"),
        P("grp", "tm"),
        P("grp", None, "tm"),
        P("grp", "tm", None),
    )
    out_specs = P("grp", "tm", None)
    return jax.shard_map(body, mesh=mesh, in_specs=in_specs, out_specs=out_specs, check_vma=False)
```

profile of v0, /device:TPU:24, one launch (start us, length us, event | category | flops | bytes accessed | tf_op | source)
XLA Modules:
  0.0 458.9 jit_solution(16825778085175328120)
XLA Ops:
  2.6 12.8 %collective-permute-start.1 = (bf16[128,2,1536]{0,2,1:T(8,128)(2,1)S(1)}, bf16[128,2,1536]{0,2,1:T(8,128)(2,1)S(1)}, u32[]{:S(2)}, u32[]{:S(2)}) collective-permute-start(bf16[128,2,1536]{0,2,1:T(8,128)(2,1)S(1)} %pad_maximum_fusion.1), channel_id=1, source_target_pairs={{1,0},{2,1},{3,2},{4,3},{5,4},{6,5},{7,6},{8,7},{9,8},{10,9},{11,1... | collective-permute-start | bytes 2359304 | tf_op jit(solution)/shard_map/ppermute | solution.py:22
  30.7 5.5 %collective-permute-done = bf16[128,2,1536]{0,2,1:T(8,128)(2,1)S(1)} collective-permute-done((bf16[128,2,1536]{0,2,1:T(8,128)(2,1)S(1)}, bf16[128,2,1536]{0,2,1:T(8,128)(2,1)S(1)}, u32[]{:S(2)}, u32[]{:S(2)}) %collective-permute-start) | collective-permute-done | bytes 786464 | tf_op jit(solution)/shard_map/ppermute | solution.py:20
  37.5 2.7 fusion.102
  45.6 11.1 %collective-permute-start.3 = (bf16[15,1536]{1,0:T(8,128)(2,1)S(1)}, bf16[15,1536]{1,0:T(8,128)(2,1)S(1)}, u32[]{:S(2)}, u32[]{:S(2)}) collective-permute-start(bf16[15,1536]{1,0:T(8,128)(2,1)S(1)} %get-tuple-element.45), channel_id=1, source_target_pairs={{1,0},{2,1},{3,2},{4,3},{5,4},{6,5},{7,6},{8,7},{9,8},{10,9},{11,1... | collective-permute-start | bytes 138248 | tf_op jit(solution)/shard_map/ppermute | solution.py:22
  58.7 4.3 convert_reduce_fusion
  63.8 28.7 %all_to_all.10 = bf16[8,20,1536]{2,1,0:T(8,128)(2,1)S(1)} all-to-all(bf16[8,20,1536]{2,1,0:T(8,128)(2,1)S(1)} %reshape.147), channel_id=1, replica_groups=mesh['grp'=8,'tm'=64] {'grp'}, dimensions={0} | all-to-all | bytes 983040 | tf_op jit(solution)/shard_map/all_to_all | solution.py:147
  92.6 11.9 %collective-permute-start.4 = (bf16[160,1536]{1,0:T(8,128)(2,1)S(1)}, bf16[160,1536]{1,0:T(8,128)(2,1)S(1)}, u32[]{:S(2)}, u32[]{:S(2)}) collective-permute-start(bf16[160,1536]{1,0:T(8,128)(2,1)S(1)} %reshape.148), channel_id=1, source_target_pairs={{0,8},{1,9},{2,10},{3,11},{4,12},{5,13},{6,14},{7,15},{8,0},{9,1},... | collective-permute-start | bytes 1474568 | tf_op jit(solution)/shard_map/ppermute | solution.py:30
  104.4 40.3 %collective-permute-done.4 = bf16[160,1536]{1,0:T(8,128)(2,1)S(1)} collective-permute-done((bf16[160,1536]{1,0:T(8,128)(2,1)S(1)}, bf16[160,1536]{1,0:T(8,128)(2,1)S(1)}, u32[]{:S(2)}, u32[]{:S(2)}) %collective-permute-start.4) | collective-permute-done | bytes 491552 | tf_op jit(solution)/shard_map/ppermute | solution.py:30
  145.0 3.8 collective-permute-start.5
  157.6 3.9 collective-permute-start.11
  161.6 9.0 %collective-permute-done.5 = bf16[320,1536]{1,0:T(8,128)(2,1)S(1)} collective-permute-done((bf16[320,1536]{1,0:T(8,128)(2,1)S(1)}, bf16[320,1536]{1,0:T(8,128)(2,1)S(1)}, u32[]{:S(2)}, u32[]{:S(2)}) %collective-permute-start.5) | collective-permute-done | bytes 983072 | tf_op jit(solution)/shard_map/ppermute | solution.py:30
  172.6 3.8 collective-permute-start.6
  176.4 2.7 maximum_select_fusion.13
  181.0 3.3 collective-permute-done.11
  188.1 67.0 %collective-permute-done.9 = bf16[1536,384]{0,1:T(8,128)(2,1)} collective-permute-done((bf16[1536,384]{0,1:T(8,128)(2,1)}, bf16[1536,384]{0,1:T(8,128)(2,1)}, u32[]{:S(2)}, u32[]{:S(2)}) %collective-permute-start.9) | collective-permute-done | bytes 1179680 | tf_op jit(solution)/shard_map/ppermute | solution.py:30
  255.1 25.1 %collective-permute-done.12 = bf16[384,1536]{1,0:T(8,128)(2,1)S(1)} collective-permute-done((bf16[384,1536]{1,0:T(8,128)(2,1)S(1)}, bf16[384,1536]{1,0:T(8,128)(2,1)S(1)}, u32[]{:S(2)}, u32[]{:S(2)}) %collective-permute-start.12) | collective-permute-done | bytes 1179680 | tf_op jit(solution)/shard_map/ppermute | solution.py:30
  280.1 15.7 %fusion.14 = f32[1280,1536]{1,0:T(8,128)} fusion(bf16[640,1536]{1,0:T(8,128)(2,1)} %maximum_select_fusion.12, bf16[640,1536]{1,0:T(8,128)(2,1)} %collective-permute-done.6, pred[]{:T(512)S(6)} %eq.78, bf16[1536,384]{0,1:T(8,128)(2,1)} %maximum_select_fusion.13, bf16[1536,384]{0,1:T(8,128)(2,1)} %collective-permute-done.9, ...), kind=kOutput, calls=%fused_computation.22 | convolution fusion | flops 6083641344 | bytes 16515074 | tf_op jit(solution)/shard_map/dot_general | solution.py:155
  295.8 3.7 select_convert_fusion
  301.9 45.7 %collective-permute-done.13 = bf16[640,1536]{1,0:T(8,128)(2,1)S(1)} collective-permute-done((bf16[640,1536]{1,0:T(8,128)(2,1)S(1)}, bf16[640,1536]{1,0:T(8,128)(2,1)S(1)}, u32[]{:S(2)}, u32[]{:S(2)}) %collective-permute-start.13) | collective-permute-done | bytes 1966112 | tf_op jit(solution)/shard_map/ppermute | solution.py:30
  347.6 4.5 convert_add_fusion
  354.3 22.7 %collective-permute-done.14 = bf16[320,1536]{1,0:T(8,128)(2,1)S(1)} collective-permute-done((bf16[320,1536]{1,0:T(8,128)(2,1)S(1)}, bf16[320,1536]{1,0:T(8,128)(2,1)S(1)}, u32[]{:S(2)}, u32[]{:S(2)}) %collective-permute-start.14) | collective-permute-done | bytes 983072 | tf_op jit(solution)/shard_map/ppermute | solution.py:30
  377.5 2.8 collective-permute-start.15
  380.3 50.1 %collective-permute-done.15 = bf16[160,1536]{1,0:T(8,128)(2,1)S(1)} collective-permute-done((bf16[160,1536]{1,0:T(8,128)(2,1)S(1)}, bf16[160,1536]{1,0:T(8,128)(2,1)S(1)}, u32[]{:S(2)}, u32[]{:S(2)}) %collective-permute-start.15) | collective-permute-done | bytes 491552 | tf_op jit(solution)/shard_map/ppermute | solution.py:30
  430.8 26.9 %all_to_all.11 = bf16[8,20,1536]{2,1,0:T(8,128)(2,1)S(1)} all-to-all(bf16[8,20,1536]{2,1,0:T(8,128)(2,1)S(1)} %reshape.149), channel_id=1, replica_groups=mesh['grp'=8,'tm'=64] {'grp'}, dimensions={0} | all-to-all | bytes 983040 | tf_op jit(solution)/shard_map/all_to_all | solution.py:159
  (120 shorter events, 49.8 us)
Async XLA Ops:
  0.0 19.0 %copy-start.29 = (s32[1,128]{1,0:T(1,128)S(1)}, s32[1,128]{1,0:T(1,128)}, u32[]{:S(2)}) copy-start(s32[1,128]{1,0:T(1,128)} %param.15) | copy-start | bytes 1540
  0.0 26.0 %copy-start = (bf16[1,128,1536]{2,1,0:T(8,128)(2,1)S(1)}, bf16[1,128,1536]{2,1,0:T(8,128)(2,1)}, u32[]{:S(2)}) copy-start(bf16[1,128,1536]{2,1,0:T(8,128)(2,1)} %param.10) | copy-start | bytes 1179652
  2.6 28.1 %collective-permute-start.1 = (bf16[128,2,1536]{0,2,1:T(8,128)(2,1)S(1)}, bf16[128,2,1536]{0,2,1:T(8,128)(2,1)S(1)}, u32[]{:S(2)}, u32[]{:S(2)}) collective-permute-start(bf16[128,2,1536]{0,2,1:T(8,128)(2,1)S(1)} %pad_maximum_fusion.1), channel_id=1, source_target_pairs={{1,0},{2,1},{3,2},{4,3},{5,4},{6,5},{7,6},{8,7},{9,8},{10,9},{11,1... | collective-permute-start | bytes 2359304 | tf_op jit(solution)/shard_map/ppermute | solution.py:22
  15.4 20.8 %collective-permute-start = (bf16[128,2,1536]{0,2,1:T(8,128)(2,1)S(1)}, bf16[128,2,1536]{0,2,1:T(8,128)(2,1)S(1)}, u32[]{:S(2)}, u32[]{:S(2)}) collective-permute-start(bf16[128,2,1536]{0,2,1:T(8,128)(2,1)S(1)} %pad_maximum_fusion.1), channel_id=1, source_target_pairs={{0,1},{1,2},{2,3},{3,4},{4,5},{5,6},{6,7},{7,8},{8,9},{9,10},{10,1... | collective-permute-start | bytes 2359304 | tf_op jit(solution)/shard_map/ppermute | solution.py:20
  42.9 20.4 %copy-start.25 = (pred[128]{0:T(512)(128)(4,1)S(1)}, pred[128]{0:T(512)(128)(4,1)}, u32[]{:S(2)}) copy-start(pred[128]{0:T(512)(128)(4,1)} %compare_and_fusion) | copy-start | bytes 388
  42.9 20.4 %copy-start.27 = (s32[128]{0:T(128)S(1)}, s32[128]{0:T(128)}, u32[]{:S(2)}) copy-start(s32[128]{0:T(128)} %fusion.91) | copy-start | bytes 1540
  43.7 14.6 %collective-permute-start.2 = (bf16[15,1536]{1,0:T(8,128)(2,1)S(1)}, bf16[15,1536]{1,0:T(8,128)(2,1)S(1)}, u32[]{:S(2)}, u32[]{:S(2)}) collective-permute-start(bf16[15,1536]{1,0:T(8,128)(2,1)S(1)} %get-tuple-element.44), channel_id=1, source_target_pairs={{0,1},{1,2},{2,3},{3,4},{4,5},{5,6},{6,7},{7,8},{8,9},{9,10},{10,1... | collective-permute-start | bytes 138248 | tf_op jit(solution)/shard_map/ppermute | solution.py:20
  45.6 12.9 %collective-permute-start.3 = (bf16[15,1536]{1,0:T(8,128)(2,1)S(1)}, bf16[15,1536]{1,0:T(8,128)(2,1)S(1)}, u32[]{:S(2)}, u32[]{:S(2)}) collective-permute-start(bf16[15,1536]{1,0:T(8,128)(2,1)S(1)} %get-tuple-element.45), channel_id=1, source_target_pairs={{1,0},{2,1},{3,2},{4,3},{5,4},{6,5},{7,6},{8,7},{9,8},{10,9},{11,1... | collective-permute-start | bytes 138248 | tf_op jit(solution)/shard_map/ppermute | solution.py:22
  63.8 85.0 %copy-start.3 = (bf16[1,1536,96]{1,2,0:T(8,128)(2,1)S(1)}, bf16[1,1536,96]{1,2,0:T(8,128)(2,1)}, u32[]{:S(2)}) copy-start(bf16[1,1536,96]{1,2,0:T(8,128)(2,1)} %param.16) | copy-start | bytes 884740
  92.6 52.1 %collective-permute-start.4 = (bf16[160,1536]{1,0:T(8,128)(2,1)S(1)}, bf16[160,1536]{1,0:T(8,128)(2,1)S(1)}, u32[]{:S(2)}, u32[]{:S(2)}) collective-permute-start(bf16[160,1536]{1,0:T(8,128)(2,1)S(1)} %reshape.148), channel_id=1, source_target_pairs={{0,8},{1,9},{2,10},{3,11},{4,12},{5,13},{6,14},{7,15},{8,0},{9,1},... | collective-permute-start | bytes 1474568 | tf_op jit(solution)/shard_map/ppermute | solution.py:30
  145.0 25.6 %collective-permute-start.5 = (bf16[320,1536]{1,0:T(8,128)(2,1)S(1)}, bf16[320,1536]{1,0:T(8,128)(2,1)S(1)}, u32[]{:S(2)}, u32[]{:S(2)}) collective-permute-start(bf16[320,1536]{1,0:T(8,128)(2,1)S(1)} %maximum_select_fusion.15), channel_id=1, source_target_pairs={{0,16},{1,17},{2,18},{3,19},{4,20},{5,21},{6,22},{7,23},{8,24},{9,... | collective-permute-start | bytes 2949128 | tf_op jit(solution)/shard_map/ppermute | solution.py:30
  148.8 4.4 collective-permute-start.7
  150.7 5.5 %collective-permute-start.10 = (bf16[96,1536]{1,0:T(8,128)(2,1)}, bf16[96,1536]{1,0:T(8,128)(2,1)}, u32[]{:S(2)}, u32[]{:S(2)}) collective-permute-start(bf16[96,1536]{1,0:T(8,128)(2,1)} %bitcast.14), channel_id=1, source_target_pairs={{0,1},{1,0},{2,3},{3,2},{4,5},{5,4},{6,7},{7,6},{8,9},{9,8},{10,11... | collective-permute-start | bytes 884744 | tf_op jit(solution)/shard_map/ppermute | solution.py:30
  154.3 22.1 %collective-permute-start.8 = (bf16[1536,192]{0,1:T(8,128)(2,1)S(1)}, bf16[1536,192]{0,1:T(8,128)(2,1)}, u32[]{:S(2)}, u32[]{:S(2)}) collective-permute-start(bf16[1536,192]{0,1:T(8,128)(2,1)S(1)} %maximum_select_fusion.16), channel_id=1, source_target_pairs={{0,2},{1,3},{2,0},{3,1},{4,6},{5,7},{6,4},{7,5},{8,10},{9,11},{10,... | collective-permute-start | bytes 1769480 | tf_op jit(solution)/shard_map/ppermute | solution.py:30
  157.6 26.7 %collective-permute-start.11 = (bf16[192,1536]{1,0:T(8,128)(2,1)S(1)}, bf16[192,1536]{1,0:T(8,128)(2,1)}, u32[]{:S(2)}, u32[]{:S(2)}) collective-permute-start(bf16[192,1536]{1,0:T(8,128)(2,1)S(1)} %maximum_select_fusion.17), channel_id=1, source_target_pairs={{0,2},{1,3},{2,0},{3,1},{4,6},{5,7},{6,4},{7,5},{8,10},{9,11},{10,... | collective-permute-start | bytes 1769480 | tf_op jit(solution)/shard_map/ppermute | solution.py:30
  172.6 107.5 %collective-permute-start.6 = (bf16[640,1536]{1,0:T(8,128)(2,1)}, bf16[640,1536]{1,0:T(8,128)(2,1)}, u32[]{:S(2)}, u32[]{:S(2)}) collective-permute-start(bf16[640,1536]{1,0:T(8,128)(2,1)} %maximum_select_fusion.12), channel_id=1, source_target_pairs={{0,32},{1,33},{2,34},{3,35},{4,36},{5,37},{6,38},{7,39},{8,40},{9,... | collective-permute-start | bytes 5898248 | tf_op jit(solution)/shard_map/ppermute | solution.py:30
  179.1 76.0 %collective-permute-start.9 = (bf16[1536,384]{0,1:T(8,128)(2,1)}, bf16[1536,384]{0,1:T(8,128)(2,1)}, u32[]{:S(2)}, u32[]{:S(2)}) collective-permute-start(bf16[1536,384]{0,1:T(8,128)(2,1)} %maximum_select_fusion.13), channel_id=1, source_target_pairs={{0,4},{1,5},{2,6},{3,7},{4,0},{5,1},{6,2},{7,3},{8,12},{9,13},{10,... | collective-permute-start | bytes 3538952 | tf_op jit(solution)/shard_map/ppermute | solution.py:30
  185.9 94.2 %collective-permute-start.12 = (bf16[384,1536]{1,0:T(8,128)(2,1)S(1)}, bf16[384,1536]{1,0:T(8,128)(2,1)S(1)}, u32[]{:S(2)}, u32[]{:S(2)}) collective-permute-start(bf16[384,1536]{1,0:T(8,128)(2,1)S(1)} %maximum_select_fusion.14), channel_id=1, source_target_pairs={{0,4},{1,5},{2,6},{3,7},{4,0},{5,1},{6,2},{7,3},{8,12},{9,13},{10,... | collective-permute-start | bytes 3538952 | tf_op jit(solution)/shard_map/ppermute | solution.py:30
  299.5 48.1 %collective-permute-start.13 = (bf16[640,1536]{1,0:T(8,128)(2,1)S(1)}, bf16[640,1536]{1,0:T(8,128)(2,1)S(1)}, u32[]{:S(2)}, u32[]{:S(2)}) collective-permute-start(bf16[640,1536]{1,0:T(8,128)(2,1)S(1)} %select_convert_fusion), channel_id=1, source_target_pairs={{0,32},{1,33},{2,34},{3,35},{4,36},{5,37},{6,38},{7,39},{8,40},{9,... | collective-permute-start | bytes 5898248 | tf_op jit(solution)/shard_map/ppermute | solution.py:30
  352.3 24.7 %collective-permute-start.14 = (bf16[320,1536]{1,0:T(8,128)(2,1)S(1)}, bf16[320,1536]{1,0:T(8,128)(2,1)S(1)}, u32[]{:S(2)}, u32[]{:S(2)}) collective-permute-start(bf16[320,1536]{1,0:T(8,128)(2,1)S(1)} %select_convert_fusion.1), channel_id=1, source_target_pairs={{0,16},{1,17},{2,18},{3,19},{4,20},{5,21},{6,22},{7,23},{8,24},{9,... | collective-permute-start | bytes 2949128 | tf_op jit(solution)/shard_map/ppermute | solution.py:30
  377.5 52.9 %collective-permute-start.15 = (bf16[160,1536]{1,0:T(8,128)(2,1)S(1)}, bf16[160,1536]{1,0:T(8,128)(2,1)S(1)}, u32[]{:S(2)}, u32[]{:S(2)}) collective-permute-start(bf16[160,1536]{1,0:T(8,128)(2,1)S(1)} %select_convert_fusion.2), channel_id=1, source_target_pairs={{0,8},{1,9},{2,10},{3,11},{4,12},{5,13},{6,14},{7,15},{8,0},{9,1},... | collective-permute-start | bytes 1474568 | tf_op jit(solution)/shard_map/ppermute | solution.py:30
  430.6 27.1 %copy-start.24 = (f32[128]{0:T(128)S(1)}, f32[128]{0:T(128)}, u32[]{:S(2)}) copy-start(f32[128]{0:T(128)} %get-tuple-element.38) | copy-start | bytes 1540
  430.6 27.1 %copy-start.26 = (pred[128]{0:T(512)(128)(4,1)S(1)}, pred[128]{0:T(512)(128)(4,1)}, u32[]{:S(2)}) copy-start(pred[128]{0:T(512)(128)(4,1)} %compare_and_fusion) | copy-start | bytes 388
  430.7 27.1 %copy-start.28 = (s32[128]{0:T(128)S(1)}, s32[128]{0:T(128)}, u32[]{:S(2)}) copy-start(s32[128]{0:T(128)} %fusion.91) | copy-start | bytes 1540
  (22 other events, 281.3 us)
where the time goes:
time: 460 us; the launch traced here: 459 us
  waiting for transfers between devices  269 us (58%)
  starting transfers between devices  68.6 us (15%)
  blocking collectives  55.5 us (12%)
  other arithmetic  33.3 us (7%)
  matrix products  22.1 us (5%)
  local copies, waits for them, and re-layouts  9.13 us (2%)
    ppermute x12, waiting for transfers between devices, from_partner(): lax.ppermute(array, axis, [(i, i ^ 1 << bit) for i in range(lax.axis_size...  263 us
    ppermute x12, starting transfers between devices, from_partner(): lax.ppermute(array, axis, [(i, i ^ 1 << bit) for i in range(lax.axis_size...  40.9 us
    all_to_all x1, blocking collectives, body(): lax.all_to_all(outgoing, 'grp', split_axis=0, concat_axis=0, tiled=True)  28.7 us
    all_to_all x1, blocking collectives, body(): lax.all_to_all(outbound, 'grp', split_axis=0, concat_axis=0, tiled=True)  26.9 us
    ppermute x2, starting transfers between devices, with_halo(): lax.ppermute(head, axis, [((i + 1) % count, i) for i in range(ends)])  23.9 us
    dot_general x1, matrix products, body(): jnp.dot(hidden, down_block, preferred_element_type=jnp.float32)  15.7 us
    select_n x6, other arithmetic, partner_join(): return jnp.where(is_upper, upper_first, lower_first)  9.22 us
  transfers between devices with their start and end apart: 16, of which 10 were waited for; matrix products, arithmetic and copies ran while one was open for 5% of the time, Pallas kernels for 0%

commit v1 on v0

--- a/solution.py
+++ b/solution.py
@@ -26,10 +26,6 @@
     return cells
 
 
-def from_partner(array, axis, bit):
-    return lax.ppermute(array, axis, [(i, i ^ 1 << bit) for i in range(lax.axis_size(axis))])
-
-
 def layer_norm(values):
     row_mean = jnp.mean(values, axis=-1, keepdims=True)
     centred = values - row_mean
@@ -41,31 +37,40 @@
     return with_halo(source, (("tm", 0),), rim_width)
 
 
-def partner_join(shard_piece, bit_index, join_dim, tm_place):
-    partner = from_partner(shard_piece, "tm", bit_index)
-    is_upper = tm_place >> bit_index & 1 == 1
-    upper_first = jnp.concatenate([partner, shard_piece], axis=join_dim)
-    lower_first = jnp.concatenate([shard_piece, partner], axis=join_dim)
-    return jnp.where(is_upper, upper_first, lower_first)
-
-
-def partner_fold(partial_value, bit_index, tm_place):
-    half_rows = partial_value.shape[0] // 2
-    is_upper = tm_place >> bit_index & 1 == 1
-    kept_half = jnp.where(is_upper, partial_value[half_rows:], partial_value[:half_rows])
-    sent_half = jnp.where(is_upper, partial_value[:half_rows], partial_value[half_rows:])
-    return kept_half + from_partner(sent_half.astype(jnp.bfloat16), "tm", bit_index).astype(
-        sent_half.dtype
+def ring_step(array, stride, count, places, shift):
+    return lax.ppermute(
+        array, "tm", [(i, i + stride * ((i // stride + shift) % count - i // stride)) for i in range(places)]
     )
 
 
-def expert_blocks(up_weight, down_weight, low_bits, tm_place):
-    up_block = up_weight[0]
-    down_block = down_weight[0]
-    for bit_index in range(low_bits):
-        up_block = partner_join(up_block, bit_index, 1, tm_place)
-        down_block = partner_join(down_block, bit_index, 0, tm_place)
-    return (up_block, down_block)
+def gather_rows(own, stride, count, places):
+    half = own.shape[0] // 2
+    before = ring_step(own, stride, count, places, 1)
+    after = ring_step(own, stride, count, places, -1)
+    far_top = ring_step(before[:half], stride, count, places, 1)
+    far_low = ring_step(after[half:], stride, count, places, -1)
+    return before, after, jnp.concatenate([far_top, far_low], axis=0)
+
+
+def fold_rows(own, before, after, far, stride, count, places):
+    half = own.shape[0] // 2
+    narrow = lambda v: v.astype(jnp.bfloat16)
+    wide = lambda v: v.astype(jnp.float32)
+    from_before = ring_step(narrow(far[:half]), stride, count, places, 1)
+    from_after = ring_step(narrow(far[half:]), stride, count, places, -1)
+    after = jnp.concatenate([after[:half] + wide(from_before), after[half:]], axis=0)
+    before = jnp.concatenate([before[:half], before[half:] + wide(from_after)], axis=0)
+    one = ring_step(narrow(after), stride, count, places, 1)
+    two = ring_step(narrow(before), stride, count, places, -1)
+    return own + wide(one) + wide(two)
+
+
+def expert(rows, up_rows, down_rows):
+    hidden = lax.dot_general(
+        rows, up_rows, (((1,), (1,)), ((), ())), preferred_element_type=jnp.float32
+    )
+    hidden = jax.nn.silu(hidden).astype(jnp.bfloat16)
+    return jnp.dot(hidden, down_rows, preferred_element_type=jnp.float32)
 
 
 def attend(query_rows, widened, query_pos, key_pos, length):
@@ -106,11 +111,18 @@
     model_width = residual.shape[2]
     conv_reach = (conv_weight.shape[0] - 1) // 2
     tm_place = lax.axis_index("tm")
-    total_bits = lax.axis_size("tm").bit_length() - 1
+    places = lax.axis_size("tm")
+    ring = 4
+    stride = places // ring
     experts = lax.axis_size("grp")
     slot_count = 5 * frames // (4 * experts)
-    row_bits = 3
-    low_bits = total_bits - row_bits
+    units = down_weight.shape[1]
+    shard = jnp.concatenate([up_weight[0].T, down_weight[0]], axis=0)
+    weights = lax.all_gather(
+        shard,
+        "tm",
+        axis_index_groups=[[g * stride + i for i in range(stride)] for g in range(ring)],
+    )
     frame_start = tm_place * frames
     query_pos = frame_start + jnp.arange(frames, dtype=jnp.int32)
     key_pos = frame_start - WIN + jnp.arange(frames + 2 * WIN, dtype=jnp.int32)
@@ -129,13 +141,12 @@
         ].astype(jnp.float32)
     conv_out = (middle.astype(jnp.float32) + jax.nn.silu(conv_sum)).astype(jnp.bfloat16)
     ffn_in = layer_norm(conv_out.astype(jnp.float32)).astype(jnp.bfloat16)
-    up_block, down_block = expert_blocks(up_weight, down_weight, low_bits, tm_place)
     language = frame_lang[0]
     onehot = (
         (language[:, None] == jnp.arange(experts, dtype=jnp.int32)[None, :]) & is_valid[:, None]
     ).astype(jnp.int32)
-    before = jnp.cumsum(onehot, axis=0) - onehot
-    slot_index = jnp.sum(before * onehot, axis=1)
+    earlier = jnp.cumsum(onehot, axis=0) - onehot
+    slot_index = jnp.sum(earlier * onehot, axis=1)
     is_kept = is_valid & (slot_index < slot_count)
     target = language * slot_count + slot_index
     route_table = (
@@ -147,15 +158,13 @@
     arrived = lax.all_to_all(outgoing, "grp", split_axis=0, concat_axis=0, tiled=True)
     item_count = arrived.shape[1]
     frame_rows = arrived.reshape(-1, model_width)
-    for bit_index in range(low_bits, total_bits):
-        frame_rows = partner_join(frame_rows, bit_index, 0, tm_place)
-    hidden = jax.nn.silu(jnp.dot(frame_rows, up_block, preferred_element_type=jnp.float32)).astype(
-        jnp.bfloat16
-    )
-    partial_value = jnp.dot(hidden, down_block, preferred_element_type=jnp.float32)
-    for bit_index in reversed(range(low_bits, total_bits)):
-        partial_value = partner_fold(partial_value, bit_index, tm_place)
-    outbound = partial_value.astype(jnp.bfloat16).reshape(experts, item_count, model_width)
+    before, after, far = gather_rows(frame_rows, stride, ring, places)
+    up_rows = weights[:, :units].reshape(-1, model_width)
+    down_rows = weights[:, units:].reshape(-1, model_width)
+    all_rows = jnp.concatenate([frame_rows, before, after, far], axis=0)
+    partial_value = expert(all_rows, up_rows, down_rows).reshape(4, -1, model_width)
+    total = fold_rows(*partial_value, stride, ring, places)
+    outbound = total.astype(jnp.bfloat16).reshape(experts, item_count, model_width)
     returned = lax.all_to_all(outbound, "grp", split_axis=0, concat_axis=0, tiled=True)
     expert_out = lax.dot_general(
         route_table,

time: 460 us -> 278 us (0.60)
  the two profiles are of different devices: /device:TPU:24 before, /device:TPU:32 now
where the time goes in v1:
time: 278 us; the launch traced here: 277 us
  blocking collectives  110 us (40%)
  starting transfers between devices  52.2 us (19%)
  waiting for transfers between devices  40.5 us (15%)
  local copies, waits for them, and re-layouts  20.5 us (7%)
  other arithmetic  19.9 us (7%)
  matrix products  19.2 us (7%)
  between operations  14.7 us (5%)
    all_to_all x1, blocking collectives, body(): lax.all_to_all(outgoing, 'grp', split_axis=0, concat_axis=0, tiled=True)  55 us
    all_to_all x1, blocking collectives, body(): lax.all_to_all(outbound, 'grp', split_axis=0, concat_axis=0, tiled=True)  54.6 us
    ppermute x8, starting transfers between devices, ring_step(): lax.ppermute(array, 'tm', [(i, i + stride * ((i // stride + shift) % coun...  40.2 us
    ppermute x8, waiting for transfers between devices, ring_step(): lax.ppermute(array, 'tm', [(i, i + stride * ((i // stride + shift) % coun...  25.2 us
    dot_general x1, matrix products, expert(): return jnp.dot(hidden, down_rows, preferred_element_type=jnp.float32)  12.8 us
    all_gather x1, waiting for transfers between devices, body(): lax.all_gather(shard, 'tm', axis_index_groups=[[g * stride + i for i in r...  11.8 us
    slice x1, local copies, waits for them, and re-layouts, body(): up_rows = weights[:, :units].reshape(-1, model_width)  8.42 us
    ppermute x2, starting transfers between devices, with_halo(): lax.ppermute(head, axis, [((i + 1) % count, i) for i in range(ends)])  7.72 us
  transfers between devices with their start and end apart: 13, of which 10 were waited for; matrix products, arithmetic and copies ran while one was open for 11% of the time, Pallas kernels for 0%

profile of v1, /device:TPU:32, one launch (start us, length us, event | category | flops | bytes accessed | tf_op | source)
XLA Modules:
  0.0 276.6 jit_solution(11814158189577019440)
XLA Ops:
  6.5 2.0 pad_maximum_fusion.2
  12.0 2.4 collective-permute-start
  20.2 2.5 slice_reduce_fusion.30
  30.5 2.7 fusion.84
  33.2 2.2 fusion.11
  36.7 5.8 %collective-permute-start.3 = (bf16[15,1536]{1,0:T(8,128)(2,1)S(1)}, bf16[15,1536]{1,0:T(8,128)(2,1)S(1)}, u32[]{:S(2)}, u32[]{:S(2)}) collective-permute-start(bf16[15,1536]{1,0:T(8,128)(2,1)S(1)} %get-tuple-element.53), channel_id=1, source_target_pairs={{1,0},{2,1},{3,2},{4,3},{5,4},{6,5},{7,6},{8,7},{9,8},{10,9},{11,1... | collective-permute-start | bytes 138248 | tf_op jit(solution)/shard_map/ppermute | solution.py:22
  46.0 2.3 collective-permute-done.2
  48.5 4.3 %convert_reduce_fusion = (f32[128]{0:T(128)S(1)}, bf16[128,1536]{1,0:T(8,128)(2,1)S(1)}) fusion(bf16[15,1536]{1,0:T(8,128)(2,1)S(1)} %collective-permute-done.3, bf16[128,1536]{1,0:T(8,128)(2,1)S(1)} %fusion.25, f32[1536]{0:T(1024)S(1)} %get-tuple-element.34, f32[1536]{0:T(1024)S(1)} %get-tuple-element.35, f32[1536]{0:T(1024)S(1)} %get-tuple-element.6, ...), kind=kLoop, calls=%fused_computation.49 | loop fusion | flops 37552000 | bytes 1462784 | tf_op jit(solution)/shard_map/reduce_sum | solution.py:30
  53.6 55.0 %all_to_all.10 = bf16[8,20,1536]{2,1,0:T(8,128)(2,1)S(1)} all-to-all(bf16[8,20,1536]{2,1,0:T(8,128)(2,1)S(1)} %reshape.165), channel_id=1, replica_groups=mesh['grp'=8,'tm'=64] {'grp'}, dimensions={0} | all-to-all | bytes 983040 | tf_op jit(solution)/shard_map/all_to_all | solution.py:158
  108.7 15.5 %collective-permute-start.4 = (bf16[160,1536]{1,0:T(8,128)(2,1)S(1)}, bf16[160,1536]{1,0:T(8,128)(2,1)S(1)}, u32[]{:S(2)}, u32[]{:S(2)}) collective-permute-start(bf16[160,1536]{1,0:T(8,128)(2,1)S(1)} %reshape.166), channel_id=1, source_target_pairs={{0,16},{1,17},{2,18},{3,19},{4,20},{5,21},{6,22},{7,23},{8,24},{9,... | collective-permute-start | bytes 1474568 | tf_op jit(solution)/shard_map/ppermute | solution.py:41
  124.2 3.7 %collective-permute-start.5 = (bf16[160,1536]{1,0:T(8,128)(2,1)S(1)}, bf16[160,1536]{1,0:T(8,128)(2,1)S(1)}, u32[]{:S(2)}, u32[]{:S(2)}) collective-permute-start(bf16[160,1536]{1,0:T(8,128)(2,1)S(1)} %reshape.166), channel_id=1, source_target_pairs={{0,48},{1,49},{2,50},{3,51},{4,52},{5,53},{6,54},{7,55},{8,56},{9,... | collective-permute-start | bytes 1474568 | tf_op jit(solution)/shard_map/ppermute | solution.py:41
  128.7 5.0 %collective-permute-done.4 = bf16[160,1536]{1,0:T(8,128)(2,1)S(1)} collective-permute-done((bf16[160,1536]{1,0:T(8,128)(2,1)S(1)}, bf16[160,1536]{1,0:T(8,128)(2,1)S(1)}, u32[]{:S(2)}, u32[]{:S(2)}) %collective-permute-start.4) | collective-permute-done | bytes 491552 | tf_op jit(solution)/shard_map/ppermute | solution.py:41
  135.8 5.3 %collective-permute-start.7 = (bf16[80,1536]{1,0:T(8,128)(2,1)S(1)}, bf16[80,1536]{1,0:T(8,128)(2,1)S(1)}, u32[]{:S(2)}, u32[]{:S(2)}) collective-permute-start(bf16[80,1536]{1,0:T(8,128)(2,1)S(1)} %slice.408), channel_id=1, source_target_pairs={{0,48},{1,49},{2,50},{3,51},{4,52},{5,53},{6,54},{7,55},{8,56},{9,... | collective-permute-start | bytes 737288 | tf_op jit(solution)/shard_map/ppermute | solution.py:41
  145.3 11.8 %all-gather.3.cloned.1.call-done = bf16[3072,1536]{1,0:T(8,128)(2,1)} async-done(((bf16[192,1536]{1,0:T(8,128)(2,1)}), bf16[3072,1536]{1,0:T(8,128)(2,1)}) %all-gather.3.cloned.1.call-update) | async-done | bytes 9437200 | tf_op jit(solution)/shard_map/all_gather | solution.py:121
  157.1 8.4 %fusion.80 = (bf16[16,96,1536]{2,1,0:T(8,128)(2,1)}, bf16[16,96,1536]{2,1,0:T(8,128)(2,1)}) fusion(bf16[16,192,1536]{2,1,0:T(8,128)(2,1)} %bitcast.54), kind=kLoop, calls=%fused_computation.195 | loop fusion | bytes 18874368 | tf_op jit(solution)/shard_map/slice | solution.py:162
  165.5 12.8 %fusion.85 = (bf16[640,1536]{1,0:T(8,128)(2,1)S(1)}, f32[640,1536]{1,0:T(8,128)}) fusion(bf16[1536,1536]{1,0:T(8,128)(2,1)} %bitcast.56, bf16[640,1536]{1,0:T(8,128)(2,1)} %constant_dynamic-update-slice_fusion, bf16[1536,1536]{1,0:T(8,128)(2,1)} %bitcast.55), kind=kOutput, calls=%fused_computation.200 | convolution fusion | flops 6045696000 | bytes 17301504 | tf_op jit(solution)/shard_map/dot_general | solution.py:73
  178.4 3.4 %collective-permute-start.8 = (bf16[80,1536]{1,0:T(8,128)(2,1)S(1)}, bf16[80,1536]{1,0:T(8,128)(2,1)S(1)}, u32[]{:S(2)}, u32[]{:S(2)}) collective-permute-start(bf16[80,1536]{1,0:T(8,128)(2,1)S(1)} %get-tuple-element.48), channel_id=1, source_target_pairs={{0,16},{1,17},{2,18},{3,19},{4,20},{5,21},{6,22},{7,23},{8,24},{9,... | collective-permute-start | bytes 737288 | tf_op jit(solution)/shard_map/ppermute | solution.py:41
  181.8 3.6 %collective-permute-start.10 = (bf16[80,1536]{1,0:T(8,128)(2,1)S(1)}, bf16[80,1536]{1,0:T(8,128)(2,1)S(1)}, u32[]{:S(2)}, u32[]{:S(2)}) collective-permute-start(bf16[80,1536]{1,0:T(8,128)(2,1)S(1)} %get-tuple-element.49), channel_id=1, source_target_pairs={{0,48},{1,49},{2,50},{3,51},{4,52},{5,53},{6,54},{7,55},{8,56},{9,... | collective-permute-start | bytes 737288 | tf_op jit(solution)/shard_map/ppermute | solution.py:41
  185.5 2.2 collective-permute-done.8
  187.7 2.5 collective-permute-done.10
  191.5 4.7 %collective-permute-start.11 = (bf16[160,1536]{1,0:T(8,128)(2,1)S(1)}, bf16[160,1536]{1,0:T(8,128)(2,1)S(1)}, u32[]{:S(2)}, u32[]{:S(2)}) collective-permute-start(bf16[160,1536]{1,0:T(8,128)(2,1)S(1)} %pad_maximum_fusion.4), channel_id=1, source_target_pairs={{0,48},{1,49},{2,50},{3,51},{4,52},{5,53},{6,54},{7,55},{8,56},{9,... | collective-permute-start | bytes 1474568 | tf_op jit(solution)/shard_map/ppermute | solution.py:41
  198.2 8.3 %collective-permute-done.11 = bf16[160,1536]{1,0:T(8,128)(2,1)S(1)} collective-permute-done((bf16[160,1536]{1,0:T(8,128)(2,1)S(1)}, bf16[160,1536]{1,0:T(8,128)(2,1)S(1)}, u32[]{:S(2)}, u32[]{:S(2)}) %collective-permute-start.11) | collective-permute-done | bytes 491552 | tf_op jit(solution)/shard_map/ppermute | solution.py:41
  206.5 6.0 %collective-permute-done.9 = bf16[160,1536]{1,0:T(8,128)(2,1)S(1)} collective-permute-done((bf16[160,1536]{1,0:T(8,128)(2,1)S(1)}, bf16[160,1536]{1,0:T(8,128)(2,1)S(1)}, u32[]{:S(2)}, u32[]{:S(2)}) %collective-permute-start.9) | collective-permute-done | bytes 491552 | tf_op jit(solution)/shard_map/ppermute | solution.py:41
  214.0 54.6 %all_to_all.11 = bf16[8,20,1536]{2,1,0:T(8,128)(2,1)S(1)} all-to-all(bf16[8,20,1536]{2,1,0:T(8,128)(2,1)S(1)} %reshape.169), channel_id=1, replica_groups=mesh['grp'=8,'tm'=64] {'grp'}, dimensions={0} | all-to-all | bytes 983040 | tf_op jit(solution)/shard_map/all_to_all | solution.py:168
  (111 shorter events, 34.8 us)
Async XLA Ops:
  6.5 150.6 %all-gather.3.cloned.1.call-start = ((), (), s32[]{:S(2)}) async-start(), calls=%async_computation.2 | async-start | bytes 10027008 | tf_op jit(solution)/shard_map/all_gather | solution.py:121
  8.5 14.7 %copy-start.1 = (bf16[1,128,1536]{2,1,0:T(8,128)(2,1)S(1)}, bf16[1,128,1536]{2,1,0:T(8,128)(2,1)}, u32[]{:S(2)}) copy-start(bf16[1,128,1536]{2,1,0:T(8,128)(2,1)} %param.10) | copy-start | bytes 1179652
  10.1 17.9 %collective-permute-start.1 = (bf16[128,2,1536]{0,2,1:T(8,128)(2,1)S(1)}, bf16[128,2,1536]{0,2,1:T(8,128)(2,1)S(1)}, u32[]{:S(2)}, u32[]{:S(2)}) collective-permute-start(bf16[128,2,1536]{0,2,1:T(8,128)(2,1)S(1)} %pad_maximum_fusion.1), channel_id=1, source_target_pairs={{1,0},{2,1},{3,2},{4,3},{5,4},{6,5},{7,6},{8,7},{9,8},{10,9},{11,1... | collective-permute-start | bytes 2359304 | tf_op jit(solution)/shard_map/ppermute | solution.py:22
  12.0 17.2 %collective-permute-start = (bf16[128,2,1536]{0,2,1:T(8,128)(2,1)S(1)}, bf16[128,2,1536]{0,2,1:T(8,128)(2,1)S(1)}, u32[]{:S(2)}, u32[]{:S(2)}) collective-permute-start(bf16[128,2,1536]{0,2,1:T(8,128)(2,1)S(1)} %pad_maximum_fusion.1), channel_id=1, source_target_pairs={{0,1},{1,2},{2,3},{3,4},{4,5},{5,6},{6,7},{7,8},{8,9},{9,10},{10,1... | collective-permute-start | bytes 2359304 | tf_op jit(solution)/shard_map/ppermute | solution.py:20
  35.5 12.9 %copy-start.5 = (f32[1536]{0:T(1024)S(1)}, f32[1536]{0:T(1024)}, u32[]{:S(2)}) copy-start(f32[1536]{0:T(1024)} %get-tuple-element.7) | copy-start | bytes 18436
  35.5 12.9 %copy-start.6 = (f32[1536]{0:T(1024)S(1)}, f32[1536]{0:T(1024)}, u32[]{:S(2)}) copy-start(f32[1536]{0:T(1024)} %get-tuple-element.8) | copy-start | bytes 18436
  35.5 12.8 %copy-start.7 = (f32[1536]{0:T(1024)S(1)}, f32[1536]{0:T(1024)}, u32[]{:S(2)}) copy-start(f32[1536]{0:T(1024)} %get-tuple-element.9) | copy-start | bytes 18436
  35.5 12.8 %copy-start.8 = (f32[1536]{0:T(1024)S(1)}, f32[1536]{0:T(1024)}, u32[]{:S(2)}) copy-start(f32[1536]{0:T(1024)} %get-tuple-element.10) | copy-start | bytes 18436
  35.5 12.8 %copy-start.9 = (f32[1536]{0:T(1024)S(1)}, f32[1536]{0:T(1024)}, u32[]{:S(2)}) copy-start(f32[1536]{0:T(1024)} %get-tuple-element.11) | copy-start | bytes 18436
  35.5 12.8 %copy-start.10 = (f32[1536]{0:T(1024)S(1)}, f32[1536]{0:T(1024)}, u32[]{:S(2)}) copy-start(f32[1536]{0:T(1024)} %get-tuple-element.12) | copy-start | bytes 18436
  35.5 12.8 %copy-start.11 = (f32[1536]{0:T(1024)S(1)}, f32[1536]{0:T(1024)}, u32[]{:S(2)}) copy-start(f32[1536]{0:T(1024)} %get-tuple-element.13) | copy-start | bytes 18436
  35.5 12.8 %copy-start.12 = (f32[1536]{0:T(1024)S(1)}, f32[1536]{0:T(1024)}, u32[]{:S(2)}) copy-start(f32[1536]{0:T(1024)} %get-tuple-element.14) | copy-start | bytes 18436
  35.9 17.1 %copy-start.24 = (s32[128]{0:T(128)S(1)}, s32[128]{0:T(128)}, u32[]{:S(2)}) copy-start(s32[128]{0:T(128)} %fusion.73) | copy-start | bytes 1540
  35.9 17.1 %copy-start.25 = (pred[128]{0:T(512)(128)(4,1)S(1)}, pred[128]{0:T(512)(128)(4,1)}, u32[]{:S(2)}) copy-start(pred[128]{0:T(512)(128)(4,1)} %compare_and_fusion) | copy-start | bytes 388
  36.7 9.2 %collective-permute-start.3 = (bf16[15,1536]{1,0:T(8,128)(2,1)S(1)}, bf16[15,1536]{1,0:T(8,128)(2,1)S(1)}, u32[]{:S(2)}, u32[]{:S(2)}) collective-permute-start(bf16[15,1536]{1,0:T(8,128)(2,1)S(1)} %get-tuple-element.53), channel_id=1, source_target_pairs={{1,0},{2,1},{3,2},{4,3},{5,4},{6,5},{7,6},{8,7},{9,8},{10,9},{11,1... | collective-permute-start | bytes 138248 | tf_op jit(solution)/shard_map/ppermute | solution.py:22
  42.6 5.8 %collective-permute-start.2 = (bf16[15,1536]{1,0:T(8,128)(2,1)S(1)}, bf16[15,1536]{1,0:T(8,128)(2,1)S(1)}, u32[]{:S(2)}, u32[]{:S(2)}) collective-permute-start(bf16[15,1536]{1,0:T(8,128)(2,1)S(1)} %get-tuple-element.52), channel_id=1, source_target_pairs={{0,1},{1,2},{2,3},{3,4},{4,5},{5,6},{6,7},{7,8},{8,9},{9,10},{10,1... | collective-permute-start | bytes 138248 | tf_op jit(solution)/shard_map/ppermute | solution.py:20
  108.7 25.1 %collective-permute-start.4 = (bf16[160,1536]{1,0:T(8,128)(2,1)S(1)}, bf16[160,1536]{1,0:T(8,128)(2,1)S(1)}, u32[]{:S(2)}, u32[]{:S(2)}) collective-permute-start(bf16[160,1536]{1,0:T(8,128)(2,1)S(1)} %reshape.166), channel_id=1, source_target_pairs={{0,16},{1,17},{2,18},{3,19},{4,20},{5,21},{6,22},{7,23},{8,24},{9,... | collective-permute-start | bytes 1474568 | tf_op jit(solution)/shard_map/ppermute | solution.py:41
  124.2 11.5 %collective-permute-start.5 = (bf16[160,1536]{1,0:T(8,128)(2,1)S(1)}, bf16[160,1536]{1,0:T(8,128)(2,1)S(1)}, u32[]{:S(2)}, u32[]{:S(2)}) collective-permute-start(bf16[160,1536]{1,0:T(8,128)(2,1)S(1)} %reshape.166), channel_id=1, source_target_pairs={{0,48},{1,49},{2,50},{3,51},{4,52},{5,53},{6,54},{7,55},{8,56},{9,... | collective-permute-start | bytes 1474568 | tf_op jit(solution)/shard_map/ppermute | solution.py:41
  133.8 9.3 %collective-permute-start.6 = (bf16[80,1536]{1,0:T(8,128)(2,1)S(1)}, bf16[80,1536]{1,0:T(8,128)(2,1)S(1)}, u32[]{:S(2)}, u32[]{:S(2)}) collective-permute-start(bf16[80,1536]{1,0:T(8,128)(2,1)S(1)} %slice.407), channel_id=1, source_target_pairs={{0,16},{1,17},{2,18},{3,19},{4,20},{5,21},{6,22},{7,23},{8,24},{9,... | collective-permute-start | bytes 737288 | tf_op jit(solution)/shard_map/ppermute | solution.py:41
  135.8 8.8 %collective-permute-start.7 = (bf16[80,1536]{1,0:T(8,128)(2,1)S(1)}, bf16[80,1536]{1,0:T(8,128)(2,1)S(1)}, u32[]{:S(2)}, u32[]{:S(2)}) collective-permute-start(bf16[80,1536]{1,0:T(8,128)(2,1)S(1)} %slice.408), channel_id=1, source_target_pairs={{0,48},{1,49},{2,50},{3,51},{4,52},{5,53},{6,54},{7,55},{8,56},{9,... | collective-permute-start | bytes 737288 | tf_op jit(solution)/shard_map/ppermute | solution.py:41
  178.4 9.3 %collective-permute-start.8 = (bf16[80,1536]{1,0:T(8,128)(2,1)S(1)}, bf16[80,1536]{1,0:T(8,128)(2,1)S(1)}, u32[]{:S(2)}, u32[]{:S(2)}) collective-permute-start(bf16[80,1536]{1,0:T(8,128)(2,1)S(1)} %get-tuple-element.48), channel_id=1, source_target_pairs={{0,16},{1,17},{2,18},{3,19},{4,20},{5,21},{6,22},{7,23},{8,24},{9,... | collective-permute-start | bytes 737288 | tf_op jit(solution)/shard_map/ppermute | solution.py:41
  181.8 8.4 %collective-permute-start.10 = (bf16[80,1536]{1,0:T(8,128)(2,1)S(1)}, bf16[80,1536]{1,0:T(8,128)(2,1)S(1)}, u32[]{:S(2)}, u32[]{:S(2)}) collective-permute-start(bf16[80,1536]{1,0:T(8,128)(2,1)S(1)} %get-tuple-element.49), channel_id=1, source_target_pairs={{0,48},{1,49},{2,50},{3,51},{4,52},{5,53},{6,54},{7,55},{8,56},{9,... | collective-permute-start | bytes 737288 | tf_op jit(solution)/shard_map/ppermute | solution.py:41
  191.5 15.0 %collective-permute-start.11 = (bf16[160,1536]{1,0:T(8,128)(2,1)S(1)}, bf16[160,1536]{1,0:T(8,128)(2,1)S(1)}, u32[]{:S(2)}, u32[]{:S(2)}) collective-permute-start(bf16[160,1536]{1,0:T(8,128)(2,1)S(1)} %pad_maximum_fusion.4), channel_id=1, source_target_pairs={{0,48},{1,49},{2,50},{3,51},{4,52},{5,53},{6,54},{7,55},{8,56},{9,... | collective-permute-start | bytes 1474568 | tf_op jit(solution)/shard_map/ppermute | solution.py:41
  196.3 16.2 %collective-permute-start.9 = (bf16[160,1536]{1,0:T(8,128)(2,1)S(1)}, bf16[160,1536]{1,0:T(8,128)(2,1)S(1)}, u32[]{:S(2)}, u32[]{:S(2)}) collective-permute-start(bf16[160,1536]{1,0:T(8,128)(2,1)S(1)} %pad_maximum_fusion.3), channel_id=1, source_target_pairs={{0,16},{1,17},{2,18},{3,19},{4,20},{5,21},{6,22},{7,23},{8,24},{9,... | collective-permute-start | bytes 1474568 | tf_op jit(solution)/shard_map/ppermute | solution.py:41
  (16 other events, 136.4 us)
Sparse Core Ops, SparseCore 0:
  9.4 147.6 all-gather.2

commit v2 on v1

--- a/solution.py
+++ b/solution.py
@@ -49,28 +49,35 @@
     after = ring_step(own, stride, count, places, -1)
     far_top = ring_step(before[:half], stride, count, places, 1)
     far_low = ring_step(after[half:], stride, count, places, -1)
-    return before, after, jnp.concatenate([far_top, far_low], axis=0)
+    return own, before, after, jnp.concatenate([far_top, far_low], axis=0)
 
 
 def fold_rows(own, before, after, far, stride, count, places):
-    half = own.shape[0] // 2
+    half = own.shape[1] // 2
     narrow = lambda v: v.astype(jnp.bfloat16)
     wide = lambda v: v.astype(jnp.float32)
-    from_before = ring_step(narrow(far[:half]), stride, count, places, 1)
-    from_after = ring_step(narrow(far[half:]), stride, count, places, -1)
-    after = jnp.concatenate([after[:half] + wide(from_before), after[half:]], axis=0)
-    before = jnp.concatenate([before[:half], before[half:] + wide(from_after)], axis=0)
+    from_before = ring_step(narrow(far[:, :half]), stride, count, places, 1)
+    from_after = ring_step(narrow(far[:, half:]), stride, count, places, -1)
+    after = jnp.concatenate([after[:, :half] + wide(from_before), after[:, half:]], axis=1)
+    before = jnp.concatenate([before[:, :half], before[:, half:] + wide(from_after)], axis=1)
     one = ring_step(narrow(after), stride, count, places, 1)
     two = ring_step(narrow(before), stride, count, places, -1)
-    return own + wide(one) + wide(two)
-
-
-def expert(rows, up_rows, down_rows):
-    hidden = lax.dot_general(
-        rows, up_rows, (((1,), (1,)), ((), ())), preferred_element_type=jnp.float32
-    )
-    hidden = jax.nn.silu(hidden).astype(jnp.bfloat16)
-    return jnp.dot(hidden, down_rows, preferred_element_type=jnp.float32)
+    return narrow(own + wide(one) + wide(two))
+
+
+def group_hop(array, hop, groups, places, stride, is_return):
+    count = groups // 2
+    pairs = []
+    for group in range(groups):
+        for place in range(places):
+            is_other, ahead = hop // count, hop % count
+            there = (group // count ^ is_other) * count + (group % count + ahead) % count
+            row, spot = place // stride, place % stride
+            if is_other:
+                spot = (stride // 2 - 1 - spot // 2) * 2 + spot % 2
+            pair = (group * places + place, there * places + row * stride + spot)
+            pairs.append(pair[::-1] if is_return else pair)
+    return lax.ppermute(array, ("grp", "tm"), pairs)
 
 
 def attend(query_rows, widened, query_pos, key_pos, length):
@@ -116,13 +123,9 @@
     stride = places // ring
     experts = lax.axis_size("grp")
     slot_count = 5 * frames // (4 * experts)
-    units = down_weight.shape[1]
-    shard = jnp.concatenate([up_weight[0].T, down_weight[0]], axis=0)
-    weights = lax.all_gather(
-        shard,
-        "tm",
-        axis_index_groups=[[g * stride + i for i in range(stride)] for g in range(ring)],
-    )
+    lines = [[g * stride + i for i in range(stride)] for g in range(ring)]
+    up_rows = lax.all_gather(up_weight[0].T, "tm", axis_index_groups=lines, tiled=True)
+    down_rows = lax.all_gather(down_weight[0], "tm", axis_index_groups=lines, tiled=True)
     frame_start = tm_place * frames
     query_pos = frame_start + jnp.arange(frames, dtype=jnp.int32)
     key_pos = frame_start - WIN + jnp.arange(frames + 2 * WIN, dtype=jnp.int32)
@@ -148,27 +151,44 @@
     earlier = jnp.cumsum(onehot, axis=0) - onehot
     slot_index = jnp.sum(earlier * onehot, axis=1)
     is_kept = is_valid & (slot_index < slot_count)
-    target = language * slot_count + slot_index
+    group = lax.axis_index("grp")
+    count = experts // 2
+    relative = (language // count ^ group // count) * count + (language - group) % count
+    target = relative * slot_count + slot_index
     route_table = (
         (target[None, :] == jnp.arange(experts * slot_count, dtype=jnp.int32)[:, None])
         & is_kept[None, :]
     ).astype(jnp.bfloat16)
     outgoing = jnp.dot(route_table, ffn_in, preferred_element_type=jnp.float32).astype(jnp.bfloat16)
     outgoing = outgoing.reshape(experts, slot_count, model_width)
-    arrived = lax.all_to_all(outgoing, "grp", split_axis=0, concat_axis=0, tiled=True)
-    item_count = arrived.shape[1]
-    frame_rows = arrived.reshape(-1, model_width)
-    before, after, far = gather_rows(frame_rows, stride, ring, places)
-    up_rows = weights[:, :units].reshape(-1, model_width)
-    down_rows = weights[:, units:].reshape(-1, model_width)
-    all_rows = jnp.concatenate([frame_rows, before, after, far], axis=0)
-    partial_value = expert(all_rows, up_rows, down_rows).reshape(4, -1, model_width)
-    total = fold_rows(*partial_value, stride, ring, places)
-    outbound = total.astype(jnp.bfloat16).reshape(experts, item_count, model_width)
-    returned = lax.all_to_all(outbound, "grp", split_axis=0, concat_axis=0, tiled=True)
+    hops = [*range(count, experts), *range(1, count)]
+    arrived = {0: outgoing[0]}
+    for hop in hops:
+        arrived[hop] = group_hop(outgoing[hop], hop, experts, places, stride, False)
+    frame_rows = jnp.concatenate([arrived[hop] for hop in range(experts)], axis=0)
+    blocks = gather_rows(frame_rows, stride, ring, places)
+    half = frame_rows.shape[0] // 2
+    all_rows = jnp.concatenate([rows[half:] for rows in blocks] + [rows[:half] for rows in blocks], axis=0)
+    hidden = lax.dot_general(all_rows, up_rows, (((1,), (1,)), ((), ())), preferred_element_type=jnp.float32)
+    hidden = jax.nn.silu(hidden).astype(jnp.bfloat16)
+
+    def finish(hidden_rows):
+        partial = jnp.dot(hidden_rows, down_rows, preferred_element_type=jnp.float32)
+        total = fold_rows(*partial.reshape(ring, half, model_width), stride, ring, places)
+        return total.reshape(count, slot_count, model_width)
+
+    far_total = finish(hidden[: ring * half])
+    returned = {}
+    for hop in range(count, experts):
+        returned[hop] = group_hop(far_total[hop - count], hop, experts, places, stride, True)
+    near_total = finish(hidden[ring * half :])
+    returned[0] = near_total[0]
+    for hop in range(1, count):
+        returned[hop] = group_hop(near_total[hop], hop, experts, places, stride, True)
+    returned = jnp.concatenate([returned[hop] for hop in range(experts)], axis=0)
     expert_out = lax.dot_general(
         route_table,
-        returned.reshape(-1, model_width),
+        returned,
         (((0,), (0,)), ((), ())),
         preferred_element_type=jnp.float32,
     )

time: 278 us -> 320 us (1.15)
  the two profiles are of different devices: /device:TPU:32 before, /device:TPU:24 now
where the time goes in v2:
time: 320 us; the launch traced here: 319 us
  waiting for transfers between devices  131 us (41%)
  starting transfers between devices  128 us (40%)
  matrix products  19.6 us (6%)
  local copies, waits for them, and re-layouts  18.4 us (6%)
  between operations  14.9 us (5%)
  other arithmetic  6.7 us (2%)
    all_gather x1, waiting for transfers between devices, body(): lax.all_gather(down_weight[0], 'tm', axis_index_groups=lines, tiled=True)  98.4 us
    ppermute x14, starting transfers between devices, group_hop(): return lax.ppermute(array, ('grp', 'tm'), pairs)  55 us
    ppermute x12, starting transfers between devices, ring_step(): lax.ppermute(array, 'tm', [(i, i + stride * ((i // stride + shift) % coun...  45 us
    ppermute x2, starting transfers between devices, with_halo(): lax.ppermute(head, axis, [((i + 1) % count, i) for i in range(ends)])  24.2 us
    ppermute x12, waiting for transfers between devices, ring_step(): lax.ppermute(array, 'tm', [(i, i + stride * ((i // stride + shift) % coun...  10.4 us
    ppermute x14, waiting for transfers between devices, group_hop(): return lax.ppermute(array, ('grp', 'tm'), pairs)  10.2 us
    concatenate x1, local copies, waits for them, and re-layouts, body(): jnp.concatenate([rows[half:] for rows in blocks] + [rows[:half] for rows...  8 us
    ppermute x2, waiting for transfers between devices, with_halo(): lax.ppermute(tail, axis, [(i, (i + 1) % count) for i in range(ends)])  7.51 us
  transfers between devices with their start and end apart: 32, of which 11 were waited for; matrix products, arithmetic and copies ran while one was open for 12% of the time, Pallas kernels for 0%

profile of v2, /device:TPU:24, one launch (start us, length us, event | category | flops | bytes accessed | tf_op | source)
XLA Modules:
  0.0 318.7 jit_solution(5661578282083673636)
XLA Ops:
  11.8 12.8 %collective-permute-start.1 = (bf16[128,2,1536]{0,2,1:T(8,128)(2,1)S(1)}, bf16[128,2,1536]{0,2,1:T(8,128)(2,1)S(1)}, u32[]{:S(2)}, u32[]{:S(2)}) collective-permute-start(bf16[128,2,1536]{0,2,1:T(8,128)(2,1)S(1)} %pad_maximum_fusion.1), channel_id=1, source_target_pairs={{1,0},{2,1},{3,2},{4,3},{5,4},{6,5},{7,6},{8,7},{9,8},{10,9},{11,1... | collective-permute-start | bytes 2359304 | tf_op jit(solution)/shard_map/ppermute | solution.py:22
  28.6 7.5 %collective-permute-done = bf16[128,2,1536]{0,2,1:T(8,128)(2,1)S(1)} collective-permute-done((bf16[128,2,1536]{0,2,1:T(8,128)(2,1)S(1)}, bf16[128,2,1536]{0,2,1:T(8,128)(2,1)S(1)}, u32[]{:S(2)}, u32[]{:S(2)}) %collective-permute-start) | collective-permute-done | bytes 786464 | tf_op jit(solution)/shard_map/ppermute | solution.py:20
  48.6 11.4 %collective-permute-start.3 = (bf16[15,1536]{1,0:T(8,128)(2,1)S(1)}, bf16[15,1536]{1,0:T(8,128)(2,1)S(1)}, u32[]{:S(2)}, u32[]{:S(2)}) collective-permute-start(bf16[15,1536]{1,0:T(8,128)(2,1)S(1)} %get-tuple-element.69), channel_id=1, source_target_pairs={{1,0},{2,1},{3,2},{4,3},{5,4},{6,5},{7,6},{8,7},{9,8},{10,9},{11,1... | collective-permute-start | bytes 138248 | tf_op jit(solution)/shard_map/ppermute | solution.py:22
  62.0 4.2 %convert_reduce_fusion = (f32[128]{0:T(128)S(1)}, bf16[128,1536]{1,0:T(8,128)(2,1)S(1)}) fusion(bf16[15,1536]{1,0:T(8,128)(2,1)S(1)} %collective-permute-done.3, bf16[128,1536]{1,0:T(8,128)(2,1)S(1)} %fusion.27, f32[1536]{0:T(1024)S(1)} %get-tuple-element.34, f32[1536]{0:T(1024)S(1)} %get-tuple-element.35, f32[1536]{0:T(1024)S(1)} %get-tuple-element.6, ...), kind=kLoop, calls=%fused_computation.51 | loop fusion | flops 37552000 | bytes 1462784 | tf_op jit(solution)/shard_map/reduce_sum | solution.py:30
  67.0 6.1 %collective-permute-start.10 = (bf16[20,1536]{1,0:T(8,128)(2,1)S(1)}, bf16[20,1536]{1,0:T(8,128)(2,1)S(1)}, u32[]{:S(2)}, u32[]{:S(2)}) collective-permute-start(bf16[20,1536]{1,0:T(8,128)(2,1)S(1)} %get-tuple-element.60), channel_id=1, source_target_pairs={{0,192},{1,193},{2,194},{3,195},{4,196},{5,197},{6,198},{7,199},{8... | collective-permute-start | bytes 184328 | tf_op jit(solution)/shard_map/ppermute | solution.py:80
  75.1 4.1 %collective-permute-start.5 = (bf16[20,1536]{1,0:T(8,128)(2,1)S(1)}, bf16[20,1536]{1,0:T(8,128)(2,1)S(1)}, u32[]{:S(2)}, u32[]{:S(2)}) collective-permute-start(bf16[20,1536]{1,0:T(8,128)(2,1)S(1)} %get-tuple-element.66), channel_id=1, source_target_pairs={{0,334},{1,335},{2,332},{3,333},{4,330},{5,331},{6,328},{7,329},{8... | collective-permute-start | bytes 184328 | tf_op jit(solution)/shard_map/ppermute | solution.py:80
  79.2 4.9 %collective-permute-start.6 = (bf16[20,1536]{1,0:T(8,128)(2,1)S(1)}, bf16[20,1536]{1,0:T(8,128)(2,1)S(1)}, u32[]{:S(2)}, u32[]{:S(2)}) collective-permute-start(bf16[20,1536]{1,0:T(8,128)(2,1)S(1)} %get-tuple-element.65), channel_id=1, source_target_pairs={{0,398},{1,399},{2,396},{3,397},{4,394},{5,395},{6,392},{7,393},{8... | collective-permute-start | bytes 184328 | tf_op jit(solution)/shard_map/ppermute | solution.py:80
  84.1 5.8 %collective-permute-start.7 = (bf16[20,1536]{1,0:T(8,128)(2,1)S(1)}, bf16[20,1536]{1,0:T(8,128)(2,1)S(1)}, u32[]{:S(2)}, u32[]{:S(2)}) collective-permute-start(bf16[20,1536]{1,0:T(8,128)(2,1)S(1)} %get-tuple-element.64), channel_id=1, source_target_pairs={{0,462},{1,463},{2,460},{3,461},{4,458},{5,459},{6,456},{7,457},{8... | collective-permute-start | bytes 184328 | tf_op jit(solution)/shard_map/ppermute | solution.py:80
  101.2 9.8 %collective-permute-start.12 = (bf16[160,1536]{1,0:T(8,128)(2,1)S(1)}, bf16[160,1536]{1,0:T(8,128)(2,1)S(1)}, u32[]{:S(2)}, u32[]{:S(2)}) collective-permute-start(bf16[160,1536]{1,0:T(8,128)(2,1)S(1)} %concatenate.69), channel_id=1, source_target_pairs={{0,48},{1,49},{2,50},{3,51},{4,52},{5,53},{6,54},{7,55},{8,56},{9,... | collective-permute-start | bytes 1474568 | tf_op jit(solution)/shard_map/ppermute | solution.py:41
  113.5 4.8 %collective-permute-done.12 = bf16[160,1536]{1,0:T(8,128)(2,1)S(1)} collective-permute-done((bf16[160,1536]{1,0:T(8,128)(2,1)S(1)}, bf16[160,1536]{1,0:T(8,128)(2,1)S(1)}, u32[]{:S(2)}, u32[]{:S(2)}) %collective-permute-start.12) | collective-permute-done | bytes 491552 | tf_op jit(solution)/shard_map/ppermute | solution.py:41
  121.8 3.6 %collective-permute-start.14 = (bf16[80,1536]{1,0:T(8,128)(2,1)S(1)}, bf16[80,1536]{1,0:T(8,128)(2,1)S(1)}, u32[]{:S(2)}, u32[]{:S(2)}) collective-permute-start(bf16[80,1536]{1,0:T(8,128)(2,1)S(1)} %get-tuple-element.58), channel_id=1, source_target_pairs={{0,16},{1,17},{2,18},{3,19},{4,20},{5,21},{6,22},{7,23},{8,24},{9,... | collective-permute-start | bytes 737288 | tf_op jit(solution)/shard_map/ppermute | solution.py:41
  125.4 4.9 %collective-permute-done.13 = bf16[80,1536]{1,0:T(8,128)(2,1)S(1)} collective-permute-done((bf16[80,1536]{1,0:T(8,128)(2,1)S(1)}, bf16[80,1536]{1,0:T(8,128)(2,1)S(1)}, u32[]{:S(2)}, u32[]{:S(2)}) %collective-permute-start.13) | collective-permute-done | bytes 245792 | tf_op jit(solution)/shard_map/ppermute | solution.py:41
  131.1 8.0 %concatenate.70 = bf16[640,1536]{1,0:T(8,128)(2,1)S(1)} concatenate(bf16[20,1536]{1,0:T(8,128)(2,1)} %copy-done.3, bf16[20,1536]{1,0:T(8,128)(2,1)} %copy-done.4, bf16[20,1536]{1,0:T(8,128)(2,1)} %copy-done.5, bf16[20,1536]{1,0:T(8,128)(2,1)} %copy-done.6, bf16[80,1536]{1,0:T(8,128)(2,1)S(1)} %get-tuple-element.59, bf16[80,1536]{1,0:T(8,128)(2,1)S(1)} %get-tuple-element.57, ...), dimensions={0} | concatenate | bytes 3932160 | tf_op jit(solution)/shard_map/concatenate | solution.py:171
  139.1 7.1 %multiply_convert_fusion = bf16[640,1536]{1,0:T(8,128)(2,1)} fusion(bf16[640,1536]{1,0:T(8,128)(2,1)S(1)} %concatenate.70, bf16[1536,1536]{1,0:T(8,128)(2,1)} %all-gather.4.cloned.1.call-done), kind=kOutput, calls=%fused_computation.5 | convolution fusion | flops 3024814080 | bytes 8650752 | tf_op jit(solution)/shard_map/dot_general | solution.py:172
  146.2 98.4 %all-gather.6.cloned.1.call-done = bf16[1,1536,1536]{2,1,0:T(8,128)(2,1)} async-done(((bf16[1,96,1536]{2,1,0:T(8,128)(2,1)}), bf16[1,1536,1536]{2,1,0:T(8,128)(2,1)}) %all-gather.6.cloned.1.call-update) | async-done | bytes 4718608 | tf_op jit(solution)/shard_map/all_gather | solution.py:128
  244.6 4.5 %fusion.100 = (bf16[320,1536]{1,0:T(8,128)(2,1)S(1)}, f32[320,1536]{1,0:T(8,128)S(1)}) fusion(bf16[1,1536,1536]{2,1,0:T(8,128)(2,1)} %all-gather.6.cloned.1.call-done, bf16[640,1536]{1,0:T(8,128)(2,1)} %multiply_convert_fusion), kind=kOutput, calls=%fused_computation.221 | convolution fusion | flops 1510440960 | bytes 8650752 | tf_op jit(solution)/shard_map/dot_general | solution.py:176
  251.6 3.6 %collective-permute-start.24 = (bf16[80,768]{1,0:T(8,128)(2,1)S(1)}, bf16[80,768]{1,0:T(8,128)(2,1)S(1)}, u32[]{:S(2)}, u32[]{:S(2)}) collective-permute-start(bf16[80,768]{1,0:T(8,128)(2,1)S(1)} %get-tuple-element.49), channel_id=1, source_target_pairs={{0,48},{1,49},{2,50},{3,51},{4,52},{5,53},{6,54},{7,55},{8,56},{9,... | collective-permute-start | bytes 368648 | tf_op jit(solution)/shard_map/ppermute | solution.py:41
  256.9 3.7 %collective-permute-start.15 = (bf16[80,768]{1,0:T(8,128)(2,1)S(1)}, bf16[80,768]{1,0:T(8,128)(2,1)S(1)}, u32[]{:S(2)}, u32[]{:S(2)}) collective-permute-start(bf16[80,768]{1,0:T(8,128)(2,1)S(1)} %get-tuple-element.52), channel_id=1, source_target_pairs={{0,16},{1,17},{2,18},{3,19},{4,20},{5,21},{6,22},{7,23},{8,24},{9,... | collective-permute-start | bytes 368648 | tf_op jit(solution)/shard_map/ppermute | solution.py:41
  262.9 4.9 %collective-permute-start.23 = (bf16[80,1536]{1,0:T(8,128)(2,1)S(1)}, bf16[80,1536]{1,0:T(8,128)(2,1)S(1)}, u32[]{:S(2)}, u32[]{:S(2)}) collective-permute-start(bf16[80,1536]{1,0:T(8,128)(2,1)S(1)} %pad_maximum_fusion.6), channel_id=1, source_target_pairs={{0,16},{1,17},{2,18},{3,19},{4,20},{5,21},{6,22},{7,23},{8,24},{9,... | collective-permute-start | bytes 737288 | tf_op jit(solution)/shard_map/ppermute | solution.py:41
  269.9 5.1 %collective-permute-start.16 = (bf16[80,1536]{1,0:T(8,128)(2,1)S(1)}, bf16[80,1536]{1,0:T(8,128)(2,1)S(1)}, u32[]{:S(2)}, u32[]{:S(2)}) collective-permute-start(bf16[80,1536]{1,0:T(8,128)(2,1)S(1)} %pad_maximum_fusion.4), channel_id=1, source_target_pairs={{0,16},{1,17},{2,18},{3,19},{4,20},{5,21},{6,22},{7,23},{8,24},{9,... | collective-permute-start | bytes 737288 | tf_op jit(solution)/shard_map/ppermute | solution.py:41
  281.1 5.9 %collective-permute-start.27 = (bf16[20,1536]{1,0:T(8,128)(2,1)S(1)}, bf16[20,1536]{1,0:T(8,128)(2,1)S(1)}, u32[]{:S(2)}, u32[]{:S(2)}) collective-permute-start(bf16[20,1536]{1,0:T(8,128)(2,1)S(1)} %get-tuple-element.72), channel_id=1, source_target_pairs={{334,0},{335,1},{332,2},{333,3},{330,4},{331,5},{328,6},{329,7},{3... | collective-permute-start | bytes 184328 | tf_op jit(solution)/shard_map/ppermute | solution.py:80
  287.1 3.7 %collective-permute-start.28 = (bf16[20,1536]{1,0:T(8,128)(2,1)S(1)}, bf16[20,1536]{1,0:T(8,128)(2,1)S(1)}, u32[]{:S(2)}, u32[]{:S(2)}) collective-permute-start(bf16[20,1536]{1,0:T(8,128)(2,1)S(1)} %get-tuple-element.71), channel_id=1, source_target_pairs={{398,0},{399,1},{396,2},{397,3},{394,4},{395,5},{392,6},{393,7},{3... | collective-permute-start | bytes 184328 | tf_op jit(solution)/shard_map/ppermute | solution.py:80
  290.8 3.9 %collective-permute-start.29 = (bf16[20,1536]{1,0:T(8,128)(2,1)S(1)}, bf16[20,1536]{1,0:T(8,128)(2,1)S(1)}, u32[]{:S(2)}, u32[]{:S(2)}) collective-permute-start(bf16[20,1536]{1,0:T(8,128)(2,1)S(1)} %get-tuple-element.70), channel_id=1, source_target_pairs={{462,0},{463,1},{460,2},{461,3},{458,4},{459,5},{456,6},{457,7},{4... | collective-permute-start | bytes 184328 | tf_op jit(solution)/shard_map/ppermute | solution.py:80
  294.8 4.3 %collective-permute-start.19 = (bf16[20,1536]{1,0:T(8,128)(2,1)S(1)}, bf16[20,1536]{1,0:T(8,128)(2,1)S(1)}, u32[]{:S(2)}, u32[]{:S(2)}) collective-permute-start(bf16[20,1536]{1,0:T(8,128)(2,1)S(1)} %get-tuple-element.76), channel_id=1, source_target_pairs={{64,0},{65,1},{66,2},{67,3},{68,4},{69,5},{70,6},{71,7},{72,8},{73... | collective-permute-start | bytes 184328 | tf_op jit(solution)/shard_map/ppermute | solution.py:80
  (124 shorter events, 71.0 us)
Async XLA Ops:
  6.5 132.6 %all-gather.4.cloned.1.call-start = ((), (), s32[]{:S(2)}) async-start(), calls=%async_computation | async-start | bytes 5013504 | tf_op jit(solution)/shard_map/all_gather | solution.py:127
  7.3 237.4 %all-gather.6.cloned.1.call-start = ((), (), s32[]{:S(2)}) async-start(), calls=%async_computation.1 | async-start | bytes 5013504 | tf_op jit(solution)/shard_map/all_gather | solution.py:128
  9.8 26.3 %collective-permute-start = (bf16[128,2,1536]{0,2,1:T(8,128)(2,1)S(1)}, bf16[128,2,1536]{0,2,1:T(8,128)(2,1)S(1)}, u32[]{:S(2)}, u32[]{:S(2)}) collective-permute-start(bf16[128,2,1536]{0,2,1:T(8,128)(2,1)S(1)} %pad_maximum_fusion.1), channel_id=1, source_target_pairs={{0,1},{1,2},{2,3},{3,4},{4,5},{5,6},{6,7},{7,8},{8,9},{9,10},{10,1... | collective-permute-start | bytes 2359304 | tf_op jit(solution)/shard_map/ppermute | solution.py:20
  11.8 27.5 %collective-permute-start.1 = (bf16[128,2,1536]{0,2,1:T(8,128)(2,1)S(1)}, bf16[128,2,1536]{0,2,1:T(8,128)(2,1)S(1)}, u32[]{:S(2)}, u32[]{:S(2)}) collective-permute-start(bf16[128,2,1536]{0,2,1:T(8,128)(2,1)S(1)} %pad_maximum_fusion.1), channel_id=1, source_target_pairs={{1,0},{2,1},{3,2},{4,3},{5,4},{6,5},{7,6},{8,7},{9,8},{10,9},{11,1... | collective-permute-start | bytes 2359304 | tf_op jit(solution)/shard_map/ppermute | solution.py:22
  46.6 14.7 %collective-permute-start.2 = (bf16[15,1536]{1,0:T(8,128)(2,1)S(1)}, bf16[15,1536]{1,0:T(8,128)(2,1)S(1)}, u32[]{:S(2)}, u32[]{:S(2)}) collective-permute-start(bf16[15,1536]{1,0:T(8,128)(2,1)S(1)} %get-tuple-element.68), channel_id=1, source_target_pairs={{0,1},{1,2},{2,3},{3,4},{4,5},{5,6},{6,7},{7,8},{8,9},{9,10},{10,1... | collective-permute-start | bytes 138248 | tf_op jit(solution)/shard_map/ppermute | solution.py:20
  48.6 13.5 %collective-permute-start.3 = (bf16[15,1536]{1,0:T(8,128)(2,1)S(1)}, bf16[15,1536]{1,0:T(8,128)(2,1)S(1)}, u32[]{:S(2)}, u32[]{:S(2)}) collective-permute-start(bf16[15,1536]{1,0:T(8,128)(2,1)S(1)} %get-tuple-element.69), channel_id=1, source_target_pairs={{1,0},{2,1},{3,2},{4,3},{5,4},{6,5},{7,6},{8,7},{9,8},{10,9},{11,1... | collective-permute-start | bytes 138248 | tf_op jit(solution)/shard_map/ppermute | solution.py:22
  67.0 22.8 %collective-permute-start.10 = (bf16[20,1536]{1,0:T(8,128)(2,1)S(1)}, bf16[20,1536]{1,0:T(8,128)(2,1)S(1)}, u32[]{:S(2)}, u32[]{:S(2)}) collective-permute-start(bf16[20,1536]{1,0:T(8,128)(2,1)S(1)} %get-tuple-element.60), channel_id=1, source_target_pairs={{0,192},{1,193},{2,194},{3,195},{4,196},{5,197},{6,198},{7,199},{8... | collective-permute-start | bytes 184328 | tf_op jit(solution)/shard_map/ppermute | solution.py:80
  73.2 19.5 %collective-permute-start.4 = (bf16[20,1536]{1,0:T(8,128)(2,1)S(1)}, bf16[20,1536]{1,0:T(8,128)(2,1)S(1)}, u32[]{:S(2)}, u32[]{:S(2)}) collective-permute-start(bf16[20,1536]{1,0:T(8,128)(2,1)S(1)} %get-tuple-element.67), channel_id=1, source_target_pairs={{0,270},{1,271},{2,268},{3,269},{4,266},{5,267},{6,264},{7,265},{8... | collective-permute-start | bytes 184328 | tf_op jit(solution)/shard_map/ppermute | solution.py:80
  75.1 20.6 %collective-permute-start.5 = (bf16[20,1536]{1,0:T(8,128)(2,1)S(1)}, bf16[20,1536]{1,0:T(8,128)(2,1)S(1)}, u32[]{:S(2)}, u32[]{:S(2)}) collective-permute-start(bf16[20,1536]{1,0:T(8,128)(2,1)S(1)} %get-tuple-element.66), channel_id=1, source_target_pairs={{0,334},{1,335},{2,332},{3,333},{4,330},{5,331},{6,328},{7,329},{8... | collective-permute-start | bytes 184328 | tf_op jit(solution)/shard_map/ppermute | solution.py:80
  79.2 16.4 %collective-permute-start.6 = (bf16[20,1536]{1,0:T(8,128)(2,1)S(1)}, bf16[20,1536]{1,0:T(8,128)(2,1)S(1)}, u32[]{:S(2)}, u32[]{:S(2)}) collective-permute-start(bf16[20,1536]{1,0:T(8,128)(2,1)S(1)} %get-tuple-element.65), channel_id=1, source_target_pairs={{0,398},{1,399},{2,396},{3,397},{4,394},{5,395},{6,392},{7,393},{8... | collective-permute-start | bytes 184328 | tf_op jit(solution)/shard_map/ppermute | solution.py:80
  84.1 11.6 %collective-permute-start.7 = (bf16[20,1536]{1,0:T(8,128)(2,1)S(1)}, bf16[20,1536]{1,0:T(8,128)(2,1)S(1)}, u32[]{:S(2)}, u32[]{:S(2)}) collective-permute-start(bf16[20,1536]{1,0:T(8,128)(2,1)S(1)} %get-tuple-element.64), channel_id=1, source_target_pairs={{0,462},{1,463},{2,460},{3,461},{4,458},{5,459},{6,456},{7,457},{8... | collective-permute-start | bytes 184328 | tf_op jit(solution)/shard_map/ppermute | solution.py:80
  101.2 17.1 %collective-permute-start.12 = (bf16[160,1536]{1,0:T(8,128)(2,1)S(1)}, bf16[160,1536]{1,0:T(8,128)(2,1)S(1)}, u32[]{:S(2)}, u32[]{:S(2)}) collective-permute-start(bf16[160,1536]{1,0:T(8,128)(2,1)S(1)} %concatenate.69), channel_id=1, source_target_pairs={{0,48},{1,49},{2,50},{3,51},{4,52},{5,53},{6,54},{7,55},{8,56},{9,... | collective-permute-start | bytes 1474568 | tf_op jit(solution)/shard_map/ppermute | solution.py:41
  111.0 10.8 %collective-permute-start.11 = (bf16[160,1536]{1,0:T(8,128)(2,1)S(1)}, bf16[160,1536]{1,0:T(8,128)(2,1)S(1)}, u32[]{:S(2)}, u32[]{:S(2)}) collective-permute-start(bf16[160,1536]{1,0:T(8,128)(2,1)S(1)} %concatenate.69), channel_id=1, source_target_pairs={{0,16},{1,17},{2,18},{3,19},{4,20},{5,21},{6,22},{7,23},{8,24},{9,... | collective-permute-start | bytes 1474568 | tf_op jit(solution)/shard_map/ppermute | solution.py:41
  118.3 12.0 %collective-permute-start.13 = (bf16[80,1536]{1,0:T(8,128)(2,1)S(1)}, bf16[80,1536]{1,0:T(8,128)(2,1)S(1)}, u32[]{:S(2)}, u32[]{:S(2)}) collective-permute-start(bf16[80,1536]{1,0:T(8,128)(2,1)S(1)} %get-tuple-element.57), channel_id=1, source_target_pairs={{0,48},{1,49},{2,50},{3,51},{4,52},{5,53},{6,54},{7,55},{8,56},{9,... | collective-permute-start | bytes 737288 | tf_op jit(solution)/shard_map/ppermute | solution.py:41
  249.1 13.7 %collective-permute-start.22 = (bf16[80,768]{1,0:T(8,128)(2,1)S(1)}, bf16[80,768]{1,0:T(8,128)(2,1)S(1)}, u32[]{:S(2)}, u32[]{:S(2)}) collective-permute-start(bf16[80,768]{1,0:T(8,128)(2,1)S(1)} %get-tuple-element.48), channel_id=1, source_target_pairs={{0,16},{1,17},{2,18},{3,19},{4,20},{5,21},{6,22},{7,23},{8,24},{9,... | collective-permute-start | bytes 368648 | tf_op jit(solution)/shard_map/ppermute | solution.py:41
  251.6 11.2 %collective-permute-start.24 = (bf16[80,768]{1,0:T(8,128)(2,1)S(1)}, bf16[80,768]{1,0:T(8,128)(2,1)S(1)}, u32[]{:S(2)}, u32[]{:S(2)}) collective-permute-start(bf16[80,768]{1,0:T(8,128)(2,1)S(1)} %get-tuple-element.49), channel_id=1, source_target_pairs={{0,48},{1,49},{2,50},{3,51},{4,52},{5,53},{6,54},{7,55},{8,56},{9,... | collective-permute-start | bytes 368648 | tf_op jit(solution)/shard_map/ppermute | solution.py:41
  256.9 12.8 %collective-permute-start.15 = (bf16[80,768]{1,0:T(8,128)(2,1)S(1)}, bf16[80,768]{1,0:T(8,128)(2,1)S(1)}, u32[]{:S(2)}, u32[]{:S(2)}) collective-permute-start(bf16[80,768]{1,0:T(8,128)(2,1)S(1)} %get-tuple-element.52), channel_id=1, source_target_pairs={{0,16},{1,17},{2,18},{3,19},{4,20},{5,21},{6,22},{7,23},{8,24},{9,... | collective-permute-start | bytes 368648 | tf_op jit(solution)/shard_map/ppermute | solution.py:41
  262.9 14.1 %collective-permute-start.23 = (bf16[80,1536]{1,0:T(8,128)(2,1)S(1)}, bf16[80,1536]{1,0:T(8,128)(2,1)S(1)}, u32[]{:S(2)}, u32[]{:S(2)}) collective-permute-start(bf16[80,1536]{1,0:T(8,128)(2,1)S(1)} %pad_maximum_fusion.6), channel_id=1, source_target_pairs={{0,16},{1,17},{2,18},{3,19},{4,20},{5,21},{6,22},{7,23},{8,24},{9,... | collective-permute-start | bytes 737288 | tf_op jit(solution)/shard_map/ppermute | solution.py:41
  269.9 20.9 %collective-permute-start.16 = (bf16[80,1536]{1,0:T(8,128)(2,1)S(1)}, bf16[80,1536]{1,0:T(8,128)(2,1)S(1)}, u32[]{:S(2)}, u32[]{:S(2)}) collective-permute-start(bf16[80,1536]{1,0:T(8,128)(2,1)S(1)} %pad_maximum_fusion.4), channel_id=1, source_target_pairs={{0,16},{1,17},{2,18},{3,19},{4,20},{5,21},{6,22},{7,23},{8,24},{9,... | collective-permute-start | bytes 737288 | tf_op jit(solution)/shard_map/ppermute | solution.py:41
  275.0 19.6 %collective-permute-start.18 = (bf16[80,1536]{1,0:T(8,128)(2,1)S(1)}, bf16[80,1536]{1,0:T(8,128)(2,1)S(1)}, u32[]{:S(2)}, u32[]{:S(2)}) collective-permute-start(bf16[80,1536]{1,0:T(8,128)(2,1)S(1)} %pad_maximum_fusion.5), channel_id=1, source_target_pairs={{0,48},{1,49},{2,50},{3,51},{4,52},{5,53},{6,54},{7,55},{8,56},{9,... | collective-permute-start | bytes 737288 | tf_op jit(solution)/shard_map/ppermute | solution.py:41
  277.8 21.2 %collective-permute-start.26 = (bf16[20,1536]{1,0:T(8,128)(2,1)S(1)}, bf16[20,1536]{1,0:T(8,128)(2,1)S(1)}, u32[]{:S(2)}, u32[]{:S(2)}) collective-permute-start(bf16[20,1536]{1,0:T(8,128)(2,1)S(1)} %get-tuple-element.73), channel_id=1, source_target_pairs={{270,0},{271,1},{268,2},{269,3},{266,4},{267,5},{264,6},{265,7},{2... | collective-permute-start | bytes 184328 | tf_op jit(solution)/shard_map/ppermute | solution.py:80
  281.1 21.5 %collective-permute-start.27 = (bf16[20,1536]{1,0:T(8,128)(2,1)S(1)}, bf16[20,1536]{1,0:T(8,128)(2,1)S(1)}, u32[]{:S(2)}, u32[]{:S(2)}) collective-permute-start(bf16[20,1536]{1,0:T(8,128)(2,1)S(1)} %get-tuple-element.72), channel_id=1, source_target_pairs={{334,0},{335,1},{332,2},{333,3},{330,4},{331,5},{328,6},{329,7},{3... | collective-permute-start | bytes 184328 | tf_op jit(solution)/shard_map/ppermute | solution.py:80
  287.1 17.5 %collective-permute-start.28 = (bf16[20,1536]{1,0:T(8,128)(2,1)S(1)}, bf16[20,1536]{1,0:T(8,128)(2,1)S(1)}, u32[]{:S(2)}, u32[]{:S(2)}) collective-permute-start(bf16[20,1536]{1,0:T(8,128)(2,1)S(1)} %get-tuple-element.71), channel_id=1, source_target_pairs={{398,0},{399,1},{396,2},{397,3},{394,4},{395,5},{392,6},{393,7},{3... | collective-permute-start | bytes 184328 | tf_op jit(solution)/shard_map/ppermute | solution.py:80
  290.8 13.7 %collective-permute-start.29 = (bf16[20,1536]{1,0:T(8,128)(2,1)S(1)}, bf16[20,1536]{1,0:T(8,128)(2,1)S(1)}, u32[]{:S(2)}, u32[]{:S(2)}) collective-permute-start(bf16[20,1536]{1,0:T(8,128)(2,1)S(1)} %get-tuple-element.70), channel_id=1, source_target_pairs={{462,0},{463,1},{460,2},{461,3},{458,4},{459,5},{456,6},{457,7},{4... | collective-permute-start | bytes 184328 | tf_op jit(solution)/shard_map/ppermute | solution.py:80
  (22 other events, 334.0 us)
Sparse Core Ops, SparseCore 0:
  9.4 124.4 all-gather.3
  136.0 108.6 all-gather.5

commit v3 on v2

--- a/solution.py
+++ b/solution.py
@@ -3,6 +3,8 @@
 import jax
 import jax.numpy as jnp
 from jax import lax
+from jax.experimental import pallas as pl
+from jax.experimental.pallas import tpu as pltpu
 from jax.sharding import PartitionSpec as P
 
 HEAD = 128
@@ -37,40 +39,15 @@
     return with_halo(source, (("tm", 0),), rim_width)
 
 
-def ring_step(array, stride, count, places, shift):
-    return lax.ppermute(
-        array, "tm", [(i, i + stride * ((i // stride + shift) % count - i // stride)) for i in range(places)]
-    )
-
-
-def gather_rows(own, stride, count, places):
-    half = own.shape[0] // 2
-    before = ring_step(own, stride, count, places, 1)
-    after = ring_step(own, stride, count, places, -1)
-    far_top = ring_step(before[:half], stride, count, places, 1)
-    far_low = ring_step(after[half:], stride, count, places, -1)
-    return own, before, after, jnp.concatenate([far_top, far_low], axis=0)
-
-
-def fold_rows(own, before, after, far, stride, count, places):
-    half = own.shape[1] // 2
-    narrow = lambda v: v.astype(jnp.bfloat16)
-    wide = lambda v: v.astype(jnp.float32)
-    from_before = ring_step(narrow(far[:, :half]), stride, count, places, 1)
-    from_after = ring_step(narrow(far[:, half:]), stride, count, places, -1)
-    after = jnp.concatenate([after[:, :half] + wide(from_before), after[:, half:]], axis=1)
-    before = jnp.concatenate([before[:, :half], before[:, half:] + wide(from_after)], axis=1)
-    one = ring_step(narrow(after), stride, count, places, 1)
-    two = ring_step(narrow(before), stride, count, places, -1)
-    return narrow(own + wide(one) + wide(two))
-
-
-def group_hop(array, hop, groups, places, stride, is_return):
+def place_hop(array, places, to):
+    return lax.ppermute(array, "tm", [(i, to(i)) for i in range(places)])
+
+
+def group_hop(array, ahead, is_other, groups, places, stride, is_return):
     count = groups // 2
     pairs = []
     for group in range(groups):
         for place in range(places):
-            is_other, ahead = hop // count, hop % count
             there = (group // count ^ is_other) * count + (group % count + ahead) % count
             row, spot = place // stride, place % stride
             if is_other:
@@ -78,6 +55,47 @@
             pair = (group * places + place, there * places + row * stride + spot)
             pairs.append(pair[::-1] if is_return else pair)
     return lax.ppermute(array, ("grp", "tm"), pairs)
+
+
+def expert_kernel(rows_ref, weights_ref, out_ref):
+    shards, twice, width = weights_ref.shape
+    units = twice // 2
+    up = weights_ref[:, :units, :].reshape(shards * units, width)
+    down = weights_ref[:, units:, :].reshape(shards * units, width)
+    hidden = lax.dot_general(
+        rows_ref[...], up, (((1,), (1,)), ((), ())), preferred_element_type=jnp.float32
+    )
+    hidden = (hidden / (1.0 + jnp.exp(-hidden))).astype(jnp.bfloat16)
+    part = jnp.dot(hidden, down, preferred_element_type=jnp.float32)
+
+    @pl.when(pl.program_id(0) == 0)
+    def _():
+        out_ref[...] = part
+
+    @pl.when(pl.program_id(0) > 0)
+    def _():
+        out_ref[...] += part
+
+
+def expert(rows, weights, step=4):
+    count, width = rows.shape
+    shards, twice, _ = weights.shape
+    return pl.pallas_call(
+        expert_kernel,
+        grid=(shards // step,),
+        in_specs=[
+            pl.BlockSpec((count, width), lambda i: (0, 0)),
+            pl.BlockSpec((step, twice, width), lambda i: (i, 0, 0)),
+        ],
+        out_specs=pl.BlockSpec((count, width), lambda i: (0, 0)),
+        out_shape=jax.ShapeDtypeStruct((count, width), jnp.float32),
+        cost_estimate=pl.CostEstimate(
+            flops=2 * count * width * shards * twice,
+            bytes_accessed=2 * weights.size + 6 * rows.size,
+            transcendentals=count * shards * twice // 2,
+        ),
+        compiler_params=pltpu.CompilerParams(vmem_limit_bytes=40 * 2**20),
+    )(rows, weights)
 
 
 def attend(query_rows, widened, query_pos, key_pos, length):
@@ -123,9 +141,13 @@
     stride = places // ring
     experts = lax.axis_size("grp")
     slot_count = 5 * frames // (4 * experts)
-    lines = [[g * stride + i for i in range(stride)] for g in range(ring)]
-    up_rows = lax.all_gather(up_weight[0].T, "tm", axis_index_groups=lines, tiled=True)
-    down_rows = lax.all_gather(down_weight[0], "tm", axis_index_groups=lines, tiled=True)
+    shard = jnp.concatenate([up_weight[0].T, down_weight[0]], axis=0)
+    loops = []
+    for pair in range(ring // 2):
+        for core in range(2):
+            up_line = [2 * pair * stride + z * 2 + core for z in range(stride // 2)]
+            loops.append(up_line + [i + stride for i in up_line[::-1]])
+    weights = lax.all_gather(shard, "tm", axis_index_groups=loops)
     frame_start = tm_place * frames
     query_pos = frame_start + jnp.arange(frames, dtype=jnp.int32)
     key_pos = frame_start - WIN + jnp.arange(frames + 2 * WIN, dtype=jnp.int32)
@@ -153,42 +175,40 @@
     is_kept = is_valid & (slot_index < slot_count)
     group = lax.axis_index("grp")
     count = experts // 2
-    relative = (language // count ^ group // count) * count + (language - group) % count
+    relative = (language - group) % count * 2 + (language // count ^ group // count)
     target = relative * slot_count + slot_index
     route_table = (
         (target[None, :] == jnp.arange(experts * slot_count, dtype=jnp.int32)[:, None])
         & is_kept[None, :]
     ).astype(jnp.bfloat16)
     outgoing = jnp.dot(route_table, ffn_in, preferred_element_type=jnp.float32).astype(jnp.bfloat16)
-    outgoing = outgoing.reshape(experts, slot_count, model_width)
-    hops = [*range(count, experts), *range(1, count)]
-    arrived = {0: outgoing[0]}
-    for hop in hops:
-        arrived[hop] = group_hop(outgoing[hop], hop, experts, places, stride, False)
-    frame_rows = jnp.concatenate([arrived[hop] for hop in range(experts)], axis=0)
-    blocks = gather_rows(frame_rows, stride, ring, places)
-    half = frame_rows.shape[0] // 2
-    all_rows = jnp.concatenate([rows[half:] for rows in blocks] + [rows[:half] for rows in blocks], axis=0)
-    hidden = lax.dot_general(all_rows, up_rows, (((1,), (1,)), ((), ())), preferred_element_type=jnp.float32)
-    hidden = jax.nn.silu(hidden).astype(jnp.bfloat16)
-
-    def finish(hidden_rows):
-        partial = jnp.dot(hidden_rows, down_rows, preferred_element_type=jnp.float32)
-        total = fold_rows(*partial.reshape(ring, half, model_width), stride, ring, places)
-        return total.reshape(count, slot_count, model_width)
-
-    far_total = finish(hidden[: ring * half])
-    returned = {}
-    for hop in range(count, experts):
-        returned[hop] = group_hop(far_total[hop - count], hop, experts, places, stride, True)
-    near_total = finish(hidden[ring * half :])
-    returned[0] = near_total[0]
-    for hop in range(1, count):
-        returned[hop] = group_hop(near_total[hop], hop, experts, places, stride, True)
-    returned = jnp.concatenate([returned[hop] for hop in range(experts)], axis=0)
+    hop = lambda v, ahead, is_other, is_return: group_hop(
+        v, ahead, is_other, experts, places, stride, is_return
+    )
+    outgoing = outgoing.reshape(count, 2, slot_count, model_width)
+    near = jnp.stack([outgoing[0]] + [hop(outgoing[i], i, 0, False) for i in range(1, count)])
+    half = count * slot_count
+    far_rows = hop(near[:, 1].reshape(half, model_width), 0, 1, False)
+    own = jnp.concatenate([far_rows, near[:, 0].reshape(half, model_width)], axis=0)
+    across = lambda i: (ring - 1 - i // stride) * stride + i % stride
+    beside = lambda i: i ^ 1
+    pair_rows = jnp.stack([own, place_hop(own, places, across)])
+    all_rows = jnp.stack([pair_rows, place_hop(pair_rows, places, beside)])
+    all_rows = all_rows.reshape(4, 2, half, model_width).swapaxes(0, 1).reshape(-1, model_width)
+    partial = expert(all_rows, weights).reshape(2, 2, 2, half, model_width)
+
+    def fold(part):
+        mine = part[0] + place_hop(part[1].astype(jnp.bfloat16), places, beside).astype(jnp.float32)
+        other = place_hop(mine[1].astype(jnp.bfloat16), places, across).astype(jnp.float32)
+        return (mine[0] + other).astype(jnp.bfloat16)
+
+    far_back = hop(fold(partial[0]), 0, 1, True).reshape(count, slot_count, model_width)
+    near_back = fold(partial[1]).reshape(count, slot_count, model_width)
+    back = jnp.stack([near_back, far_back], axis=1)
+    returned = jnp.stack([back[0]] + [hop(back[i], i, 0, True) for i in range(1, count)])
     expert_out = lax.dot_general(
         route_table,
-        returned,
+        returned.reshape(-1, model_width),
         (((0,), (0,)), ((), ())),
         preferred_element_type=jnp.float32,
     )

time: 320 us -> 233 us (0.73)
  starting transfers between devices: 128 us -> 75.8 us
  waiting for transfers between devices: 131 us -> 95.1 us
  matrix products: 19.6 us -> 6.38 us
  Pallas kernels: 0 us -> 12.2 us
  other arithmetic: 6.7 us -> 18.1 us
  local copies, waits for them, and re-layouts: 18.4 us -> 8.55 us
    all_gather x2 -> x1, waiting for transfers between devices: 98.4 us -> 19.9 us  [body(): weights = lax.all_gather(shard, 'tm', axis_index_groups=loops)]
    ppermute x12 -> x6, starting transfers between devices: 45 us -> 15.9 us  [place_hop(): return lax.ppermute(array, 'tm', [(i, to(i)) for i in range(places)])]
    ppermute x14 -> x8, waiting for transfers between devices: 10.2 us -> 37.8 us  [group_hop(): return lax.ppermute(array, ('grp', 'tm'), pairs)]
    ppermute x14 -> x8, starting transfers between devices: 55 us -> 32.2 us  [group_hop(): return lax.ppermute(array, ('grp', 'tm'), pairs)]
    dot_general x4 -> x1, matrix products: 14.3 us -> 1.07 us  [body(): lax.dot_general(route_table, returned.reshape(-1, model_width), (((0,), (...]
    pallas_call x0 -> x1, Pallas kernels: none -> 12.2 us  [expert(): pl.pallas_call(expert_kernel, grid=(shards // step,), in_specs=[pl.BlockS...]
    ppermute x12 -> x6, waiting for transfers between devices: 10.4 us -> 22.6 us  [place_hop(): return lax.ppermute(array, 'tm', [(i, to(i)) for i in range(places)])]
    concatenate x3 -> x1, local copies, waits for them, and re-layouts: 9.55 us -> 0.02 us  [body(): jnp.concatenate([far_rows, near[:, 0].reshape(half, model_width)], axis=0)]
  transfers between devices with their start and end apart: 32 -> 19, of which waited for: 11 -> 13; matrix products, arithmetic and copies ran while one was open for 12% -> 12% of each run, Pallas kernels for 0% -> 0%
where the time goes in v3:
time: 233 us; the launch traced here: 231 us
  waiting for transfers between devices  95.1 us (41%)
  starting transfers between devices  75.8 us (33%)
  other arithmetic  18.1 us (8%)
  between operations  14.9 us (6%)
  Pallas kernels  12.2 us (5%)
  local copies, waits for them, and re-layouts  8.55 us (4%)
  matrix products  6.38 us (3%)
    ppermute x8, waiting for transfers between devices, group_hop(): return lax.ppermute(array, ('grp', 'tm'), pairs)  37.8 us
    ppermute x8, starting transfers between devices, group_hop(): return lax.ppermute(array, ('grp', 'tm'), pairs)  32.2 us
    ppermute x2, starting transfers between devices, with_halo(): lax.ppermute(head, axis, [((i + 1) % count, i) for i in range(ends)])  23.9 us
    ppermute x6, waiting for transfers between devices, place_hop(): return lax.ppermute(array, 'tm', [(i, to(i)) for i in range(places)])  22.6 us
    all_gather x1, waiting for transfers between devices, body(): weights = lax.all_gather(shard, 'tm', axis_index_groups=loops)  19.9 us
    ppermute x6, starting transfers between devices, place_hop(): return lax.ppermute(array, 'tm', [(i, to(i)) for i in range(places)])  15.9 us
    ppermute x2, waiting for transfers between devices, with_halo(): lax.ppermute(tail, axis, [(i, (i + 1) % count) for i in range(ends)])  12.4 us
    pallas_call x1, Pallas kernels, expert(): pl.pallas_call(expert_kernel, grid=(shards // step,), in_specs=[pl.BlockS...  12.2 us
  transfers between devices with their start and end apart: 19, of which 13 were waited for; matrix products, arithmetic and copies ran while one was open for 12% of the time, Pallas kernels for 0%

profile of v3, /device:TPU:24, one launch (start us, length us, event | category | flops | bytes accessed | tf_op | source)
XLA Modules:
  0.0 231.1 jit_solution(4337089531292431658)
XLA Ops:
  10.1 12.8 %collective-permute-start.1 = (bf16[128,2,1536]{0,2,1:T(8,128)(2,1)S(1)}, bf16[128,2,1536]{0,2,1:T(8,128)(2,1)S(1)}, u32[]{:S(2)}, u32[]{:S(2)}) collective-permute-start(bf16[128,2,1536]{0,2,1:T(8,128)(2,1)S(1)} %pad_maximum_fusion.3), channel_id=1, source_target_pairs={{1,0},{2,1},{3,2},{4,3},{5,4},{6,5},{7,6},{8,7},{9,8},{10,9},{11,1... | collective-permute-start | bytes 2359304 | tf_op jit(solution)/shard_map/ppermute | solution.py:24
  31.1 2.4 %slice_reduce_fusion.30 = (f32[1536]{0:T(1024)S(1)}, f32[1536]{0:T(1024)S(1)}, f32[1536]{0:T(1024)}, f32[1536]{0:T(1024)}, f32[1536]{0:T(1024)}, /*index=5*/f32[...) fusion(f32[31,1536]{1,0:T(8,128)} %param.13), kind=kLoop, calls=%fused_computation.186 | loop fusion | bytes 233472 | tf_op jit(solution)/shard_map/slice | solution.py:164
  39.9 12.4 %collective-permute-done = bf16[128,2,1536]{0,2,1:T(8,128)(2,1)S(1)} collective-permute-done((bf16[128,2,1536]{0,2,1:T(8,128)(2,1)S(1)}, bf16[128,2,1536]{0,2,1:T(8,128)(2,1)S(1)}, u32[]{:S(2)}, u32[]{:S(2)}) %collective-permute-start) | collective-permute-done | bytes 786464 | tf_op jit(solution)/shard_map/ppermute | solution.py:22
  53.6 2.7 %fusion.89 = (f32[12,128]{1,0:T(8,128)S(1)}, f32[12,128,384]{1,2,0:T(8,128)}) fusion(pred[128,384]{0,1:T(8,128)(4,1)S(1)} %copy-done.4, bf16[384,12,128]{0,2,1:T(8,128)(2,1)S(1)} %bitcast.105, bf16[128,12,128]{0,2,1:T(8,128)(2,1)S(1)} %bitcast.112), kind=kOutput, calls=%fused_computation.218 | convolution fusion | flops 305529216 | bytes 3987456 | tf_op jit(solution)/shard_map/sub | solution.py:116
  56.3 2.2 fusion.9
  61.8 11.1 %collective-permute-start.3 = (bf16[15,1536]{1,0:T(8,128)(2,1)S(1)}, bf16[15,1536]{1,0:T(8,128)(2,1)S(1)}, u32[]{:S(2)}, u32[]{:S(2)}) collective-permute-start(bf16[15,1536]{1,0:T(8,128)(2,1)S(1)} %get-tuple-element.61), channel_id=1, source_target_pairs={{1,0},{2,1},{3,2},{4,3},{5,4},{6,5},{7,6},{8,7},{9,8},{10,9},{11,1... | collective-permute-start | bytes 138248 | tf_op jit(solution)/shard_map/ppermute | solution.py:24
  75.1 4.3 %convert_reduce_fusion = (f32[128]{0:T(128)S(1)}, bf16[128,1536]{1,0:T(8,128)(2,1)S(1)}) fusion(bf16[15,1536]{1,0:T(8,128)(2,1)S(1)} %collective-permute-done.3, bf16[128,1536]{1,0:T(8,128)(2,1)S(1)} %fusion.21, f32[1536]{0:T(1024)S(1)} %get-tuple-element.34, f32[1536]{0:T(1024)S(1)} %get-tuple-element.35, f32[1536]{0:T(1024)S(1)} %get-tuple-element.6, ...), kind=kLoop, calls=%fused_computation.47 | loop fusion | flops 37552000 | bytes 1462784 | tf_op jit(solution)/shard_map/reduce_sum | solution.py:32
  80.3 3.5 %collective-permute-start.4 = (bf16[2,20,1536]{2,1,0:T(8,128)(2,1)S(1)}, bf16[2,20,1536]{2,1,0:T(8,128)(2,1)S(1)}, u32[]{:S(2)}, u32[]{:S(2)}) collective-permute-start(bf16[2,20,1536]{2,1,0:T(8,128)(2,1)S(1)} %squeeze.48), channel_id=1, source_target_pairs={{0,64},{1,65},{2,66},{3,67},{4,68},{5,69},{6,70},{7,71},{8,72},{9,... | collective-permute-start | bytes 368648 | tf_op jit(solution)/shard_map/ppermute | solution.py:57
  83.8 4.7 %collective-permute-start.5 = (bf16[2,20,1536]{2,1,0:T(8,128)(2,1)S(1)}, bf16[2,20,1536]{2,1,0:T(8,128)(2,1)S(1)}, u32[]{:S(2)}, u32[]{:S(2)}) collective-permute-start(bf16[2,20,1536]{2,1,0:T(8,128)(2,1)S(1)} %squeeze.49), channel_id=1, source_target_pairs={{0,128},{1,129},{2,130},{3,131},{4,132},{5,133},{6,134},{7,135},{8... | collective-permute-start | bytes 368648 | tf_op jit(solution)/shard_map/ppermute | solution.py:57
  88.5 3.3 %collective-permute-start.6 = (bf16[2,20,1536]{2,1,0:T(8,128)(2,1)S(1)}, bf16[2,20,1536]{2,1,0:T(8,128)(2,1)S(1)}, u32[]{:S(2)}, u32[]{:S(2)}) collective-permute-start(bf16[2,20,1536]{2,1,0:T(8,128)(2,1)S(1)} %squeeze.50), channel_id=1, source_target_pairs={{0,192},{1,193},{2,194},{3,195},{4,196},{5,197},{6,198},{7,199},{8... | collective-permute-start | bytes 368648 | tf_op jit(solution)/shard_map/ppermute | solution.py:57
  92.3 3.2 %collective-permute-done.6 = bf16[2,20,1536]{2,1,0:T(8,128)(2,1)S(1)} collective-permute-done((bf16[2,20,1536]{2,1,0:T(8,128)(2,1)S(1)}, bf16[2,20,1536]{2,1,0:T(8,128)(2,1)S(1)}, u32[]{:S(2)}, u32[]{:S(2)}) %collective-permute-start.6) | collective-permute-done | bytes 122912 | tf_op jit(solution)/shard_map/ppermute | solution.py:57
  97.8 11.0 %collective-permute-done.7 = bf16[80,1536]{1,0:T(8,128)(2,1)S(1)} collective-permute-done((bf16[80,1536]{1,0:T(8,128)(2,1)S(1)}, bf16[80,1536]{1,0:T(8,128)(2,1)S(1)}, u32[]{:S(2)}, u32[]{:S(2)}) %collective-permute-start.7) | collective-permute-done | bytes 245792 | tf_op jit(solution)/shard_map/ppermute | solution.py:57
  110.7 14.4 %collective-permute-done.8 = bf16[160,1536]{1,0:T(8,128)(2,1)S(1)} collective-permute-done((bf16[160,1536]{1,0:T(8,128)(2,1)S(1)}, bf16[160,1536]{1,0:T(8,128)(2,1)S(1)}, u32[]{:S(2)}, u32[]{:S(2)}) %collective-permute-start.8) | collective-permute-done | bytes 491552 | tf_op jit(solution)/shard_map/ppermute | solution.py:43
  125.3 2.6 %collective-permute-start.9 = (bf16[2,160,1536]{2,1,0:T(8,128)(2,1)S(1)}, bf16[2,160,1536]{2,1,0:T(8,128)(2,1)S(1)}, u32[]{:S(2)}, u32[]{:S(2)}) collective-permute-start(bf16[2,160,1536]{2,1,0:T(8,128)(2,1)S(1)} %get-tuple-element.49), channel_id=1, source_target_pairs={{0,1},{1,0},{2,3},{3,2},{4,5},{5,4},{6,7},{7,6},{8,9},{9,8},{10,11... | collective-permute-start | bytes 2949128 | tf_op jit(solution)/shard_map/ppermute | solution.py:43
  130.4 19.9 %all-gather.3.cloned.1.call-done = bf16[3072,1536]{1,0:T(8,128)(2,1)} async-done(((bf16[192,1536]{1,0:T(8,128)(2,1)}), bf16[3072,1536]{1,0:T(8,128)(2,1)}) %all-gather.3.cloned.1.call-update) | async-done | bytes 9437200 | tf_op jit(solution)/shard_map/all_gather | solution.py:150
  150.3 12.2 %shard_map.91 = f32[640,1536]{1,0:T(8,128)S(1)} custom-call(bf16[640,1536]{1,0:T(8,128)(2,1)S(1)} %bitcast.96, bf16[16,192,1536]{2,1,0:T(8,128)(2,1)} %bitcast.123), custom_call_target="tpu_custom_call" | custom-call | flops 6039797760 | bytes 15335424 | tf_op jit(solution)/shard_map/pallas_call | solution.py:83
  164.7 2.4 %collective-permute-start.12 = (bf16[2,80,1536]{2,1,0:T(8,128)(2,1)S(1)}, bf16[2,80,1536]{2,1,0:T(8,128)(2,1)S(1)}, u32[]{:S(2)}, u32[]{:S(2)}) collective-permute-start(bf16[2,80,1536]{2,1,0:T(8,128)(2,1)S(1)} %bitcast.111), channel_id=1, source_target_pairs={{0,1},{1,0},{2,3},{3,2},{4,5},{5,4},{6,7},{7,6},{8,9},{9,8},{10,11... | collective-permute-start | bytes 1474568 | tf_op jit(solution)/shard_map/ppermute | solution.py:43
  168.8 5.0 %collective-permute-start.13 = (bf16[80,1536]{1,0:T(8,128)(2,1)S(1)}, bf16[80,1536]{1,0:T(8,128)(2,1)S(1)}, u32[]{:S(2)}, u32[]{:S(2)}) collective-permute-start(bf16[80,1536]{1,0:T(8,128)(2,1)S(1)} %fusion.60), channel_id=1, source_target_pairs={{0,48},{1,49},{2,50},{3,51},{4,52},{5,53},{6,54},{7,55},{8,56},{9,... | collective-permute-start | bytes 737288 | tf_op jit(solution)/shard_map/ppermute | solution.py:43
  176.0 4.6 %collective-permute-done.13 = bf16[80,1536]{1,0:T(8,128)(2,1)S(1)} collective-permute-done((bf16[80,1536]{1,0:T(8,128)(2,1)S(1)}, bf16[80,1536]{1,0:T(8,128)(2,1)S(1)}, u32[]{:S(2)}, u32[]{:S(2)}) %collective-permute-start.13) | collective-permute-done | bytes 245792 | tf_op jit(solution)/shard_map/ppermute | solution.py:43
  180.7 7.9 %collective-permute-start.14 = (bf16[80,1536]{1,0:T(8,128)(2,1)S(1)}, bf16[80,1536]{1,0:T(8,128)(2,1)S(1)}, u32[]{:S(2)}, u32[]{:S(2)}) collective-permute-start(bf16[80,1536]{1,0:T(8,128)(2,1)S(1)} %fusion.25), channel_id=1, source_target_pairs={{270,0},{271,1},{268,2},{269,3},{266,4},{267,5},{264,6},{265,7},{2... | collective-permute-start | bytes 737288 | tf_op jit(solution)/shard_map/ppermute | solution.py:57
  188.8 17.4 %collective-permute-done.14 = bf16[80,1536]{1,0:T(8,128)(2,1)S(1)} collective-permute-done((bf16[80,1536]{1,0:T(8,128)(2,1)S(1)}, bf16[80,1536]{1,0:T(8,128)(2,1)S(1)}, u32[]{:S(2)}, u32[]{:S(2)}) %collective-permute-start.14) | collective-permute-done | bytes 245792 | tf_op jit(solution)/shard_map/ppermute | solution.py:57
  206.3 4.9 %collective-permute-start.15 = (bf16[2,20,1536]{2,1,0:T(8,128)(2,1)S(1)}, bf16[2,20,1536]{2,1,0:T(8,128)(2,1)S(1)}, u32[]{:S(2)}, u32[]{:S(2)}) collective-permute-start(bf16[2,20,1536]{2,1,0:T(8,128)(2,1)S(1)} %get-tuple-element.51), channel_id=1, source_target_pairs={{64,0},{65,1},{66,2},{67,3},{68,4},{69,5},{70,6},{71,7},{72,8},{73... | collective-permute-start | bytes 368648 | tf_op jit(solution)/shard_map/ppermute | solution.py:57
  213.1 4.0 %collective-permute-start.16 = (bf16[2,20,1536]{2,1,0:T(8,128)(2,1)S(1)}, bf16[2,20,1536]{2,1,0:T(8,128)(2,1)S(1)}, u32[]{:S(2)}, u32[]{:S(2)}) collective-permute-start(bf16[2,20,1536]{2,1,0:T(8,128)(2,1)S(1)} %get-tuple-element.53), channel_id=1, source_target_pairs={{128,0},{129,1},{130,2},{131,3},{132,4},{133,5},{134,6},{135,7},{1... | collective-permute-start | bytes 368648 | tf_op jit(solution)/shard_map/ppermute | solution.py:57
  217.1 5.8 %collective-permute-done.17 = bf16[2,20,1536]{2,1,0:T(8,128)(2,1)S(1)} collective-permute-done((bf16[2,20,1536]{2,1,0:T(8,128)(2,1)S(1)}, bf16[2,20,1536]{2,1,0:T(8,128)(2,1)S(1)}, u32[]{:S(2)}, u32[]{:S(2)}) %collective-permute-start.17) | collective-permute-done | bytes 122912 | tf_op jit(solution)/shard_map/ppermute | solution.py:57
  (134 shorter events, 41.4 us)
Async XLA Ops:
  6.5 143.8 %all-gather.3.cloned.1.call-start = ((), (), s32[]{:S(2)}) async-start(), calls=%async_computation | async-start | bytes 10027008 | tf_op jit(solution)/shard_map/all_gather | solution.py:150
  6.5 19.5 %copy-start.23 = (s32[1,128]{1,0:T(1,128)S(1)}, s32[1,128]{1,0:T(1,128)}, u32[]{:S(2)}) copy-start(s32[1,128]{1,0:T(1,128)} %param.15) | copy-start | bytes 1540
  8.5 24.9 %copy-start.1 = (bf16[1,128,1536]{2,1,0:T(8,128)(2,1)S(1)}, bf16[1,128,1536]{2,1,0:T(8,128)(2,1)}, u32[]{:S(2)}) copy-start(bf16[1,128,1536]{2,1,0:T(8,128)(2,1)} %param.10) | copy-start | bytes 1179652
  10.1 29.8 %collective-permute-start.1 = (bf16[128,2,1536]{0,2,1:T(8,128)(2,1)S(1)}, bf16[128,2,1536]{0,2,1:T(8,128)(2,1)S(1)}, u32[]{:S(2)}, u32[]{:S(2)}) collective-permute-start(bf16[128,2,1536]{0,2,1:T(8,128)(2,1)S(1)} %pad_maximum_fusion.3), channel_id=1, source_target_pairs={{1,0},{2,1},{3,2},{4,3},{5,4},{6,5},{7,6},{8,7},{9,8},{10,9},{11,1... | collective-permute-start | bytes 2359304 | tf_op jit(solution)/shard_map/ppermute | solution.py:24
  22.9 29.4 %collective-permute-start = (bf16[128,2,1536]{0,2,1:T(8,128)(2,1)S(1)}, bf16[128,2,1536]{0,2,1:T(8,128)(2,1)S(1)}, u32[]{:S(2)}, u32[]{:S(2)}) collective-permute-start(bf16[128,2,1536]{0,2,1:T(8,128)(2,1)S(1)} %pad_maximum_fusion.3), channel_id=1, source_target_pairs={{0,1},{1,2},{2,3},{3,4},{4,5},{5,6},{6,7},{7,8},{8,9},{9,10},{10,1... | collective-permute-start | bytes 2359304 | tf_op jit(solution)/shard_map/ppermute | solution.py:22
  58.6 16.4 %copy-start.5 = (f32[1536]{0:T(1024)S(1)}, f32[1536]{0:T(1024)}, u32[]{:S(2)}) copy-start(f32[1536]{0:T(1024)} %get-tuple-element.7) | copy-start | bytes 18436
  59.0 20.7 %copy-start.22 = (s32[128]{0:T(128)S(1)}, s32[128]{0:T(128)}, u32[]{:S(2)}) copy-start(s32[128]{0:T(128)} %fusion.76) | copy-start | bytes 1540
  59.0 20.7 %copy-start.26 = (pred[128]{0:T(512)(128)(4,1)S(1)}, pred[128]{0:T(512)(128)(4,1)}, u32[]{:S(2)}) copy-start(pred[128]{0:T(512)(128)(4,1)} %compare_and_fusion) | copy-start | bytes 388
  59.9 14.5 %collective-permute-start.2 = (bf16[15,1536]{1,0:T(8,128)(2,1)S(1)}, bf16[15,1536]{1,0:T(8,128)(2,1)S(1)}, u32[]{:S(2)}, u32[]{:S(2)}) collective-permute-start(bf16[15,1536]{1,0:T(8,128)(2,1)S(1)} %get-tuple-element.60), channel_id=1, source_target_pairs={{0,1},{1,2},{2,3},{3,4},{4,5},{5,6},{6,7},{7,8},{8,9},{9,10},{10,1... | collective-permute-start | bytes 138248 | tf_op jit(solution)/shard_map/ppermute | solution.py:22
  61.8 13.2 %collective-permute-start.3 = (bf16[15,1536]{1,0:T(8,128)(2,1)S(1)}, bf16[15,1536]{1,0:T(8,128)(2,1)S(1)}, u32[]{:S(2)}, u32[]{:S(2)}) collective-permute-start(bf16[15,1536]{1,0:T(8,128)(2,1)S(1)} %get-tuple-element.61), channel_id=1, source_target_pairs={{1,0},{2,1},{3,2},{4,3},{5,4},{6,5},{7,6},{8,7},{9,8},{10,9},{11,1... | collective-permute-start | bytes 138248 | tf_op jit(solution)/shard_map/ppermute | solution.py:24
  80.3 11.6 %collective-permute-start.4 = (bf16[2,20,1536]{2,1,0:T(8,128)(2,1)S(1)}, bf16[2,20,1536]{2,1,0:T(8,128)(2,1)S(1)}, u32[]{:S(2)}, u32[]{:S(2)}) collective-permute-start(bf16[2,20,1536]{2,1,0:T(8,128)(2,1)S(1)} %squeeze.48), channel_id=1, source_target_pairs={{0,64},{1,65},{2,66},{3,67},{4,68},{5,69},{6,70},{7,71},{8,72},{9,... | collective-permute-start | bytes 368648 | tf_op jit(solution)/shard_map/ppermute | solution.py:57
  83.8 8.5 %collective-permute-start.5 = (bf16[2,20,1536]{2,1,0:T(8,128)(2,1)S(1)}, bf16[2,20,1536]{2,1,0:T(8,128)(2,1)S(1)}, u32[]{:S(2)}, u32[]{:S(2)}) collective-permute-start(bf16[2,20,1536]{2,1,0:T(8,128)(2,1)S(1)} %squeeze.49), channel_id=1, source_target_pairs={{0,128},{1,129},{2,130},{3,131},{4,132},{5,133},{6,134},{7,135},{8... | collective-permute-start | bytes 368648 | tf_op jit(solution)/shard_map/ppermute | solution.py:57
  88.5 7.0 %collective-permute-start.6 = (bf16[2,20,1536]{2,1,0:T(8,128)(2,1)S(1)}, bf16[2,20,1536]{2,1,0:T(8,128)(2,1)S(1)}, u32[]{:S(2)}, u32[]{:S(2)}) collective-permute-start(bf16[2,20,1536]{2,1,0:T(8,128)(2,1)S(1)} %squeeze.50), channel_id=1, source_target_pairs={{0,192},{1,193},{2,194},{3,195},{4,196},{5,197},{6,198},{7,199},{8... | collective-permute-start | bytes 368648 | tf_op jit(solution)/shard_map/ppermute | solution.py:57
  95.8 13.0 %collective-permute-start.7 = (bf16[80,1536]{1,0:T(8,128)(2,1)S(1)}, bf16[80,1536]{1,0:T(8,128)(2,1)S(1)}, u32[]{:S(2)}, u32[]{:S(2)}) collective-permute-start(bf16[80,1536]{1,0:T(8,128)(2,1)S(1)} %reshape_squeeze.18), channel_id=1, source_target_pairs={{0,270},{1,271},{2,268},{3,269},{4,266},{5,267},{6,264},{7,265},{8... | collective-permute-start | bytes 737288 | tf_op jit(solution)/shard_map/ppermute | solution.py:57
  108.8 16.4 %collective-permute-start.8 = (bf16[160,1536]{1,0:T(8,128)(2,1)S(1)}, bf16[160,1536]{1,0:T(8,128)(2,1)S(1)}, u32[]{:S(2)}, u32[]{:S(2)}) collective-permute-start(bf16[160,1536]{1,0:T(8,128)(2,1)S(1)} %constant_dynamic-update-slice_fusion), channel_id=1, source_target_pairs={{0,48},{1,49},{2,50},{3,51},{4,52},{5,53},{6,54},{7,55},{8,56},{9,... | collective-permute-start | bytes 1474568 | tf_op jit(solution)/shard_map/ppermute | solution.py:43
  125.3 4.7 %collective-permute-start.9 = (bf16[2,160,1536]{2,1,0:T(8,128)(2,1)S(1)}, bf16[2,160,1536]{2,1,0:T(8,128)(2,1)S(1)}, u32[]{:S(2)}, u32[]{:S(2)}) collective-permute-start(bf16[2,160,1536]{2,1,0:T(8,128)(2,1)S(1)} %get-tuple-element.49), channel_id=1, source_target_pairs={{0,1},{1,0},{2,3},{3,2},{4,5},{5,4},{6,7},{7,6},{8,9},{9,8},{10,11... | collective-permute-start | bytes 2949128 | tf_op jit(solution)/shard_map/ppermute | solution.py:43
  162.8 11.0 %collective-permute-start.10 = (bf16[2,80,1536]{2,1,0:T(8,128)(2,1)S(1)}, bf16[2,80,1536]{2,1,0:T(8,128)(2,1)S(1)}, u32[]{:S(2)}, u32[]{:S(2)}) collective-permute-start(bf16[2,80,1536]{2,1,0:T(8,128)(2,1)S(1)} %bitcast.110), channel_id=1, source_target_pairs={{0,1},{1,0},{2,3},{3,2},{4,5},{5,4},{6,7},{7,6},{8,9},{9,8},{10,11... | collective-permute-start | bytes 1474568 | tf_op jit(solution)/shard_map/ppermute | solution.py:43
  164.7 3.9 %collective-permute-start.12 = (bf16[2,80,1536]{2,1,0:T(8,128)(2,1)S(1)}, bf16[2,80,1536]{2,1,0:T(8,128)(2,1)S(1)}, u32[]{:S(2)}, u32[]{:S(2)}) collective-permute-start(bf16[2,80,1536]{2,1,0:T(8,128)(2,1)S(1)} %bitcast.111), channel_id=1, source_target_pairs={{0,1},{1,0},{2,3},{3,2},{4,5},{5,4},{6,7},{7,6},{8,9},{9,8},{10,11... | collective-permute-start | bytes 1474568 | tf_op jit(solution)/shard_map/ppermute | solution.py:43
  168.8 11.9 %collective-permute-start.13 = (bf16[80,1536]{1,0:T(8,128)(2,1)S(1)}, bf16[80,1536]{1,0:T(8,128)(2,1)S(1)}, u32[]{:S(2)}, u32[]{:S(2)}) collective-permute-start(bf16[80,1536]{1,0:T(8,128)(2,1)S(1)} %fusion.60), channel_id=1, source_target_pairs={{0,48},{1,49},{2,50},{3,51},{4,52},{5,53},{6,54},{7,55},{8,56},{9,... | collective-permute-start | bytes 737288 | tf_op jit(solution)/shard_map/ppermute | solution.py:43
  173.9 14.7 %collective-permute-start.11 = (bf16[80,1536]{1,0:T(8,128)(2,1)S(1)}, bf16[80,1536]{1,0:T(8,128)(2,1)S(1)}, u32[]{:S(2)}, u32[]{:S(2)}) collective-permute-start(bf16[80,1536]{1,0:T(8,128)(2,1)S(1)} %fusion.59), channel_id=1, source_target_pairs={{0,48},{1,49},{2,50},{3,51},{4,52},{5,53},{6,54},{7,55},{8,56},{9,... | collective-permute-start | bytes 737288 | tf_op jit(solution)/shard_map/ppermute | solution.py:43
  180.7 25.5 %collective-permute-start.14 = (bf16[80,1536]{1,0:T(8,128)(2,1)S(1)}, bf16[80,1536]{1,0:T(8,128)(2,1)S(1)}, u32[]{:S(2)}, u32[]{:S(2)}) collective-permute-start(bf16[80,1536]{1,0:T(8,128)(2,1)S(1)} %fusion.25), channel_id=1, source_target_pairs={{270,0},{271,1},{268,2},{269,3},{266,4},{267,5},{264,6},{265,7},{2... | collective-permute-start | bytes 737288 | tf_op jit(solution)/shard_map/ppermute | solution.py:57
  206.3 10.9 %collective-permute-start.15 = (bf16[2,20,1536]{2,1,0:T(8,128)(2,1)S(1)}, bf16[2,20,1536]{2,1,0:T(8,128)(2,1)S(1)}, u32[]{:S(2)}, u32[]{:S(2)}) collective-permute-start(bf16[2,20,1536]{2,1,0:T(8,128)(2,1)S(1)} %get-tuple-element.51), channel_id=1, source_target_pairs={{64,0},{65,1},{66,2},{67,3},{68,4},{69,5},{70,6},{71,7},{72,8},{73... | collective-permute-start | bytes 368648 | tf_op jit(solution)/shard_map/ppermute | solution.py:57
  211.2 11.8 %collective-permute-start.17 = (bf16[2,20,1536]{2,1,0:T(8,128)(2,1)S(1)}, bf16[2,20,1536]{2,1,0:T(8,128)(2,1)S(1)}, u32[]{:S(2)}, u32[]{:S(2)}) collective-permute-start(bf16[2,20,1536]{2,1,0:T(8,128)(2,1)S(1)} %get-tuple-element.52), channel_id=1, source_target_pairs={{192,0},{193,1},{194,2},{195,3},{196,4},{197,5},{198,6},{199,7},{2... | collective-permute-start | bytes 368648 | tf_op jit(solution)/shard_map/ppermute | solution.py:57
  213.1 9.8 %collective-permute-start.16 = (bf16[2,20,1536]{2,1,0:T(8,128)(2,1)S(1)}, bf16[2,20,1536]{2,1,0:T(8,128)(2,1)S(1)}, u32[]{:S(2)}, u32[]{:S(2)}) collective-permute-start(bf16[2,20,1536]{2,1,0:T(8,128)(2,1)S(1)} %get-tuple-element.53), channel_id=1, source_target_pairs={{128,0},{129,1},{130,2},{131,3},{132,4},{133,5},{134,6},{135,7},{1... | collective-permute-start | bytes 368648 | tf_op jit(solution)/shard_map/ppermute | solution.py:57
  (22 other events, 274.5 us)
Sparse Core Ops, SparseCore 0:
  9.4 140.8 all-gather.2

commit v4 on v3

--- a/solution.py
+++ b/solution.py
@@ -77,7 +77,7 @@
         out_ref[...] += part
 
 
-def expert(rows, weights, step=4):
+def expert(rows, weights, step=8):
     count, width = rows.shape
     shards, twice, _ = weights.shape
     return pl.pallas_call(
@@ -94,7 +94,7 @@
             bytes_accessed=2 * weights.size + 6 * rows.size,
             transcendentals=count * shards * twice // 2,
         ),
-        compiler_params=pltpu.CompilerParams(vmem_limit_bytes=40 * 2**20),
+        compiler_params=pltpu.CompilerParams(vmem_limit_bytes=51 * 2**20),
     )(rows, weights)
 
 
@@ -194,18 +194,20 @@
     beside = lambda i: i ^ 1
     pair_rows = jnp.stack([own, place_hop(own, places, across)])
     all_rows = jnp.stack([pair_rows, place_hop(pair_rows, places, beside)])
-    all_rows = all_rows.reshape(4, 2, half, model_width).swapaxes(0, 1).reshape(-1, model_width)
-    partial = expert(all_rows, weights).reshape(2, 2, 2, half, model_width)
-
-    def fold(part):
-        mine = part[0] + place_hop(part[1].astype(jnp.bfloat16), places, beside).astype(jnp.float32)
+    all_rows = all_rows.reshape(4, 2, half, model_width)
+
+    def finish(part):
+        partial = expert(all_rows[:, part].reshape(-1, model_width), weights)
+        partial = partial.reshape(2, 2, half, model_width)
+        mine = partial[0] + place_hop(partial[1].astype(jnp.bfloat16), places, beside).astype(jnp.float32)
         other = place_hop(mine[1].astype(jnp.bfloat16), places, across).astype(jnp.float32)
-        return (mine[0] + other).astype(jnp.bfloat16)
-
-    far_back = hop(fold(partial[0]), 0, 1, True).reshape(count, slot_count, model_width)
-    near_back = fold(partial[1]).reshape(count, slot_count, model_width)
-    back = jnp.stack([near_back, far_back], axis=1)
-    returned = jnp.stack([back[0]] + [hop(back[i], i, 0, True) for i in range(1, count)])
+        return (mine[0] + other).astype(jnp.bfloat16).reshape(count, slot_count, model_width)
+
+    far_total = finish(0)
+    far_back = [hop(far_total[i], i, 1, True) for i in range(count)]
+    near_total = finish(1)
+    near_back = [near_total[0]] + [hop(near_total[i], i, 0, True) for i in range(1, count)]
+    returned = jnp.stack([jnp.stack(pair) for pair in zip(near_back, far_back)])
     expert_out = lax.dot_general(
         route_table,
         returned.reshape(-1, model_width),

time: 233 us -> 238 us (1.021)
  the two profiles are of different devices: /device:TPU:24 before, /device:TPU:112 now
where the time goes in v4:
time: 238 us; the launch traced here: 237 us
  starting transfers between devices  94.9 us (40%)
  waiting for transfers between devices  80.8 us (34%)
  other arithmetic  16.3 us (7%)
  between operations  14.9 us (6%)
  Pallas kernels  13.9 us (6%)
  local copies, waits for them, and re-layouts  9.55 us (4%)
  matrix products  6.39 us (3%)
    ppermute x11, starting transfers between devices, group_hop(): return lax.ppermute(array, ('grp', 'tm'), pairs)  65.5 us
    ppermute x11, waiting for transfers between devices, group_hop(): return lax.ppermute(array, ('grp', 'tm'), pairs)  27.6 us
    ppermute x6, waiting for transfers between devices, place_hop(): return lax.ppermute(array, 'tm', [(i, to(i)) for i in range(places)])  20.8 us
    all_gather x1, waiting for transfers between devices, body(): weights = lax.all_gather(shard, 'tm', axis_index_groups=loops)  17.7 us
    ppermute x6, starting transfers between devices, place_hop(): return lax.ppermute(array, 'tm', [(i, to(i)) for i in range(places)])  14.6 us
    ppermute x2, waiting for transfers between devices, with_halo(): lax.ppermute(head, axis, [((i + 1) % count, i) for i in range(ends)])  14.6 us
    pallas_call x2, Pallas kernels, expert(): pl.pallas_call(expert_kernel, grid=(shards // step,), in_specs=[pl.BlockS...  13.9 us
    ppermute x2, starting transfers between devices, with_halo(): lax.ppermute(tail, axis, [(i, (i + 1) % count) for i in range(ends)])  9.23 us
  transfers between devices with their start and end apart: 22, of which 11 were waited for; matrix products, arithmetic and copies ran while one was open for 11% of the time, Pallas kernels for 3%

profile of v4, /device:TPU:112, one launch (start us, length us, event | category | flops | bytes accessed | tf_op | source)
XLA Modules:
  0.0 236.8 jit_solution(938304015063290757)
XLA Ops:
  12.0 3.6 %collective-permute-start.1 = (bf16[128,2,1536]{0,2,1:T(8,128)(2,1)S(1)}, bf16[128,2,1536]{0,2,1:T(8,128)(2,1)S(1)}, u32[]{:S(2)}, u32[]{:S(2)}) collective-permute-start(bf16[128,2,1536]{0,2,1:T(8,128)(2,1)S(1)} %pad_maximum_fusion.3), channel_id=1, source_target_pairs={{1,0},{2,1},{3,2},{4,3},{5,4},{6,5},{7,6},{8,7},{9,8},{10,9},{11,1... | collective-permute-start | bytes 2359304 | tf_op jit(solution)/shard_map/ppermute | solution.py:24
  27.4 13.2 %collective-permute-done.1 = bf16[128,2,1536]{0,2,1:T(8,128)(2,1)S(1)} collective-permute-done((bf16[128,2,1536]{0,2,1:T(8,128)(2,1)S(1)}, bf16[128,2,1536]{0,2,1:T(8,128)(2,1)S(1)}, u32[]{:S(2)}, u32[]{:S(2)}) %collective-permute-start.1) | collective-permute-done | bytes 786464 | tf_op jit(solution)/shard_map/ppermute | solution.py:24
  41.9 2.7 %fusion.89 = (f32[12,128]{1,0:T(8,128)S(1)}, f32[12,128,384]{1,2,0:T(8,128)}) fusion(pred[128,384]{0,1:T(8,128)(4,1)S(1)} %fusion.61, bf16[384,12,128]{0,2,1:T(8,128)(2,1)S(1)} %bitcast.109, bf16[128,12,128]{0,2,1:T(8,128)(2,1)S(1)} %bitcast.116), kind=kOutput, calls=%fused_computation.219 | convolution fusion | flops 305529216 | bytes 3987456 | tf_op jit(solution)/shard_map/sub | solution.py:116
  48.2 7.3 %collective-permute-start.2 = (bf16[15,1536]{1,0:T(8,128)(2,1)S(1)}, bf16[15,1536]{1,0:T(8,128)(2,1)S(1)}, u32[]{:S(2)}, u32[]{:S(2)}) collective-permute-start(bf16[15,1536]{1,0:T(8,128)(2,1)S(1)} %get-tuple-element.54), channel_id=1, source_target_pairs={{0,1},{1,2},{2,3},{3,4},{4,5},{5,6},{6,7},{7,8},{8,9},{9,10},{10,1... | collective-permute-start | bytes 138248 | tf_op jit(solution)/shard_map/ppermute | solution.py:22
  60.4 4.3 %convert_reduce_fusion = (f32[128]{0:T(128)S(1)}, bf16[128,1536]{1,0:T(8,128)(2,1)S(1)}) fusion(bf16[15,1536]{1,0:T(8,128)(2,1)S(1)} %collective-permute-done.3, bf16[128,1536]{1,0:T(8,128)(2,1)S(1)} %fusion.21, f32[1536]{0:T(1024)S(1)} %get-tuple-element.34, f32[1536]{0:T(1024)S(1)} %get-tuple-element.35, f32[1536]{0:T(1024)S(1)} %get-tuple-element.6, ...), kind=kLoop, calls=%fused_computation.47 | loop fusion | flops 37552000 | bytes 1462784 | tf_op jit(solution)/shard_map/reduce_sum | solution.py:32
  65.4 3.4 %collective-permute-start.4 = (bf16[2,20,1536]{2,1,0:T(8,128)(2,1)S(1)}, bf16[2,20,1536]{2,1,0:T(8,128)(2,1)S(1)}, u32[]{:S(2)}, u32[]{:S(2)}) collective-permute-start(bf16[2,20,1536]{2,1,0:T(8,128)(2,1)S(1)} %squeeze.21), channel_id=1, source_target_pairs={{0,64},{1,65},{2,66},{3,67},{4,68},{5,69},{6,70},{7,71},{8,72},{9,... | collective-permute-start | bytes 368648 | tf_op jit(solution)/shard_map/ppermute | solution.py:57
  68.9 4.7 %collective-permute-start.5 = (bf16[2,20,1536]{2,1,0:T(8,128)(2,1)S(1)}, bf16[2,20,1536]{2,1,0:T(8,128)(2,1)S(1)}, u32[]{:S(2)}, u32[]{:S(2)}) collective-permute-start(bf16[2,20,1536]{2,1,0:T(8,128)(2,1)S(1)} %squeeze.22), channel_id=1, source_target_pairs={{0,128},{1,129},{2,130},{3,131},{4,132},{5,133},{6,134},{7,135},{8... | collective-permute-start | bytes 368648 | tf_op jit(solution)/shard_map/ppermute | solution.py:57
  73.6 3.3 %collective-permute-start.6 = (bf16[2,20,1536]{2,1,0:T(8,128)(2,1)S(1)}, bf16[2,20,1536]{2,1,0:T(8,128)(2,1)S(1)}, u32[]{:S(2)}, u32[]{:S(2)}) collective-permute-start(bf16[2,20,1536]{2,1,0:T(8,128)(2,1)S(1)} %squeeze.46), channel_id=1, source_target_pairs={{0,192},{1,193},{2,194},{3,195},{4,196},{5,197},{6,198},{7,199},{8... | collective-permute-start | bytes 368648 | tf_op jit(solution)/shard_map/ppermute | solution.py:57
  80.8 9.5 %collective-permute-start.7 = (bf16[80,1536]{1,0:T(8,128)(2,1)S(1)}, bf16[80,1536]{1,0:T(8,128)(2,1)S(1)}, u32[]{:S(2)}, u32[]{:S(2)}) collective-permute-start(bf16[80,1536]{1,0:T(8,128)(2,1)S(1)} %reshape_squeeze.24), channel_id=1, source_target_pairs={{0,270},{1,271},{2,268},{3,269},{4,266},{5,267},{6,264},{7,265},{8... | collective-permute-start | bytes 737288 | tf_op jit(solution)/shard_map/ppermute | solution.py:57
  90.4 12.7 %collective-permute-done.7 = bf16[80,1536]{1,0:T(8,128)(2,1)S(1)} collective-permute-done((bf16[80,1536]{1,0:T(8,128)(2,1)S(1)}, bf16[80,1536]{1,0:T(8,128)(2,1)S(1)}, u32[]{:S(2)}, u32[]{:S(2)}) %collective-permute-start.7) | collective-permute-done | bytes 245792 | tf_op jit(solution)/shard_map/ppermute | solution.py:57
  105.3 13.7 %collective-permute-done.8 = bf16[160,1536]{1,0:T(8,128)(2,1)S(1)} collective-permute-done((bf16[160,1536]{1,0:T(8,128)(2,1)S(1)}, bf16[160,1536]{1,0:T(8,128)(2,1)S(1)}, u32[]{:S(2)}, u32[]{:S(2)}) %collective-permute-start.8) | collective-permute-done | bytes 491552 | tf_op jit(solution)/shard_map/ppermute | solution.py:43
  123.9 17.7 %all-gather.3.cloned.1.call-done = bf16[3072,1536]{1,0:T(8,128)(2,1)} async-done(((bf16[192,1536]{1,0:T(8,128)(2,1)}), bf16[3072,1536]{1,0:T(8,128)(2,1)}) %all-gather.3.cloned.1.call-update) | async-done | bytes 9437200 | tf_op jit(solution)/shard_map/all_gather | solution.py:150
  141.7 6.9 %shard_map.92 = f32[320,1536]{1,0:T(8,128)S(1)} custom-call(bf16[320,1536]{1,0:T(8,128)(2,1)S(1)} %bitcast.99, bf16[16,192,1536]{2,1,0:T(8,128)(2,1)} %bitcast.100), custom_call_target="tpu_custom_call" | custom-call | flops 3019898880 | bytes 12386304 | tf_op jit(solution)/shard_map/pallas_call | solution.py:83
  150.8 7.0 %shard_map.91 = f32[320,1536]{1,0:T(8,128)S(1)} custom-call(bf16[320,1536]{1,0:T(8,128)(2,1)S(1)} %bitcast.98, bf16[16,192,1536]{2,1,0:T(8,128)(2,1)} %bitcast.101), custom_call_target="tpu_custom_call" | custom-call | flops 3019898880 | bytes 12386304 | tf_op jit(solution)/shard_map/pallas_call | solution.py:83
  163.8 3.9 %collective-permute-start.11 = (bf16[80,1536]{1,0:T(8,128)(2,1)S(1)}, bf16[80,1536]{1,0:T(8,128)(2,1)S(1)}, u32[]{:S(2)}, u32[]{:S(2)}) collective-permute-start(bf16[80,1536]{1,0:T(8,128)(2,1)S(1)} %fusion.59), channel_id=1, source_target_pairs={{0,48},{1,49},{2,50},{3,51},{4,52},{5,53},{6,54},{7,55},{8,56},{9,... | collective-permute-start | bytes 737288 | tf_op jit(solution)/shard_map/ppermute | solution.py:43
  167.7 4.7 %collective-permute-done.13 = bf16[80,1536]{1,0:T(8,128)(2,1)S(1)} collective-permute-done((bf16[80,1536]{1,0:T(8,128)(2,1)S(1)}, bf16[80,1536]{1,0:T(8,128)(2,1)S(1)}, u32[]{:S(2)}, u32[]{:S(2)}) %collective-permute-start.13) | collective-permute-done | bytes 245792 | tf_op jit(solution)/shard_map/ppermute | solution.py:43
  172.5 15.8 %collective-permute-start.14 = (bf16[20,1536]{1,0:T(8,128)(2,1)S(1)}, bf16[20,1536]{1,0:T(8,128)(2,1)S(1)}, u32[]{:S(2)}, u32[]{:S(2)}) collective-permute-start(bf16[20,1536]{1,0:T(8,128)(2,1)S(1)} %get-tuple-element.60), channel_id=1, source_target_pairs={{270,0},{271,1},{268,2},{269,3},{266,4},{267,5},{264,6},{265,7},{2... | collective-permute-start | bytes 184328 | tf_op jit(solution)/shard_map/ppermute | solution.py:57
  188.4 4.4 %collective-permute-start.15 = (bf16[20,1536]{1,0:T(8,128)(2,1)S(1)}, bf16[20,1536]{1,0:T(8,128)(2,1)S(1)}, u32[]{:S(2)}, u32[]{:S(2)}) collective-permute-start(bf16[20,1536]{1,0:T(8,128)(2,1)S(1)} %get-tuple-element.59), channel_id=1, source_target_pairs={{64,0},{65,1},{66,2},{67,3},{68,4},{69,5},{70,6},{71,7},{72,8},{73... | collective-permute-start | bytes 184328 | tf_op jit(solution)/shard_map/ppermute | solution.py:57
  192.9 4.3 %collective-permute-start.16 = (bf16[20,1536]{1,0:T(8,128)(2,1)S(1)}, bf16[20,1536]{1,0:T(8,128)(2,1)S(1)}, u32[]{:S(2)}, u32[]{:S(2)}) collective-permute-start(bf16[20,1536]{1,0:T(8,128)(2,1)S(1)} %get-tuple-element.63), channel_id=1, source_target_pairs={{334,0},{335,1},{332,2},{333,3},{330,4},{331,5},{328,6},{329,7},{3... | collective-permute-start | bytes 184328 | tf_op jit(solution)/shard_map/ppermute | solution.py:57
  197.2 2.8 %collective-permute-start.17 = (bf16[20,1536]{1,0:T(8,128)(2,1)S(1)}, bf16[20,1536]{1,0:T(8,128)(2,1)S(1)}, u32[]{:S(2)}, u32[]{:S(2)}) collective-permute-start(bf16[20,1536]{1,0:T(8,128)(2,1)S(1)} %get-tuple-element.58), channel_id=1, source_target_pairs={{128,0},{129,1},{130,2},{131,3},{132,4},{133,5},{134,6},{135,7},{1... | collective-permute-start | bytes 184328 | tf_op jit(solution)/shard_map/ppermute | solution.py:57
  200.0 10.3 %collective-permute-start.18 = (bf16[20,1536]{1,0:T(8,128)(2,1)S(1)}, bf16[20,1536]{1,0:T(8,128)(2,1)S(1)}, u32[]{:S(2)}, u32[]{:S(2)}) collective-permute-start(bf16[20,1536]{1,0:T(8,128)(2,1)S(1)} %get-tuple-element.62), channel_id=1, source_target_pairs={{398,0},{399,1},{396,2},{397,3},{394,4},{395,5},{392,6},{393,7},{3... | collective-permute-start | bytes 184328 | tf_op jit(solution)/shard_map/ppermute | solution.py:57
  210.4 3.2 %collective-permute-start.19 = (bf16[20,1536]{1,0:T(8,128)(2,1)S(1)}, bf16[20,1536]{1,0:T(8,128)(2,1)S(1)}, u32[]{:S(2)}, u32[]{:S(2)}) collective-permute-start(bf16[20,1536]{1,0:T(8,128)(2,1)S(1)} %get-tuple-element.57), channel_id=1, source_target_pairs={{192,0},{193,1},{194,2},{195,3},{196,4},{197,5},{198,6},{199,7},{2... | collective-permute-start | bytes 184328 | tf_op jit(solution)/shard_map/ppermute | solution.py:57
  213.6 3.7 %collective-permute-start.20 = (bf16[20,1536]{1,0:T(8,128)(2,1)S(1)}, bf16[20,1536]{1,0:T(8,128)(2,1)S(1)}, u32[]{:S(2)}, u32[]{:S(2)}) collective-permute-start(bf16[20,1536]{1,0:T(8,128)(2,1)S(1)} %get-tuple-element.61), channel_id=1, source_target_pairs={{462,0},{463,1},{460,2},{461,3},{458,4},{459,5},{456,6},{457,7},{4... | collective-permute-start | bytes 184328 | tf_op jit(solution)/shard_map/ppermute | solution.py:57
  217.8 10.8 %collective-permute-done.20 = bf16[20,1536]{1,0:T(8,128)(2,1)S(1)} collective-permute-done((bf16[20,1536]{1,0:T(8,128)(2,1)S(1)}, bf16[20,1536]{1,0:T(8,128)(2,1)S(1)}, u32[]{:S(2)}, u32[]{:S(2)}) %collective-permute-start.20) | collective-permute-done | bytes 61472 | tf_op jit(solution)/shard_map/ppermute | solution.py:57
  (140 shorter events, 47.8 us)
Async XLA Ops:
  6.5 135.1 %all-gather.3.cloned.1.call-start = ((), (), s32[]{:S(2)}) async-start(), calls=%async_computation | async-start | bytes 10027008 | tf_op jit(solution)/shard_map/all_gather | solution.py:150
  8.5 15.8 %copy-start.2 = (bf16[1,128,1536]{2,1,0:T(8,128)(2,1)S(1)}, bf16[1,128,1536]{2,1,0:T(8,128)(2,1)}, u32[]{:S(2)}) copy-start(bf16[1,128,1536]{2,1,0:T(8,128)(2,1)} %param.10) | copy-start | bytes 1179652
  10.1 17.3 %collective-permute-start = (bf16[128,2,1536]{0,2,1:T(8,128)(2,1)S(1)}, bf16[128,2,1536]{0,2,1:T(8,128)(2,1)S(1)}, u32[]{:S(2)}, u32[]{:S(2)}) collective-permute-start(bf16[128,2,1536]{0,2,1:T(8,128)(2,1)S(1)} %pad_maximum_fusion.3), channel_id=1, source_target_pairs={{0,1},{1,2},{2,3},{3,4},{4,5},{5,6},{6,7},{7,8},{8,9},{9,10},{10,1... | collective-permute-start | bytes 2359304 | tf_op jit(solution)/shard_map/ppermute | solution.py:22
  12.0 28.6 %collective-permute-start.1 = (bf16[128,2,1536]{0,2,1:T(8,128)(2,1)S(1)}, bf16[128,2,1536]{0,2,1:T(8,128)(2,1)S(1)}, u32[]{:S(2)}, u32[]{:S(2)}) collective-permute-start(bf16[128,2,1536]{0,2,1:T(8,128)(2,1)S(1)} %pad_maximum_fusion.3), channel_id=1, source_target_pairs={{1,0},{2,1},{3,2},{4,3},{5,4},{6,5},{7,6},{8,7},{9,8},{10,9},{11,1... | collective-permute-start | bytes 2359304 | tf_op jit(solution)/shard_map/ppermute | solution.py:24
  46.9 13.3 %copy-start.5 = (f32[1536]{0:T(1024)S(1)}, f32[1536]{0:T(1024)}, u32[]{:S(2)}) copy-start(f32[1536]{0:T(1024)} %get-tuple-element.7) | copy-start | bytes 18436
  48.2 10.6 %collective-permute-start.2 = (bf16[15,1536]{1,0:T(8,128)(2,1)S(1)}, bf16[15,1536]{1,0:T(8,128)(2,1)S(1)}, u32[]{:S(2)}, u32[]{:S(2)}) collective-permute-start(bf16[15,1536]{1,0:T(8,128)(2,1)S(1)} %get-tuple-element.54), channel_id=1, source_target_pairs={{0,1},{1,2},{2,3},{3,4},{4,5},{5,6},{6,7},{7,8},{8,9},{9,10},{10,1... | collective-permute-start | bytes 138248 | tf_op jit(solution)/shard_map/ppermute | solution.py:22
  55.5 4.7 %collective-permute-start.3 = (bf16[15,1536]{1,0:T(8,128)(2,1)S(1)}, bf16[15,1536]{1,0:T(8,128)(2,1)S(1)}, u32[]{:S(2)}, u32[]{:S(2)}) collective-permute-start(bf16[15,1536]{1,0:T(8,128)(2,1)S(1)} %get-tuple-element.55), channel_id=1, source_target_pairs={{1,0},{2,1},{3,2},{4,3},{5,4},{6,5},{7,6},{8,7},{9,8},{10,9},{11,1... | collective-permute-start | bytes 138248 | tf_op jit(solution)/shard_map/ppermute | solution.py:24
  65.4 11.6 %collective-permute-start.4 = (bf16[2,20,1536]{2,1,0:T(8,128)(2,1)S(1)}, bf16[2,20,1536]{2,1,0:T(8,128)(2,1)S(1)}, u32[]{:S(2)}, u32[]{:S(2)}) collective-permute-start(bf16[2,20,1536]{2,1,0:T(8,128)(2,1)S(1)} %squeeze.21), channel_id=1, source_target_pairs={{0,64},{1,65},{2,66},{3,67},{4,68},{5,69},{6,70},{7,71},{8,72},{9,... | collective-permute-start | bytes 368648 | tf_op jit(solution)/shard_map/ppermute | solution.py:57
  68.9 10.0 %collective-permute-start.5 = (bf16[2,20,1536]{2,1,0:T(8,128)(2,1)S(1)}, bf16[2,20,1536]{2,1,0:T(8,128)(2,1)S(1)}, u32[]{:S(2)}, u32[]{:S(2)}) collective-permute-start(bf16[2,20,1536]{2,1,0:T(8,128)(2,1)S(1)} %squeeze.22), channel_id=1, source_target_pairs={{0,128},{1,129},{2,130},{3,131},{4,132},{5,133},{6,134},{7,135},{8... | collective-permute-start | bytes 368648 | tf_op jit(solution)/shard_map/ppermute | solution.py:57
  73.6 7.0 %collective-permute-start.6 = (bf16[2,20,1536]{2,1,0:T(8,128)(2,1)S(1)}, bf16[2,20,1536]{2,1,0:T(8,128)(2,1)S(1)}, u32[]{:S(2)}, u32[]{:S(2)}) collective-permute-start(bf16[2,20,1536]{2,1,0:T(8,128)(2,1)S(1)} %squeeze.46), channel_id=1, source_target_pairs={{0,192},{1,193},{2,194},{3,195},{4,196},{5,197},{6,198},{7,199},{8... | collective-permute-start | bytes 368648 | tf_op jit(solution)/shard_map/ppermute | solution.py:57
  80.8 22.2 %collective-permute-start.7 = (bf16[80,1536]{1,0:T(8,128)(2,1)S(1)}, bf16[80,1536]{1,0:T(8,128)(2,1)S(1)}, u32[]{:S(2)}, u32[]{:S(2)}) collective-permute-start(bf16[80,1536]{1,0:T(8,128)(2,1)S(1)} %reshape_squeeze.24), channel_id=1, source_target_pairs={{0,270},{1,271},{2,268},{3,269},{4,266},{5,267},{6,264},{7,265},{8... | collective-permute-start | bytes 737288 | tf_op jit(solution)/shard_map/ppermute | solution.py:57
  103.1 15.9 %collective-permute-start.8 = (bf16[160,1536]{1,0:T(8,128)(2,1)S(1)}, bf16[160,1536]{1,0:T(8,128)(2,1)S(1)}, u32[]{:S(2)}, u32[]{:S(2)}) collective-permute-start(bf16[160,1536]{1,0:T(8,128)(2,1)S(1)} %constant_dynamic-update-slice_fusion), channel_id=1, source_target_pairs={{0,48},{1,49},{2,50},{3,51},{4,52},{5,53},{6,54},{7,55},{8,56},{9,... | collective-permute-start | bytes 1474568 | tf_op jit(solution)/shard_map/ppermute | solution.py:43
  119.1 4.5 %collective-permute-start.9 = (bf16[2,160,1536]{2,1,0:T(8,128)(2,1)S(1)}, bf16[2,160,1536]{2,1,0:T(8,128)(2,1)S(1)}, u32[]{:S(2)}, u32[]{:S(2)}) collective-permute-start(bf16[2,160,1536]{2,1,0:T(8,128)(2,1)S(1)} %get-tuple-element.47), channel_id=1, source_target_pairs={{0,1},{1,0},{2,3},{3,2},{4,5},{5,4},{6,7},{7,6},{8,9},{9,8},{10,11... | collective-permute-start | bytes 2949128 | tf_op jit(solution)/shard_map/ppermute | solution.py:43
  148.7 12.9 %collective-permute-start.12 = (bf16[2,80,1536]{2,1,0:T(8,128)(2,1)S(1)}, bf16[2,80,1536]{2,1,0:T(8,128)(2,1)S(1)}, u32[]{:S(2)}, u32[]{:S(2)}) collective-permute-start(bf16[2,80,1536]{2,1,0:T(8,128)(2,1)S(1)} %bitcast.114), channel_id=1, source_target_pairs={{0,1},{1,0},{2,3},{3,2},{4,5},{5,4},{6,7},{7,6},{8,9},{9,8},{10,11... | collective-permute-start | bytes 1474568 | tf_op jit(solution)/shard_map/ppermute | solution.py:43
  159.0 4.6 %collective-permute-start.10 = (bf16[2,80,1536]{2,1,0:T(8,128)(2,1)S(1)}, bf16[2,80,1536]{2,1,0:T(8,128)(2,1)S(1)}, u32[]{:S(2)}, u32[]{:S(2)}) collective-permute-start(bf16[2,80,1536]{2,1,0:T(8,128)(2,1)S(1)} %bitcast.113), channel_id=1, source_target_pairs={{0,1},{1,0},{2,3},{3,2},{4,5},{5,4},{6,7},{7,6},{8,9},{9,8},{10,11... | collective-permute-start | bytes 1474568 | tf_op jit(solution)/shard_map/ppermute | solution.py:43
  161.7 10.7 %collective-permute-start.13 = (bf16[80,1536]{1,0:T(8,128)(2,1)S(1)}, bf16[80,1536]{1,0:T(8,128)(2,1)S(1)}, u32[]{:S(2)}, u32[]{:S(2)}) collective-permute-start(bf16[80,1536]{1,0:T(8,128)(2,1)S(1)} %fusion.60), channel_id=1, source_target_pairs={{0,48},{1,49},{2,50},{3,51},{4,52},{5,53},{6,54},{7,55},{8,56},{9,... | collective-permute-start | bytes 737288 | tf_op jit(solution)/shard_map/ppermute | solution.py:43
  163.8 24.5 %collective-permute-start.11 = (bf16[80,1536]{1,0:T(8,128)(2,1)S(1)}, bf16[80,1536]{1,0:T(8,128)(2,1)S(1)}, u32[]{:S(2)}, u32[]{:S(2)}) collective-permute-start(bf16[80,1536]{1,0:T(8,128)(2,1)S(1)} %fusion.59), channel_id=1, source_target_pairs={{0,48},{1,49},{2,50},{3,51},{4,52},{5,53},{6,54},{7,55},{8,56},{9,... | collective-permute-start | bytes 737288 | tf_op jit(solution)/shard_map/ppermute | solution.py:43
  172.5 37.8 %collective-permute-start.14 = (bf16[20,1536]{1,0:T(8,128)(2,1)S(1)}, bf16[20,1536]{1,0:T(8,128)(2,1)S(1)}, u32[]{:S(2)}, u32[]{:S(2)}) collective-permute-start(bf16[20,1536]{1,0:T(8,128)(2,1)S(1)} %get-tuple-element.60), channel_id=1, source_target_pairs={{270,0},{271,1},{268,2},{269,3},{266,4},{267,5},{264,6},{265,7},{2... | collective-permute-start | bytes 184328 | tf_op jit(solution)/shard_map/ppermute | solution.py:57
  188.4 25.2 %collective-permute-start.15 = (bf16[20,1536]{1,0:T(8,128)(2,1)S(1)}, bf16[20,1536]{1,0:T(8,128)(2,1)S(1)}, u32[]{:S(2)}, u32[]{:S(2)}) collective-permute-start(bf16[20,1536]{1,0:T(8,128)(2,1)S(1)} %get-tuple-element.59), channel_id=1, source_target_pairs={{64,0},{65,1},{66,2},{67,3},{68,4},{69,5},{70,6},{71,7},{72,8},{73... | collective-permute-start | bytes 184328 | tf_op jit(solution)/shard_map/ppermute | solution.py:57
  192.9 24.4 %collective-permute-start.16 = (bf16[20,1536]{1,0:T(8,128)(2,1)S(1)}, bf16[20,1536]{1,0:T(8,128)(2,1)S(1)}, u32[]{:S(2)}, u32[]{:S(2)}) collective-permute-start(bf16[20,1536]{1,0:T(8,128)(2,1)S(1)} %get-tuple-element.63), channel_id=1, source_target_pairs={{334,0},{335,1},{332,2},{333,3},{330,4},{331,5},{328,6},{329,7},{3... | collective-permute-start | bytes 184328 | tf_op jit(solution)/shard_map/ppermute | solution.py:57
  197.2 20.1 %collective-permute-start.17 = (bf16[20,1536]{1,0:T(8,128)(2,1)S(1)}, bf16[20,1536]{1,0:T(8,128)(2,1)S(1)}, u32[]{:S(2)}, u32[]{:S(2)}) collective-permute-start(bf16[20,1536]{1,0:T(8,128)(2,1)S(1)} %get-tuple-element.58), channel_id=1, source_target_pairs={{128,0},{129,1},{130,2},{131,3},{132,4},{133,5},{134,6},{135,7},{1... | collective-permute-start | bytes 184328 | tf_op jit(solution)/shard_map/ppermute | solution.py:57
  200.0 17.4 %collective-permute-start.18 = (bf16[20,1536]{1,0:T(8,128)(2,1)S(1)}, bf16[20,1536]{1,0:T(8,128)(2,1)S(1)}, u32[]{:S(2)}, u32[]{:S(2)}) collective-permute-start(bf16[20,1536]{1,0:T(8,128)(2,1)S(1)} %get-tuple-element.62), channel_id=1, source_target_pairs={{398,0},{399,1},{396,2},{397,3},{394,4},{395,5},{392,6},{393,7},{3... | collective-permute-start | bytes 184328 | tf_op jit(solution)/shard_map/ppermute | solution.py:57
  210.4 7.5 %collective-permute-start.19 = (bf16[20,1536]{1,0:T(8,128)(2,1)S(1)}, bf16[20,1536]{1,0:T(8,128)(2,1)S(1)}, u32[]{:S(2)}, u32[]{:S(2)}) collective-permute-start(bf16[20,1536]{1,0:T(8,128)(2,1)S(1)} %get-tuple-element.57), channel_id=1, source_target_pairs={{192,0},{193,1},{194,2},{195,3},{196,4},{197,5},{198,6},{199,7},{2... | collective-permute-start | bytes 184328 | tf_op jit(solution)/shard_map/ppermute | solution.py:57
  213.6 15.0 %collective-permute-start.20 = (bf16[20,1536]{1,0:T(8,128)(2,1)S(1)}, bf16[20,1536]{1,0:T(8,128)(2,1)S(1)}, u32[]{:S(2)}, u32[]{:S(2)}) collective-permute-start(bf16[20,1536]{1,0:T(8,128)(2,1)S(1)} %get-tuple-element.61), channel_id=1, source_target_pairs={{462,0},{463,1},{460,2},{461,3},{458,4},{459,5},{456,6},{457,7},{4... | collective-permute-start | bytes 184328 | tf_op jit(solution)/shard_map/ppermute | solution.py:57
  (24 other events, 240.5 us)
Sparse Core Ops, SparseCore 0:
  9.4 132.1 all-gather.2

commit v5 on v3

--- a/solution.py
+++ b/solution.py
@@ -77,7 +77,7 @@
         out_ref[...] += part
 
 
-def expert(rows, weights, step=4):
+def expert(rows, weights, step=8):
     count, width = rows.shape
     shards, twice, _ = weights.shape
     return pl.pallas_call(

time: 233 us -> 231 us (level)
  no operation moved by 1% of the time
where the time goes in v5:
time: 231 us; the launch traced here: 230 us
  waiting for transfers between devices  94.9 us (41%)
  starting transfers between devices  76.1 us (33%)
  other arithmetic  18.1 us (8%)
  between operations  14.9 us (6%)
  Pallas kernels  10.9 us (5%)
  local copies, waits for them, and re-layouts  8.55 us (4%)
  matrix products  6.38 us (3%)
    ppermute x8, waiting for transfers between devices, group_hop(): return lax.ppermute(array, ('grp', 'tm'), pairs)  37.9 us
    ppermute x8, starting transfers between devices, group_hop(): return lax.ppermute(array, ('grp', 'tm'), pairs)  32.3 us
    ppermute x2, starting transfers between devices, with_halo(): lax.ppermute(head, axis, [((i + 1) % count, i) for i in range(ends)])  23.9 us
    ppermute x6, waiting for transfers between devices, place_hop(): return lax.ppermute(array, 'tm', [(i, to(i)) for i in range(places)])  22.4 us
    all_gather x1, waiting for transfers between devices, body(): weights = lax.all_gather(shard, 'tm', axis_index_groups=loops)  19.9 us
    ppermute x6, starting transfers between devices, place_hop(): return lax.ppermute(array, 'tm', [(i, to(i)) for i in range(places)])  16.1 us
    ppermute x2, waiting for transfers between devices, with_halo(): lax.ppermute(tail, axis, [(i, (i + 1) % count) for i in range(ends)])  12.4 us
    pallas_call x1, Pallas kernels, expert(): pl.pallas_call(expert_kernel, grid=(shards // step,), in_specs=[pl.BlockS...  10.9 us
  transfers between devices with their start and end apart: 19, of which 13 were waited for; matrix products, arithmetic and copies ran while one was open for 12% of the time, Pallas kernels for 0%

profile of v5, /device:TPU:24, one launch (start us, length us, event | category | flops | bytes accessed | tf_op | source)
XLA Modules:
  0.0 229.8 jit_solution(3716237453258741798)
XLA Ops:
  10.1 12.8 %collective-permute-start.1 = (bf16[128,2,1536]{0,2,1:T(8,128)(2,1)S(1)}, bf16[128,2,1536]{0,2,1:T(8,128)(2,1)S(1)}, u32[]{:S(2)}, u32[]{:S(2)}) collective-permute-start(bf16[128,2,1536]{0,2,1:T(8,128)(2,1)S(1)} %pad_maximum_fusion.3), channel_id=1, source_target_pairs={{1,0},{2,1},{3,2},{4,3},{5,4},{6,5},{7,6},{8,7},{9,8},{10,9},{11,1... | collective-permute-start | bytes 2359304 | tf_op jit(solution)/shard_map/ppermute | solution.py:24
  31.1 2.4 %slice_reduce_fusion.30 = (f32[1536]{0:T(1024)S(1)}, f32[1536]{0:T(1024)S(1)}, f32[1536]{0:T(1024)}, f32[1536]{0:T(1024)}, f32[1536]{0:T(1024)}, /*index=5*/f32[...) fusion(f32[31,1536]{1,0:T(8,128)} %param.13), kind=kLoop, calls=%fused_computation.186 | loop fusion | bytes 233472 | tf_op jit(solution)/shard_map/slice | solution.py:164
  39.9 12.4 %collective-permute-done = bf16[128,2,1536]{0,2,1:T(8,128)(2,1)S(1)} collective-permute-done((bf16[128,2,1536]{0,2,1:T(8,128)(2,1)S(1)}, bf16[128,2,1536]{0,2,1:T(8,128)(2,1)S(1)}, u32[]{:S(2)}, u32[]{:S(2)}) %collective-permute-start) | collective-permute-done | bytes 786464 | tf_op jit(solution)/shard_map/ppermute | solution.py:22
  53.6 2.7 %fusion.89 = (f32[12,128]{1,0:T(8,128)S(1)}, f32[12,128,384]{1,2,0:T(8,128)}) fusion(pred[128,384]{0,1:T(8,128)(4,1)S(1)} %copy-done.4, bf16[384,12,128]{0,2,1:T(8,128)(2,1)S(1)} %bitcast.105, bf16[128,12,128]{0,2,1:T(8,128)(2,1)S(1)} %bitcast.112), kind=kOutput, calls=%fused_computation.218 | convolution fusion | flops 305529216 | bytes 3987456 | tf_op jit(solution)/shard_map/sub | solution.py:116
  56.3 2.2 fusion.9
  61.8 11.1 %collective-permute-start.3 = (bf16[15,1536]{1,0:T(8,128)(2,1)S(1)}, bf16[15,1536]{1,0:T(8,128)(2,1)S(1)}, u32[]{:S(2)}, u32[]{:S(2)}) collective-permute-start(bf16[15,1536]{1,0:T(8,128)(2,1)S(1)} %get-tuple-element.61), channel_id=1, source_target_pairs={{1,0},{2,1},{3,2},{4,3},{5,4},{6,5},{7,6},{8,7},{9,8},{10,9},{11,1... | collective-permute-start | bytes 138248 | tf_op jit(solution)/shard_map/ppermute | solution.py:24
  75.0 4.3 %convert_reduce_fusion = (f32[128]{0:T(128)S(1)}, bf16[128,1536]{1,0:T(8,128)(2,1)S(1)}) fusion(bf16[15,1536]{1,0:T(8,128)(2,1)S(1)} %collective-permute-done.3, bf16[128,1536]{1,0:T(8,128)(2,1)S(1)} %fusion.21, f32[1536]{0:T(1024)S(1)} %get-tuple-element.34, f32[1536]{0:T(1024)S(1)} %get-tuple-element.35, f32[1536]{0:T(1024)S(1)} %get-tuple-element.6, ...), kind=kLoop, calls=%fused_computation.47 | loop fusion | flops 37552000 | bytes 1462784 | tf_op jit(solution)/shard_map/reduce_sum | solution.py:32
  80.2 3.6 %collective-permute-start.4 = (bf16[2,20,1536]{2,1,0:T(8,128)(2,1)S(1)}, bf16[2,20,1536]{2,1,0:T(8,128)(2,1)S(1)}, u32[]{:S(2)}, u32[]{:S(2)}) collective-permute-start(bf16[2,20,1536]{2,1,0:T(8,128)(2,1)S(1)} %squeeze.48), channel_id=1, source_target_pairs={{0,64},{1,65},{2,66},{3,67},{4,68},{5,69},{6,70},{7,71},{8,72},{9,... | collective-permute-start | bytes 368648 | tf_op jit(solution)/shard_map/ppermute | solution.py:57
  83.8 4.7 %collective-permute-start.5 = (bf16[2,20,1536]{2,1,0:T(8,128)(2,1)S(1)}, bf16[2,20,1536]{2,1,0:T(8,128)(2,1)S(1)}, u32[]{:S(2)}, u32[]{:S(2)}) collective-permute-start(bf16[2,20,1536]{2,1,0:T(8,128)(2,1)S(1)} %squeeze.49), channel_id=1, source_target_pairs={{0,128},{1,129},{2,130},{3,131},{4,132},{5,133},{6,134},{7,135},{8... | collective-permute-start | bytes 368648 | tf_op jit(solution)/shard_map/ppermute | solution.py:57
  88.5 3.3 %collective-permute-start.6 = (bf16[2,20,1536]{2,1,0:T(8,128)(2,1)S(1)}, bf16[2,20,1536]{2,1,0:T(8,128)(2,1)S(1)}, u32[]{:S(2)}, u32[]{:S(2)}) collective-permute-start(bf16[2,20,1536]{2,1,0:T(8,128)(2,1)S(1)} %squeeze.50), channel_id=1, source_target_pairs={{0,192},{1,193},{2,194},{3,195},{4,196},{5,197},{6,198},{7,199},{8... | collective-permute-start | bytes 368648 | tf_op jit(solution)/shard_map/ppermute | solution.py:57
  92.3 3.2 %collective-permute-done.6 = bf16[2,20,1536]{2,1,0:T(8,128)(2,1)S(1)} collective-permute-done((bf16[2,20,1536]{2,1,0:T(8,128)(2,1)S(1)}, bf16[2,20,1536]{2,1,0:T(8,128)(2,1)S(1)}, u32[]{:S(2)}, u32[]{:S(2)}) %collective-permute-start.6) | collective-permute-done | bytes 122912 | tf_op jit(solution)/shard_map/ppermute | solution.py:57
  97.8 11.0 %collective-permute-done.7 = bf16[80,1536]{1,0:T(8,128)(2,1)S(1)} collective-permute-done((bf16[80,1536]{1,0:T(8,128)(2,1)S(1)}, bf16[80,1536]{1,0:T(8,128)(2,1)S(1)}, u32[]{:S(2)}, u32[]{:S(2)}) %collective-permute-start.7) | collective-permute-done | bytes 245792 | tf_op jit(solution)/shard_map/ppermute | solution.py:57
  110.7 14.4 %collective-permute-done.8 = bf16[160,1536]{1,0:T(8,128)(2,1)S(1)} collective-permute-done((bf16[160,1536]{1,0:T(8,128)(2,1)S(1)}, bf16[160,1536]{1,0:T(8,128)(2,1)S(1)}, u32[]{:S(2)}, u32[]{:S(2)}) %collective-permute-start.8) | collective-permute-done | bytes 491552 | tf_op jit(solution)/shard_map/ppermute | solution.py:43
  125.3 2.7 %collective-permute-start.9 = (bf16[2,160,1536]{2,1,0:T(8,128)(2,1)S(1)}, bf16[2,160,1536]{2,1,0:T(8,128)(2,1)S(1)}, u32[]{:S(2)}, u32[]{:S(2)}) collective-permute-start(bf16[2,160,1536]{2,1,0:T(8,128)(2,1)S(1)} %get-tuple-element.49), channel_id=1, source_target_pairs={{0,1},{1,0},{2,3},{3,2},{4,5},{5,4},{6,7},{7,6},{8,9},{9,8},{10,11... | collective-permute-start | bytes 2949128 | tf_op jit(solution)/shard_map/ppermute | solution.py:43
  130.4 19.9 %all-gather.3.cloned.1.call-done = bf16[3072,1536]{1,0:T(8,128)(2,1)} async-done(((bf16[192,1536]{1,0:T(8,128)(2,1)}), bf16[3072,1536]{1,0:T(8,128)(2,1)}) %all-gather.3.cloned.1.call-update) | async-done | bytes 9437200 | tf_op jit(solution)/shard_map/all_gather | solution.py:150
  150.3 10.9 %shard_map.91 = f32[640,1536]{1,0:T(8,128)S(1)} custom-call(bf16[640,1536]{1,0:T(8,128)(2,1)S(1)} %bitcast.96, bf16[16,192,1536]{2,1,0:T(8,128)(2,1)} %bitcast.123), custom_call_target="tpu_custom_call" | custom-call | flops 6039797760 | bytes 15335424 | tf_op jit(solution)/shard_map/pallas_call | solution.py:83
  163.5 2.4 %collective-permute-start.12 = (bf16[2,80,1536]{2,1,0:T(8,128)(2,1)S(1)}, bf16[2,80,1536]{2,1,0:T(8,128)(2,1)S(1)}, u32[]{:S(2)}, u32[]{:S(2)}) collective-permute-start(bf16[2,80,1536]{2,1,0:T(8,128)(2,1)S(1)} %bitcast.111), channel_id=1, source_target_pairs={{0,1},{1,0},{2,3},{3,2},{4,5},{5,4},{6,7},{7,6},{8,9},{9,8},{10,11... | collective-permute-start | bytes 1474568 | tf_op jit(solution)/shard_map/ppermute | solution.py:43
  167.5 5.0 %collective-permute-start.13 = (bf16[80,1536]{1,0:T(8,128)(2,1)S(1)}, bf16[80,1536]{1,0:T(8,128)(2,1)S(1)}, u32[]{:S(2)}, u32[]{:S(2)}) collective-permute-start(bf16[80,1536]{1,0:T(8,128)(2,1)S(1)} %fusion.60), channel_id=1, source_target_pairs={{0,48},{1,49},{2,50},{3,51},{4,52},{5,53},{6,54},{7,55},{8,56},{9,... | collective-permute-start | bytes 737288 | tf_op jit(solution)/shard_map/ppermute | solution.py:43
  174.8 4.6 %collective-permute-done.13 = bf16[80,1536]{1,0:T(8,128)(2,1)S(1)} collective-permute-done((bf16[80,1536]{1,0:T(8,128)(2,1)S(1)}, bf16[80,1536]{1,0:T(8,128)(2,1)S(1)}, u32[]{:S(2)}, u32[]{:S(2)}) %collective-permute-start.13) | collective-permute-done | bytes 245792 | tf_op jit(solution)/shard_map/ppermute | solution.py:43
  179.4 7.9 %collective-permute-start.14 = (bf16[80,1536]{1,0:T(8,128)(2,1)S(1)}, bf16[80,1536]{1,0:T(8,128)(2,1)S(1)}, u32[]{:S(2)}, u32[]{:S(2)}) collective-permute-start(bf16[80,1536]{1,0:T(8,128)(2,1)S(1)} %fusion.25), channel_id=1, source_target_pairs={{270,0},{271,1},{268,2},{269,3},{266,4},{267,5},{264,6},{265,7},{2... | collective-permute-start | bytes 737288 | tf_op jit(solution)/shard_map/ppermute | solution.py:57
  187.5 17.4 %collective-permute-done.14 = bf16[80,1536]{1,0:T(8,128)(2,1)S(1)} collective-permute-done((bf16[80,1536]{1,0:T(8,128)(2,1)S(1)}, bf16[80,1536]{1,0:T(8,128)(2,1)S(1)}, u32[]{:S(2)}, u32[]{:S(2)}) %collective-permute-start.14) | collective-permute-done | bytes 245792 | tf_op jit(solution)/shard_map/ppermute | solution.py:57
  205.1 4.9 %collective-permute-start.15 = (bf16[2,20,1536]{2,1,0:T(8,128)(2,1)S(1)}, bf16[2,20,1536]{2,1,0:T(8,128)(2,1)S(1)}, u32[]{:S(2)}, u32[]{:S(2)}) collective-permute-start(bf16[2,20,1536]{2,1,0:T(8,128)(2,1)S(1)} %get-tuple-element.51), channel_id=1, source_target_pairs={{64,0},{65,1},{66,2},{67,3},{68,4},{69,5},{70,6},{71,7},{72,8},{73... | collective-permute-start | bytes 368648 | tf_op jit(solution)/shard_map/ppermute | solution.py:57
  211.9 4.0 %collective-permute-start.16 = (bf16[2,20,1536]{2,1,0:T(8,128)(2,1)S(1)}, bf16[2,20,1536]{2,1,0:T(8,128)(2,1)S(1)}, u32[]{:S(2)}, u32[]{:S(2)}) collective-permute-start(bf16[2,20,1536]{2,1,0:T(8,128)(2,1)S(1)} %get-tuple-element.53), channel_id=1, source_target_pairs={{128,0},{129,1},{130,2},{131,3},{132,4},{133,5},{134,6},{135,7},{1... | collective-permute-start | bytes 368648 | tf_op jit(solution)/shard_map/ppermute | solution.py:57
  215.9 5.8 %collective-permute-done.17 = bf16[2,20,1536]{2,1,0:T(8,128)(2,1)S(1)} collective-permute-done((bf16[2,20,1536]{2,1,0:T(8,128)(2,1)S(1)}, bf16[2,20,1536]{2,1,0:T(8,128)(2,1)S(1)}, u32[]{:S(2)}, u32[]{:S(2)}) %collective-permute-start.17) | collective-permute-done | bytes 122912 | tf_op jit(solution)/shard_map/ppermute | solution.py:57
  (134 shorter events, 41.1 us)
Async XLA Ops:
  6.5 143.8 %all-gather.3.cloned.1.call-start = ((), (), s32[]{:S(2)}) async-start(), calls=%async_computation | async-start | bytes 10027008 | tf_op jit(solution)/shard_map/all_gather | solution.py:150
  6.5 19.5 %copy-start.23 = (s32[1,128]{1,0:T(1,128)S(1)}, s32[1,128]{1,0:T(1,128)}, u32[]{:S(2)}) copy-start(s32[1,128]{1,0:T(1,128)} %param.15) | copy-start | bytes 1540
  8.5 24.9 %copy-start.1 = (bf16[1,128,1536]{2,1,0:T(8,128)(2,1)S(1)}, bf16[1,128,1536]{2,1,0:T(8,128)(2,1)}, u32[]{:S(2)}) copy-start(bf16[1,128,1536]{2,1,0:T(8,128)(2,1)} %param.10) | copy-start | bytes 1179652
  10.1 29.8 %collective-permute-start.1 = (bf16[128,2,1536]{0,2,1:T(8,128)(2,1)S(1)}, bf16[128,2,1536]{0,2,1:T(8,128)(2,1)S(1)}, u32[]{:S(2)}, u32[]{:S(2)}) collective-permute-start(bf16[128,2,1536]{0,2,1:T(8,128)(2,1)S(1)} %pad_maximum_fusion.3), channel_id=1, source_target_pairs={{1,0},{2,1},{3,2},{4,3},{5,4},{6,5},{7,6},{8,7},{9,8},{10,9},{11,1... | collective-permute-start | bytes 2359304 | tf_op jit(solution)/shard_map/ppermute | solution.py:24
  22.9 29.4 %collective-permute-start = (bf16[128,2,1536]{0,2,1:T(8,128)(2,1)S(1)}, bf16[128,2,1536]{0,2,1:T(8,128)(2,1)S(1)}, u32[]{:S(2)}, u32[]{:S(2)}) collective-permute-start(bf16[128,2,1536]{0,2,1:T(8,128)(2,1)S(1)} %pad_maximum_fusion.3), channel_id=1, source_target_pairs={{0,1},{1,2},{2,3},{3,4},{4,5},{5,6},{6,7},{7,8},{8,9},{9,10},{10,1... | collective-permute-start | bytes 2359304 | tf_op jit(solution)/shard_map/ppermute | solution.py:22
  58.6 16.3 %copy-start.5 = (f32[1536]{0:T(1024)S(1)}, f32[1536]{0:T(1024)}, u32[]{:S(2)}) copy-start(f32[1536]{0:T(1024)} %get-tuple-element.7) | copy-start | bytes 18436
  59.0 20.6 %copy-start.22 = (s32[128]{0:T(128)S(1)}, s32[128]{0:T(128)}, u32[]{:S(2)}) copy-start(s32[128]{0:T(128)} %fusion.76) | copy-start | bytes 1540
  59.0 20.6 %copy-start.26 = (pred[128]{0:T(512)(128)(4,1)S(1)}, pred[128]{0:T(512)(128)(4,1)}, u32[]{:S(2)}) copy-start(pred[128]{0:T(512)(128)(4,1)} %compare_and_fusion) | copy-start | bytes 388
  59.9 14.5 %collective-permute-start.2 = (bf16[15,1536]{1,0:T(8,128)(2,1)S(1)}, bf16[15,1536]{1,0:T(8,128)(2,1)S(1)}, u32[]{:S(2)}, u32[]{:S(2)}) collective-permute-start(bf16[15,1536]{1,0:T(8,128)(2,1)S(1)} %get-tuple-element.60), channel_id=1, source_target_pairs={{0,1},{1,2},{2,3},{3,4},{4,5},{5,6},{6,7},{7,8},{8,9},{9,10},{10,1... | collective-permute-start | bytes 138248 | tf_op jit(solution)/shard_map/ppermute | solution.py:22
  61.8 13.1 %collective-permute-start.3 = (bf16[15,1536]{1,0:T(8,128)(2,1)S(1)}, bf16[15,1536]{1,0:T(8,128)(2,1)S(1)}, u32[]{:S(2)}, u32[]{:S(2)}) collective-permute-start(bf16[15,1536]{1,0:T(8,128)(2,1)S(1)} %get-tuple-element.61), channel_id=1, source_target_pairs={{1,0},{2,1},{3,2},{4,3},{5,4},{6,5},{7,6},{8,7},{9,8},{10,9},{11,1... | collective-permute-start | bytes 138248 | tf_op jit(solution)/shard_map/ppermute | solution.py:24
  80.2 11.7 %collective-permute-start.4 = (bf16[2,20,1536]{2,1,0:T(8,128)(2,1)S(1)}, bf16[2,20,1536]{2,1,0:T(8,128)(2,1)S(1)}, u32[]{:S(2)}, u32[]{:S(2)}) collective-permute-start(bf16[2,20,1536]{2,1,0:T(8,128)(2,1)S(1)} %squeeze.48), channel_id=1, source_target_pairs={{0,64},{1,65},{2,66},{3,67},{4,68},{5,69},{6,70},{7,71},{8,72},{9,... | collective-permute-start | bytes 368648 | tf_op jit(solution)/shard_map/ppermute | solution.py:57
  83.8 8.5 %collective-permute-start.5 = (bf16[2,20,1536]{2,1,0:T(8,128)(2,1)S(1)}, bf16[2,20,1536]{2,1,0:T(8,128)(2,1)S(1)}, u32[]{:S(2)}, u32[]{:S(2)}) collective-permute-start(bf16[2,20,1536]{2,1,0:T(8,128)(2,1)S(1)} %squeeze.49), channel_id=1, source_target_pairs={{0,128},{1,129},{2,130},{3,131},{4,132},{5,133},{6,134},{7,135},{8... | collective-permute-start | bytes 368648 | tf_op jit(solution)/shard_map/ppermute | solution.py:57
  88.5 7.0 %collective-permute-start.6 = (bf16[2,20,1536]{2,1,0:T(8,128)(2,1)S(1)}, bf16[2,20,1536]{2,1,0:T(8,128)(2,1)S(1)}, u32[]{:S(2)}, u32[]{:S(2)}) collective-permute-start(bf16[2,20,1536]{2,1,0:T(8,128)(2,1)S(1)} %squeeze.50), channel_id=1, source_target_pairs={{0,192},{1,193},{2,194},{3,195},{4,196},{5,197},{6,198},{7,199},{8... | collective-permute-start | bytes 368648 | tf_op jit(solution)/shard_map/ppermute | solution.py:57
  95.8 13.0 %collective-permute-start.7 = (bf16[80,1536]{1,0:T(8,128)(2,1)S(1)}, bf16[80,1536]{1,0:T(8,128)(2,1)S(1)}, u32[]{:S(2)}, u32[]{:S(2)}) collective-permute-start(bf16[80,1536]{1,0:T(8,128)(2,1)S(1)} %reshape_squeeze.18), channel_id=1, source_target_pairs={{0,270},{1,271},{2,268},{3,269},{4,266},{5,267},{6,264},{7,265},{8... | collective-permute-start | bytes 737288 | tf_op jit(solution)/shard_map/ppermute | solution.py:57
  108.8 16.4 %collective-permute-start.8 = (bf16[160,1536]{1,0:T(8,128)(2,1)S(1)}, bf16[160,1536]{1,0:T(8,128)(2,1)S(1)}, u32[]{:S(2)}, u32[]{:S(2)}) collective-permute-start(bf16[160,1536]{1,0:T(8,128)(2,1)S(1)} %constant_dynamic-update-slice_fusion), channel_id=1, source_target_pairs={{0,48},{1,49},{2,50},{3,51},{4,52},{5,53},{6,54},{7,55},{8,56},{9,... | collective-permute-start | bytes 1474568 | tf_op jit(solution)/shard_map/ppermute | solution.py:43
  125.3 4.7 %collective-permute-start.9 = (bf16[2,160,1536]{2,1,0:T(8,128)(2,1)S(1)}, bf16[2,160,1536]{2,1,0:T(8,128)(2,1)S(1)}, u32[]{:S(2)}, u32[]{:S(2)}) collective-permute-start(bf16[2,160,1536]{2,1,0:T(8,128)(2,1)S(1)} %get-tuple-element.49), channel_id=1, source_target_pairs={{0,1},{1,0},{2,3},{3,2},{4,5},{5,4},{6,7},{7,6},{8,9},{9,8},{10,11... | collective-permute-start | bytes 2949128 | tf_op jit(solution)/shard_map/ppermute | solution.py:43
  161.6 11.0 %collective-permute-start.10 = (bf16[2,80,1536]{2,1,0:T(8,128)(2,1)S(1)}, bf16[2,80,1536]{2,1,0:T(8,128)(2,1)S(1)}, u32[]{:S(2)}, u32[]{:S(2)}) collective-permute-start(bf16[2,80,1536]{2,1,0:T(8,128)(2,1)S(1)} %bitcast.110), channel_id=1, source_target_pairs={{0,1},{1,0},{2,3},{3,2},{4,5},{5,4},{6,7},{7,6},{8,9},{9,8},{10,11... | collective-permute-start | bytes 1474568 | tf_op jit(solution)/shard_map/ppermute | solution.py:43
  163.5 3.9 %collective-permute-start.12 = (bf16[2,80,1536]{2,1,0:T(8,128)(2,1)S(1)}, bf16[2,80,1536]{2,1,0:T(8,128)(2,1)S(1)}, u32[]{:S(2)}, u32[]{:S(2)}) collective-permute-start(bf16[2,80,1536]{2,1,0:T(8,128)(2,1)S(1)} %bitcast.111), channel_id=1, source_target_pairs={{0,1},{1,0},{2,3},{3,2},{4,5},{5,4},{6,7},{7,6},{8,9},{9,8},{10,11... | collective-permute-start | bytes 1474568 | tf_op jit(solution)/shard_map/ppermute | solution.py:43
  167.5 11.9 %collective-permute-start.13 = (bf16[80,1536]{1,0:T(8,128)(2,1)S(1)}, bf16[80,1536]{1,0:T(8,128)(2,1)S(1)}, u32[]{:S(2)}, u32[]{:S(2)}) collective-permute-start(bf16[80,1536]{1,0:T(8,128)(2,1)S(1)} %fusion.60), channel_id=1, source_target_pairs={{0,48},{1,49},{2,50},{3,51},{4,52},{5,53},{6,54},{7,55},{8,56},{9,... | collective-permute-start | bytes 737288 | tf_op jit(solution)/shard_map/ppermute | solution.py:43
  172.7 14.6 %collective-permute-start.11 = (bf16[80,1536]{1,0:T(8,128)(2,1)S(1)}, bf16[80,1536]{1,0:T(8,128)(2,1)S(1)}, u32[]{:S(2)}, u32[]{:S(2)}) collective-permute-start(bf16[80,1536]{1,0:T(8,128)(2,1)S(1)} %fusion.59), channel_id=1, source_target_pairs={{0,48},{1,49},{2,50},{3,51},{4,52},{5,53},{6,54},{7,55},{8,56},{9,... | collective-permute-start | bytes 737288 | tf_op jit(solution)/shard_map/ppermute | solution.py:43
  179.4 25.5 %collective-permute-start.14 = (bf16[80,1536]{1,0:T(8,128)(2,1)S(1)}, bf16[80,1536]{1,0:T(8,128)(2,1)S(1)}, u32[]{:S(2)}, u32[]{:S(2)}) collective-permute-start(bf16[80,1536]{1,0:T(8,128)(2,1)S(1)} %fusion.25), channel_id=1, source_target_pairs={{270,0},{271,1},{268,2},{269,3},{266,4},{267,5},{264,6},{265,7},{2... | collective-permute-start | bytes 737288 | tf_op jit(solution)/shard_map/ppermute | solution.py:57
  205.1 10.8 %collective-permute-start.15 = (bf16[2,20,1536]{2,1,0:T(8,128)(2,1)S(1)}, bf16[2,20,1536]{2,1,0:T(8,128)(2,1)S(1)}, u32[]{:S(2)}, u32[]{:S(2)}) collective-permute-start(bf16[2,20,1536]{2,1,0:T(8,128)(2,1)S(1)} %get-tuple-element.51), channel_id=1, source_target_pairs={{64,0},{65,1},{66,2},{67,3},{68,4},{69,5},{70,6},{71,7},{72,8},{73... | collective-permute-start | bytes 368648 | tf_op jit(solution)/shard_map/ppermute | solution.py:57
  209.9 11.8 %collective-permute-start.17 = (bf16[2,20,1536]{2,1,0:T(8,128)(2,1)S(1)}, bf16[2,20,1536]{2,1,0:T(8,128)(2,1)S(1)}, u32[]{:S(2)}, u32[]{:S(2)}) collective-permute-start(bf16[2,20,1536]{2,1,0:T(8,128)(2,1)S(1)} %get-tuple-element.52), channel_id=1, source_target_pairs={{192,0},{193,1},{194,2},{195,3},{196,4},{197,5},{198,6},{199,7},{2... | collective-permute-start | bytes 368648 | tf_op jit(solution)/shard_map/ppermute | solution.py:57
  211.9 9.8 %collective-permute-start.16 = (bf16[2,20,1536]{2,1,0:T(8,128)(2,1)S(1)}, bf16[2,20,1536]{2,1,0:T(8,128)(2,1)S(1)}, u32[]{:S(2)}, u32[]{:S(2)}) collective-permute-start(bf16[2,20,1536]{2,1,0:T(8,128)(2,1)S(1)} %get-tuple-element.53), channel_id=1, source_target_pairs={{128,0},{129,1},{130,2},{131,3},{132,4},{133,5},{134,6},{135,7},{1... | collective-permute-start | bytes 368648 | tf_op jit(solution)/shard_map/ppermute | solution.py:57
  (22 other events, 272.8 us)
Sparse Core Ops, SparseCore 0:
  9.4 140.8 all-gather.2
